TPU v7x, 768 devices: a whole 4x8x12 slice. The times are simulated.
768 devices in a mesh: gx: 96 (over y, z), gy: 8 (over x, core).
Axes of the slice: x: 4, y: 8, z: 12, core: 2. Of those that a mesh axis runs over, the one named last changes fastest.
Arguments:
- concentration: float32 [16, 768, 1024], P(None, 'gx', 'gy'), may hold values from 0 to 1
- labels: int32 [16, 768, 1024], P(None, 'gx', 'gy'), may hold values from 1 to 4096
- curve_scale: float32 [8], replicated, may hold values from 0.3 to 3
- curve_slope: float32 [8], replicated, may hold values from -1.5 to 1.5
- coarse_inv: float32 [8, 6144, 6144], P('gy', 'gx'), may hold values from -1 to 1.3, as said below
Outputs:
- updated: float32 [16, 768, 1024], P(None, 'gx', 'gy')
- residual: float32 [16, 768, 1024], P(None, 'gx', 'gy')
Inputs may be any that keep to these rules, and one draw needn't show every extreme that they name: `coarse_inv`: symmetric and positive definite for each column of subdomains.
All inputs are finite; a program needn't handle non-finite values.
Results may differ from a plain program's by a relative error of at most 0.0003.
Values sent between devices are 32-bit elements; how exact they have to be, the bound alone decides.
No kernel may reach another device: no remote copies, remote signals or barrier semaphores. Data moves between devices by JAX's collectives and lax.ppermute only.
A program may use at most 32 MiB of HBM per device.

v0:
```python
import math

import jax
import jax.numpy as jnp
from jax import lax
from jax.sharding import PartitionSpec as P

OV = 2
SWEEPS = 3
CHEB = 4
MZ = 2
MX = 4
MY = 8
KINDS = 8


INVERSE_STEP = 0.004
CONTACT = 0.3
LOWER_BOUND = 0.1
UPPER_BOUND = 1.9


def extended(array, sides, width):
    for axis, dim in sides:
        size, length = (lax.axis_size(axis), array.shape[dim])
        up = [(i, (i + 1) % size) for i in range(size - 1)]
        down = [(j, i) for i, j in up]
        last = lax.slice_in_dim(array, length - width, length, axis=dim)
        initial = lax.slice_in_dim(array, 0, width, axis=dim)
        before = lax.ppermute(last, axis, up)
        after = lax.ppermute(initial, axis, down)
        array = jnp.concatenate([before, array, after], axis=dim)
    return array


def pad_frame(values, margin):
    return jnp.pad(values, ((0, 0), (margin, margin), (margin, margin)))


def pair_weight(first_coeff, second_coeff, first_label, second_label):
    inside = jnp.where(first_label > 0.5, 1.0, 0.0) * jnp.where(second_label > 0.5, 1.0, 0.0)
    return (
        0.5
        * (first_coeff + second_coeff)
        * inside
        * jnp.where(first_label == second_label, 1.0, CONTACT)
    )


def face_weights(coeff_box, label_box):
    mid_coeff = coeff_box[:, 1:-1, 1:-1]
    mid_label = label_box[:, 1:-1, 1:-1]
    west_weight = pair_weight(
        mid_coeff, coeff_box[:, :-2, 1:-1], mid_label, label_box[:, :-2, 1:-1]
    )
    east_weight = pair_weight(mid_coeff, coeff_box[:, 2:, 1:-1], mid_label, label_box[:, 2:, 1:-1])
    south_weight = pair_weight(
        mid_coeff, coeff_box[:, 1:-1, :-2], mid_label, label_box[:, 1:-1, :-2]
    )
    north_weight = pair_weight(mid_coeff, coeff_box[:, 1:-1, 2:], mid_label, label_box[:, 1:-1, 2:])
    vertical = pair_weight(mid_coeff[:-1], mid_coeff[1:], mid_label[:-1], mid_label[1:])
    zero_layer = jnp.zeros_like(mid_coeff[:1])
    below_weight = jnp.concatenate([zero_layer, vertical], 0)
    above_weight = jnp.concatenate([vertical, zero_layer], 0)
    weights = (west_weight, east_weight, south_weight, north_weight, below_weight, above_weight)
    diagonal = (
        INVERSE_STEP
        + west_weight
        + east_weight
        + south_weight
        + north_weight
        + below_weight
        + above_weight
    )
    return (weights, diagonal)


def apply_op(field_box, weights, diagonal):
    west_weight, east_weight, south_weight, north_weight, below_weight, above_weight = weights
    centre_cells = field_box[:, 1:-1, 1:-1]
    zero_layer = jnp.zeros_like(centre_cells[:1])
    below_cells = jnp.concatenate([zero_layer, centre_cells[:-1]], 0)
    above_cells = jnp.concatenate([centre_cells[1:], zero_layer], 0)
    beside = west_weight * field_box[:, :-2, 1:-1] + east_weight * field_box[:, 2:, 1:-1]
    beside = beside + south_weight * field_box[:, 1:-1, :-2] + north_weight * field_box[:, 1:-1, 2:]
    beside = beside + below_weight * below_cells + above_weight * above_cells
    return diagonal * centre_cells - beside


def smooth_local(residual_box, weights, diagonal):
    centre = (UPPER_BOUND + LOWER_BOUND) / 2.0
    radius = (UPPER_BOUND - LOWER_BOUND) / 2.0
    spread = centre / radius
    ratio_now = 1.0 / spread
    inverse = 1.0 / diagonal
    update = inverse * residual_box / centre
    result = update
    remain = residual_box
    for iteration in range(CHEB - 1):
        remain = remain - apply_op(pad_frame(update, 1), weights, diagonal)
        ratio_next = 1.0 / (2.0 * spread - ratio_now)
        update = ratio_next * ratio_now * update + 2.0 * ratio_next / radius * inverse * remain
        result = result + update
        ratio_now = ratio_next
    return result


def cosine_table(mode_count, length):
    position = jnp.arange(length, dtype=jnp.float32) + 0.5
    order = jnp.arange(mode_count, dtype=jnp.float32)
    scaling = jnp.where(order == 0, math.sqrt(1.0 / length), math.sqrt(2.0 / length))
    return scaling[:, None] * jnp.cos(math.pi * order[:, None] * position[None, :] / length)


def interior(values):
    return values[:, OV:-OV, OV:-OV]


def coarse_part(residual_own, own_rows):
    depth_table = cosine_table(MZ, residual_own.shape[0])
    first_table = cosine_table(MX, residual_own.shape[1])
    second_table = cosine_table(MY, residual_own.shape[2])
    moments = jnp.einsum(
        "sz,px,qy,zxy->spq",
        depth_table,
        first_table,
        second_table,
        residual_own,
        precision=lax.Precision.HIGHEST,
    ).reshape(-1)
    answer = jnp.dot(
        own_rows, lax.all_gather(moments, "gx", axis=0, tiled=True), precision=lax.Precision.HIGHEST
    )
    return jnp.einsum(
        "sz,px,qy,spq->zxy",
        depth_table,
        first_table,
        second_table,
        answer.reshape(MZ, MX, MY),
        precision=lax.Precision.HIGHEST,
    )


def on_device(concentration, labels, curve_scale, curve_slope, coarse_inv):
    frame_width = OV + 1
    material = labels % KINDS
    selector = material[None] == jnp.arange(KINDS, dtype=jnp.int32)[:, None, None, None]
    scale_cells = jnp.sum(jnp.where(selector, curve_scale[:, None, None, None], 0.0), 0)
    slope_cells = jnp.sum(jnp.where(selector, curve_slope[:, None, None, None], 0.0), 0)
    diffusivity = scale_cells * jnp.exp(slope_cells * concentration)
    stacked = jnp.stack([concentration, diffusivity, labels.astype(jnp.float32)])
    framed = extended(stacked, (("gx", 2), ("gy", 3)), frame_width)
    weights, diagonal = face_weights(framed[1], framed[2])
    source = INVERSE_STEP * framed[0][:, 1:-1, 1:-1] - apply_op(framed[0], weights, diagonal)
    own_weights = tuple((interior(w) for w in weights))
    own_diagonal = interior(diagonal)
    source_own = interior(source)
    own_rows = coarse_inv[0]

    def own_residual(newton_update):
        rim_update = extended(newton_update, (("gx", 1), ("gy", 2)), 1)
        return source_own - apply_op(rim_update, own_weights, own_diagonal)

    newton_update = jnp.zeros_like(concentration)
    residual_box = source
    for sweep_index in range(SWEEPS):
        if sweep_index > 0:
            residual_box = extended(own_residual(newton_update), (("gx", 1), ("gy", 2)), OV)
        residual_own = interior(residual_box)
        local_part = interior(smooth_local(residual_box, weights, diagonal))
        newton_update = newton_update + local_part + coarse_part(residual_own, own_rows)
    residual_last = own_residual(newton_update)
    return (concentration + newton_update, residual_last)


def solution(mesh):
    return jax.shard_map(
        on_device,
        mesh=mesh,
        in_specs=(P(None, "gx", "gy"), P(None, "gx", "gy"), P(), P(), P("gy", "gx", None)),
        out_specs=(P(None, "gx", "gy"), P(None, "gx", "gy")),
        check_vma=False,
    )
```

profile of v0, /device:TPU:1, one launch (start us, length us, event | category | flops | bytes accessed | tf_op | source)
XLA Modules:
  0.0 1405.5 jit_solution(2986966371187457971)
XLA Ops:
  4.3 4.8 collective-permute-start
  10.6 4.2 collective-permute-done.1
  15.0 4.8 collective-permute-start.2
  19.9 5.9 collective-permute-start.3
  34.5 1.9 fusion.179
  38.5 340.7 %all-reduce.37 = f32[6144]{0:T(1024)S(1)} all-reduce(f32[6144]{0:T(1024)S(1)} %dynamic-update-slice), channel_id=1, replica_groups=mesh['gx'=96,'gy'=8] {'gx'}, use_global_device_ids=true, to_apply=%add.37 | all-reduce | flops 6144 | bytes 49152
  379.2 10.4 fusion.315
  390.2 1.5 fusion.2
  394.2 3.3 collective-permute-done.5
  397.6 84.7 %collective-permute-start.6 = (f32[16,10,1]{2,0,1:T(8,128)S(1)}, f32[16,10,1]{2,0,1:T(8,128)S(1)}, u32[]{:S(2)}, u32[]{:S(2)}) collective-permute-start(f32[16,10,1]{2,0,1:T(8,128)S(1)} %get-tuple-element.64), channel_id=1, source_target_pairs={{0,1},{1,2},{2,3},{3,4},{4,5},{5,6},{6,7},{8,9},{9,10},{10,11},{11... | collective-permute-start | bytes 1928 | tf_op jit(solution)/shard_map/ppermute | solution.py:30
  482.3 2.1 collective-permute-start.7
  484.4 3.6 collective-permute-done.7
  490.3 1.4 collective-permute-start.8
  494.1 331.6 %all-reduce.38 = f32[6144]{0:T(1024)S(1)} all-reduce(f32[6144]{0:T(1024)S(1)} %dynamic-update-slice.1), channel_id=1, replica_groups=mesh['gx'=96,'gy'=8] {'gx'}, use_global_device_ids=true, to_apply=%add.38 | all-reduce | flops 6144 | bytes 49152
  825.6 10.4 fusion.316
  836.4 84.0 %collective-permute-start.10 = (f32[16,12,2]{2,0,1:T(8,128)S(1)}, f32[16,12,2]{2,0,1:T(8,128)S(1)}, u32[]{:S(2)}, u32[]{:S(2)}) collective-permute-start(f32[16,12,2]{2,0,1:T(8,128)S(1)} %get-tuple-element.58), channel_id=1, source_target_pairs={{0,1},{1,2},{2,3},{3,4},{4,5},{5,6},{6,7},{8,9},{9,10},{10,11},{11... | collective-permute-start | bytes 4616 | tf_op jit(solution)/shard_map/ppermute | solution.py:30
  920.5 1.9 collective-permute-start.11
  922.7 3.7 collective-permute-done.11
  932.1 3.1 collective-permute-done.13
  935.3 3.0 collective-permute-start.14
  938.2 1.9 collective-permute-start.15
  940.2 3.8 collective-permute-done.15
  945.9 1.4 collective-permute-start.16
  951.6 332.4 %all-reduce.39 = f32[6144]{0:T(1024)S(1)} all-reduce(f32[6144]{0:T(1024)S(1)} %dynamic-update-slice.2), channel_id=1, replica_groups=mesh['gx'=96,'gy'=8] {'gx'}, use_global_device_ids=true, to_apply=%add.39 | all-reduce | flops 6144 | bytes 49152
  1284.0 10.4 fusion.317
  1295.5 84.0 %collective-permute-start.18 = (f32[16,12,2]{2,0,1:T(8,128)S(1)}, f32[16,12,2]{2,0,1:T(8,128)S(1)}, u32[]{:S(2)}, u32[]{:S(2)}) collective-permute-start(f32[16,12,2]{2,0,1:T(8,128)S(1)} %get-tuple-element.56), channel_id=1, source_target_pairs={{0,1},{1,2},{2,3},{3,4},{4,5},{5,6},{6,7},{8,9},{9,10},{10,11},{11... | collective-permute-start | bytes 4616 | tf_op jit(solution)/shard_map/ppermute | solution.py:30
  1379.6 1.9 collective-permute-start.19
  1381.8 3.7 collective-permute-done.19
  1392.6 3.1 collective-permute-done.21
  1395.8 3.0 collective-permute-start.22
  1398.8 1.9 collective-permute-start.23
  1401.4 3.2 collective-permute-done.23
  (160 shorter events, 45.9 us)
Async XLA Ops:
  4.3 6.4 collective-permute-start
  9.1 5.7 collective-permute-start.1
  10.4 912.0 %copy-start.10 = (f32[4]{0:T(128)}, f32[4]{0:T(128)S(1)}, u32[]{:S(2)}) copy-start(f32[4]{0:T(128)S(1)} %get-tuple-element.89) | copy-start | bytes 52
  10.4 912.0 %copy-start.12 = (f32[4]{0:T(128)}, f32[4]{0:T(128)S(1)}, u32[]{:S(2)}) copy-start(f32[4]{0:T(128)S(1)} %get-tuple-element.90) | copy-start | bytes 52
  10.5 825.6 %copy-start.14 = (f32[8]{0:T(128)}, f32[8]{0:T(128)S(1)}, u32[]{:S(2)}) copy-start(f32[8]{0:T(128)S(1)} %get-tuple-element.91) | copy-start | bytes 100
  10.5 825.6 %copy-start.16 = (f32[8]{0:T(128)}, f32[8]{0:T(128)S(1)}, u32[]{:S(2)}) copy-start(f32[8]{0:T(128)S(1)} %get-tuple-element.92) | copy-start | bytes 100
  10.6 934.3 %copy-start.8 = (f32[2,16]{1,0:T(2,128)}, f32[2,16]{1,0:T(2,128)S(1)}, u32[]{:S(2)}) copy-start(f32[2,16]{1,0:T(2,128)S(1)} %cosine_multiply_fusion.14) | copy-start | bytes 388
  10.6 911.8 %copy-start.18 = (f32[8]{0:T(128)}, f32[8]{0:T(128)S(1)}, u32[]{:S(2)}) copy-start(f32[8]{0:T(128)S(1)} %iota_add_fusion.1) | copy-start | bytes 100
  15.0 12.7 collective-permute-start.2
  19.9 8.6 collective-permute-start.3
  25.7 810.3 %copy-start.20 = (f32[128]{0:T(128)}, f32[128]{0:T(128)S(1)}, u32[]{:S(2)}) copy-start(f32[128]{0:T(128)S(1)} %iota_add_fusion) | copy-start | bytes 1540
  391.6 2.6 collective-permute-start.4
  392.9 4.6 collective-permute-start.5
  397.6 86.8 %collective-permute-start.6 = (f32[16,10,1]{2,0,1:T(8,128)S(1)}, f32[16,10,1]{2,0,1:T(8,128)S(1)}, u32[]{:S(2)}, u32[]{:S(2)}) collective-permute-start(f32[16,10,1]{2,0,1:T(8,128)S(1)} %get-tuple-element.64), channel_id=1, source_target_pairs={{0,1},{1,2},{2,3},{3,4},{4,5},{5,6},{6,7},{8,9},{9,10},{10,11},{11... | collective-permute-start | bytes 1928 | tf_op jit(solution)/shard_map/ppermute | solution.py:30
  482.3 5.8 collective-permute-start.7
  490.3 346.0 %collective-permute-start.8 = (f32[16,2,128]{2,0,1:T(8,128)S(1)}, f32[16,2,128]{2,0,1:T(8,128)S(1)}, u32[]{:S(2)}, u32[]{:S(2)}) collective-permute-start(f32[16,2,128]{2,0,1:T(8,128)S(1)} %get-tuple-element.76), channel_id=1, source_target_pairs={{0,8},{8,16},{16,24},{24,32},{32,40},{40,48},{48,56},{56,64},{64,7... | collective-permute-start | bytes 49160 | tf_op jit(solution)/shard_map/ppermute | solution.py:30
  491.7 344.6 %collective-permute-start.9 = (f32[16,2,128]{2,0,1:T(8,128)S(1)}, f32[16,2,128]{2,0,1:T(8,128)S(1)}, u32[]{:S(2)}, u32[]{:S(2)}) collective-permute-start(f32[16,2,128]{2,0,1:T(8,128)S(1)} %get-tuple-element.77), channel_id=1, source_target_pairs={{8,0},{16,8},{24,16},{32,24},{40,32},{48,40},{56,48},{64,56},{72,6... | collective-permute-start | bytes 49160 | tf_op jit(solution)/shard_map/ppermute | solution.py:31
  836.4 86.3 %collective-permute-start.10 = (f32[16,12,2]{2,0,1:T(8,128)S(1)}, f32[16,12,2]{2,0,1:T(8,128)S(1)}, u32[]{:S(2)}, u32[]{:S(2)}) collective-permute-start(f32[16,12,2]{2,0,1:T(8,128)S(1)} %get-tuple-element.58), channel_id=1, source_target_pairs={{0,1},{1,2},{2,3},{3,4},{4,5},{5,6},{6,7},{8,9},{9,10},{10,11},{11... | collective-permute-start | bytes 4616 | tf_op jit(solution)/shard_map/ppermute | solution.py:30
  920.5 5.9 collective-permute-start.11
  929.5 2.6 collective-permute-start.12
  930.8 4.4 collective-permute-start.13
  935.3 4.9 collective-permute-start.14
  938.2 5.8 collective-permute-start.15
  945.9 348.8 %collective-permute-start.16 = (f32[16,2,128]{2,0,1:T(8,128)}, f32[16,2,128]{2,0,1:T(8,128)S(1)}, u32[]{:S(2)}, u32[]{:S(2)}) collective-permute-start(f32[16,2,128]{2,0,1:T(8,128)} %get-tuple-element.70), channel_id=1, source_target_pairs={{0,8},{8,16},{16,24},{24,32},{32,40},{40,48},{48,56},{56,64},{64,7... | collective-permute-start | bytes 49160 | tf_op jit(solution)/shard_map/ppermute | solution.py:30
  947.3 347.4 %collective-permute-start.17 = (f32[16,2,128]{2,0,1:T(8,128)}, f32[16,2,128]{2,0,1:T(8,128)}, u32[]{:S(2)}, u32[]{:S(2)}) collective-permute-start(f32[16,2,128]{2,0,1:T(8,128)} %get-tuple-element.71), channel_id=1, source_target_pairs={{8,0},{16,8},{24,16},{32,24},{40,32},{48,40},{56,48},{64,56},{72,6... | collective-permute-start | bytes 49160 | tf_op jit(solution)/shard_map/ppermute | solution.py:31
  949.4 432.1 %copy-start.11 = (f32[4]{0:T(128)S(1)}, f32[4]{0:T(128)}, u32[]{:S(2)}) copy-start(f32[4]{0:T(128)} %copy-done.10) | copy-start | bytes 52
  1295.5 86.3 %collective-permute-start.18 = (f32[16,12,2]{2,0,1:T(8,128)S(1)}, f32[16,12,2]{2,0,1:T(8,128)S(1)}, u32[]{:S(2)}, u32[]{:S(2)}) collective-permute-start(f32[16,12,2]{2,0,1:T(8,128)S(1)} %get-tuple-element.56), channel_id=1, source_target_pairs={{0,1},{1,2},{2,3},{3,4},{4,5},{5,6},{6,7},{8,9},{9,10},{10,11},{11... | collective-permute-start | bytes 4616 | tf_op jit(solution)/shard_map/ppermute | solution.py:30
  1379.6 5.9 collective-permute-start.19
  1390.0 2.6 collective-permute-start.20
  1391.3 4.4 collective-permute-start.21
  1395.8 5.6 collective-permute-start.22
  1398.8 5.8 collective-permute-start.23
  (14 other events, 2647.2 us)
where the time goes:
time: 1430 us; the launch traced here: 1410 us
  blocking collectives  1000 us (70%)
  starting transfers between devices  298 us (21%)
  matrix products  43.5 us (3%)
  waiting for transfers between devices  32.3 us (2%)
  other arithmetic  15 us (1%)
    unnamed x3, blocking collectives  1000 us
    ppermute x12, starting transfers between devices, extended(): before = lax.ppermute(last, axis, up)  275 us
    ppermute x12, waiting for transfers between devices, extended(): after = lax.ppermute(initial, axis, down)  32.3 us
    dot_general x3, matrix products, coarse_part(): jnp.dot(own_rows, lax.all_gather(moments, 'gx', axis=0, tiled=True), prec...  31.2 us
  transfers between devices with their start and end apart: 24, of which 10 were waited for; matrix products, arithmetic and copies ran while one was open for 2% of the time, Pallas kernels for 0%

commit v1 on v0

--- a/solution.py
+++ b/solution.py
@@ -12,6 +12,8 @@
 MX = 4
 MY = 8
 KINDS = 8
+N_Y = 8
+N_Z = 12
 
 
 INVERSE_STEP = 0.004
@@ -116,6 +118,23 @@
     return values[:, OV:-OV, OV:-OV]
 
 
+def gathered(moments):
+    along_z = [[y * N_Z + z for z in range(N_Z)] for y in range(N_Y)]
+    along_y = [[y * N_Z + z for y in range(N_Y)] for z in range(N_Z)]
+    size = moments.shape[0]
+    line = lax.all_to_all(
+        jnp.broadcast_to(moments[None], (N_Z, size)), "gx", 0, 0, tiled=True, axis_index_groups=along_z
+    )
+    return lax.all_to_all(
+        jnp.broadcast_to(line.reshape(1, N_Z * size), (N_Y, N_Z * size)),
+        "gx",
+        0,
+        0,
+        tiled=True,
+        axis_index_groups=along_y,
+    ).reshape(-1)
+
+
 def coarse_part(residual_own, own_rows):
     depth_table = cosine_table(MZ, residual_own.shape[0])
     first_table = cosine_table(MX, residual_own.shape[1])
@@ -128,9 +147,7 @@
         residual_own,
         precision=lax.Precision.HIGHEST,
     ).reshape(-1)
-    answer = jnp.dot(
-        own_rows, lax.all_gather(moments, "gx", axis=0, tiled=True), precision=lax.Precision.HIGHEST
-    )
+    answer = jnp.sum(own_rows * gathered(moments)[None], axis=1)
     return jnp.einsum(
         "sz,px,qy,spq->zxy",
         depth_table,
@@ -161,11 +178,15 @@
         rim_update = extended(newton_update, (("gx", 1), ("gy", 2)), 1)
         return source_own - apply_op(rim_update, own_weights, own_diagonal)
 
+    def box_residual(newton_update):
+        frame_update = extended(newton_update, (("gx", 1), ("gy", 2)), frame_width)
+        return source - apply_op(frame_update, weights, diagonal)
+
     newton_update = jnp.zeros_like(concentration)
     residual_box = source
     for sweep_index in range(SWEEPS):
         if sweep_index > 0:
-            residual_box = extended(own_residual(newton_update), (("gx", 1), ("gy", 2)), OV)
+            residual_box = box_residual(newton_update)
         residual_own = interior(residual_box)
         local_part = interior(smooth_local(residual_box, weights, diagonal))
         newton_update = newton_update + local_part + coarse_part(residual_own, own_rows)

time: 1430 us -> 208 us (0.15); the launches traced: 1410 us -> 206 us
  blocking collectives: 1000 us -> 0 us
  starting transfers between devices: 298 us -> 91.8 us
  waiting for transfers between devices: 32.3 us -> 60.8 us
  matrix products: 43.5 us -> 15.1 us
    unnamed x3 -> x0, blocking collectives: 1000 us -> none
    ppermute x12 -> x8, starting transfers between devices: 275 us -> 33.9 us  [extended(): before = lax.ppermute(last, axis, up)]
    all_to_all x0 -> x6, starting transfers between devices: none -> 41 us  [the longest x3 26.9 us: gathered(): lax.all_to_all(jnp.broadcast_to(moments[None], (N_Z, size)), 'gx', 0, 0,...]
    all_to_all x0 -> x6, waiting for transfers between devices: none -> 33 us  [the longest x3 18.3 us: gathered(): lax.all_to_all(jnp.broadcast_to(moments[None], (N_Z, size)), 'gx', 0, 0,...]
    dot_general x3 -> x0, matrix products: 31.2 us -> none  [coarse_part(): jnp.dot(own_rows, lax.all_gather(moments, 'gx', axis=0, tiled=True), prec...]
    ppermute x12 -> x8, waiting for transfers between devices: 32.3 us -> 27.8 us  [extended(): after = lax.ppermute(initial, axis, down)]
  transfers between devices with their start and end apart: 24 -> 22, of which waited for: 10 -> 14; matrix products, arithmetic and copies ran while one was open for 2% -> 7% of each run, Pallas kernels for 0% -> 0%
where the time goes in v1:
time: 208 us; the launch traced here: 206 us
  starting transfers between devices  91.8 us (44%)
  waiting for transfers between devices  60.8 us (29%)
  other arithmetic  23.8 us (11%)
  matrix products  15.1 us (7%)
  local copies, waits for them, and re-layouts  13.4 us (6%)
    ppermute x8, starting transfers between devices, extended(): before = lax.ppermute(last, axis, up)  33.9 us
    ppermute x8, waiting for transfers between devices, extended(): after = lax.ppermute(initial, axis, down)  27.8 us
    all_to_all x3, starting transfers between devices, gathered(): lax.all_to_all(jnp.broadcast_to(moments[None], (N_Z, size)), 'gx', 0, 0,...  26.9 us
    all_to_all x3, waiting for transfers between devices, gathered(): lax.all_to_all(jnp.broadcast_to(moments[None], (N_Z, size)), 'gx', 0, 0,...  18.3 us
    ppermute x8, starting transfers between devices, extended(): after = lax.ppermute(initial, axis, down)  17 us
    all_to_all x3, waiting for transfers between devices, gathered(): lax.all_to_all(jnp.broadcast_to(line.reshape(1, N_Z * size), (N_Y, N_Z *...  14.7 us
    all_to_all x3, starting transfers between devices, gathered(): lax.all_to_all(jnp.broadcast_to(line.reshape(1, N_Z * size), (N_Y, N_Z *...  14.1 us
    dot_general x9, matrix products, coarse_part(): jnp.einsum('sz,px,qy,spq->zxy', depth_table, first_table, second_table, a...  8.73 us
  transfers between devices with their start and end apart: 22, of which 14 were waited for; matrix products, arithmetic and copies ran while one was open for 7% of the time, Pallas kernels for 0%

profile of v1, /device:TPU:1, one launch (start us, length us, event | category | flops | bytes accessed | tf_op | source)
XLA Modules:
  0.0 206.4 jit_solution(11420749442489126032)
XLA Ops:
  4.1 4.8 %collective-permute-start = (f32[3,16,3,128]{3,1,2,0:T(8,128)S(1)}, f32[3,16,3,128]{3,1,2,0:T(8,128)S(1)}, u32[]{:S(2)}, u32[]{:S(2)}) collective-permute-start(f32[3,16,3,128]{3,1,2,0:T(8,128)S(1)} %get-tuple-element.62), channel_id=1, source_target_pairs={{0,8},{8,16},{16,24},{24,32},{32,40},{40,48},{48,56},{56,64},{64,7... | collective-permute-start | bytes 221192 | tf_op jit(solution)/shard_map/ppermute | solution.py:32
  10.5 4.2 %collective-permute-done.1 = f32[3,16,3,128]{3,1,2,0:T(8,128)S(1)} collective-permute-done((f32[3,16,3,128]{3,1,2,0:T(8,128)S(1)}, f32[3,16,3,128]{3,1,2,0:T(8,128)S(1)}, u32[]{:S(2)}, u32[]{:S(2)}) %collective-permute-start.1) | collective-permute-done | bytes 73760 | tf_op jit(solution)/shard_map/ppermute | solution.py:33
  14.9 4.8 %collective-permute-start.2 = (f32[3,16,14,3]{3,1,2,0:T(8,128)S(1)}, f32[3,16,14,3]{3,1,2,0:T(8,128)S(1)}, u32[]{:S(2)}, u32[]{:S(2)}) collective-permute-start(f32[3,16,14,3]{3,1,2,0:T(8,128)S(1)} %get-tuple-element.36), channel_id=1, source_target_pairs={{0,1},{1,2},{2,3},{3,4},{4,5},{5,6},{6,7},{8,9},{9,10},{10,11},{11... | collective-permute-start | bytes 24200 | tf_op jit(solution)/shard_map/ppermute | solution.py:32
  19.7 5.9 %collective-permute-start.3 = (f32[3,16,14,3]{3,1,2,0:T(8,128)S(1)}, f32[3,16,14,3]{3,1,2,0:T(8,128)S(1)}, u32[]{:S(2)}, u32[]{:S(2)}) collective-permute-start(f32[3,16,14,3]{3,1,2,0:T(8,128)S(1)} %get-tuple-element.37), channel_id=1, source_target_pairs={{1,0},{2,1},{3,2},{4,3},{5,4},{6,5},{7,6},{9,8},{10,9},{11,10},{12... | collective-permute-start | bytes 24200 | tf_op jit(solution)/shard_map/ppermute | solution.py:33
  25.6 2.7 %collective-permute-done.3 = f32[3,16,14,3]{3,1,2,0:T(8,128)S(1)} collective-permute-done((f32[3,16,14,3]{3,1,2,0:T(8,128)S(1)}, f32[3,16,14,3]{3,1,2,0:T(8,128)S(1)}, u32[]{:S(2)}, u32[]{:S(2)}) %collective-permute-start.3) | collective-permute-done | bytes 8096 | tf_op jit(solution)/shard_map/ppermute | solution.py:33
  34.2 14.8 %all-to-all-start = ((f32[12,1,64]{2,1,0:T(1,128)}), f32[12,1,64]{2,1,0:T(1,128)}, u32[]{:S(2)}, u32[]{:S(2)}) async-start(f32[12,1,64]{2,1,0:T(1,128)} %broadcast_in_dim.187), calls=%async_computation | async-start | bytes 12288 | tf_op jit(solution)/shard_map/all_to_all | solution.py:125
  50.9 7.0 %all-to-all-done = f32[12,1,64]{2,1,0:T(1,128)} async-done(((f32[12,1,64]{2,1,0:T(1,128)}), f32[12,1,64]{2,1,0:T(1,128)}, u32[]{:S(2)}, u32[]{:S(2)}) %all-to-all-start) | async-done | bytes 3104 | tf_op jit(solution)/shard_map/all_to_all | solution.py:125
  59.3 6.8 %all-to-all-start.1 = ((f32[8,1,768]{2,1,0:T(1,128)}), f32[8,1,768]{2,1,0:T(1,128)}, u32[]{:S(2)}, u32[]{:S(2)}) async-start(f32[8,1,768]{2,1,0:T(1,128)} %broadcast_in_dim.189), calls=%async_computation.1 | async-start | bytes 49152 | tf_op jit(solution)/shard_map/all_to_all | solution.py:128
  67.9 5.0 %all-to-all-done.1 = f32[8,1,768]{2,1,0:T(1,128)} async-done(((f32[8,1,768]{2,1,0:T(1,128)}), f32[8,1,768]{2,1,0:T(1,128)}, u32[]{:S(2)}, u32[]{:S(2)}) %all-to-all-start.1) | async-done | bytes 24608 | tf_op jit(solution)/shard_map/all_to_all | solution.py:128
  77.3 2.3 %collective-permute-start.4 = (f32[16,3,128]{2,0,1:T(8,128)S(1)}, f32[16,3,128]{2,0,1:T(8,128)S(1)}, u32[]{:S(2)}, u32[]{:S(2)}) collective-permute-start(f32[16,3,128]{2,0,1:T(8,128)S(1)} %get-tuple-element.76), channel_id=1, source_target_pairs={{0,8},{8,16},{16,24},{24,32},{32,40},{40,48},{48,56},{56,64},{64,7... | collective-permute-start | bytes 73736 | tf_op jit(solution)/shard_map/ppermute | solution.py:32
  81.0 3.3 %collective-permute-done.5 = f32[16,3,128]{2,0,1:T(8,128)S(1)} collective-permute-done((f32[16,3,128]{2,0,1:T(8,128)S(1)}, f32[16,3,128]{2,0,1:T(8,128)S(1)}, u32[]{:S(2)}, u32[]{:S(2)}) %collective-permute-start.5) | collective-permute-done | bytes 24608 | tf_op jit(solution)/shard_map/ppermute | solution.py:33
  84.3 5.9 %collective-permute-start.6 = (f32[16,14,3]{2,0,1:T(8,128)S(1)}, f32[16,14,3]{2,0,1:T(8,128)S(1)}, u32[]{:S(2)}, u32[]{:S(2)}) collective-permute-start(f32[16,14,3]{2,0,1:T(8,128)S(1)} %get-tuple-element.66), channel_id=1, source_target_pairs={{0,1},{1,2},{2,3},{3,4},{4,5},{5,6},{6,7},{8,9},{9,10},{10,11},{11... | collective-permute-start | bytes 8072 | tf_op jit(solution)/shard_map/ppermute | solution.py:32
  90.2 1.9 collective-permute-start.7
  92.2 4.2 %collective-permute-done.7 = f32[16,14,3]{2,0,1:T(8,128)S(1)} collective-permute-done((f32[16,14,3]{2,0,1:T(8,128)S(1)}, f32[16,14,3]{2,0,1:T(8,128)S(1)}, u32[]{:S(2)}, u32[]{:S(2)}) %collective-permute-start.7) | collective-permute-done | bytes 2720 | tf_op jit(solution)/shard_map/ppermute | solution.py:33
  102.2 6.1 %all-to-all-start.2 = ((f32[12,1,64]{2,1,0:T(1,128)}), f32[12,1,64]{2,1,0:T(1,128)}, u32[]{:S(2)}, u32[]{:S(2)}) async-start(f32[12,1,64]{2,1,0:T(1,128)} %broadcast_in_dim.191), calls=%async_computation.2 | async-start | bytes 12288 | tf_op jit(solution)/shard_map/all_to_all | solution.py:125
  111.5 5.6 %all-to-all-done.2 = f32[12,1,64]{2,1,0:T(1,128)} async-done(((f32[12,1,64]{2,1,0:T(1,128)}), f32[12,1,64]{2,1,0:T(1,128)}, u32[]{:S(2)}, u32[]{:S(2)}) %all-to-all-start.2) | async-done | bytes 3104 | tf_op jit(solution)/shard_map/all_to_all | solution.py:125
  118.5 3.9 %all-to-all-start.3 = ((f32[8,1,768]{2,1,0:T(1,128)}), f32[8,1,768]{2,1,0:T(1,128)}, u32[]{:S(2)}, u32[]{:S(2)}) async-start(f32[8,1,768]{2,1,0:T(1,128)} %broadcast_in_dim.193), calls=%async_computation.3 | async-start | bytes 49152 | tf_op jit(solution)/shard_map/all_to_all | solution.py:128
  124.3 5.0 %all-to-all-done.3 = f32[8,1,768]{2,1,0:T(1,128)} async-done(((f32[8,1,768]{2,1,0:T(1,128)}), f32[8,1,768]{2,1,0:T(1,128)}, u32[]{:S(2)}, u32[]{:S(2)}) %all-to-all-start.3) | async-done | bytes 24608 | tf_op jit(solution)/shard_map/all_to_all | solution.py:128
  133.7 2.3 %collective-permute-start.8 = (f32[16,3,128]{2,0,1:T(8,128)S(1)}, f32[16,3,128]{2,0,1:T(8,128)S(1)}, u32[]{:S(2)}, u32[]{:S(2)}) collective-permute-start(f32[16,3,128]{2,0,1:T(8,128)S(1)} %get-tuple-element.74), channel_id=1, source_target_pairs={{0,8},{8,16},{16,24},{24,32},{32,40},{40,48},{48,56},{56,64},{64,7... | collective-permute-start | bytes 73736 | tf_op jit(solution)/shard_map/ppermute | solution.py:32
  137.3 3.3 %collective-permute-done.9 = f32[16,3,128]{2,0,1:T(8,128)S(1)} collective-permute-done((f32[16,3,128]{2,0,1:T(8,128)S(1)}, f32[16,3,128]{2,0,1:T(8,128)S(1)}, u32[]{:S(2)}, u32[]{:S(2)}) %collective-permute-start.9) | collective-permute-done | bytes 24608 | tf_op jit(solution)/shard_map/ppermute | solution.py:33
  140.7 5.7 %collective-permute-start.10 = (f32[16,14,3]{2,0,1:T(8,128)S(1)}, f32[16,14,3]{2,0,1:T(8,128)S(1)}, u32[]{:S(2)}, u32[]{:S(2)}) collective-permute-start(f32[16,14,3]{2,0,1:T(8,128)S(1)} %get-tuple-element.64), channel_id=1, source_target_pairs={{0,1},{1,2},{2,3},{3,4},{4,5},{5,6},{6,7},{8,9},{9,10},{10,11},{11... | collective-permute-start | bytes 8072 | tf_op jit(solution)/shard_map/ppermute | solution.py:32
  146.4 2.1 %collective-permute-start.11 = (f32[16,14,3]{2,0,1:T(8,128)S(1)}, f32[16,14,3]{2,0,1:T(8,128)S(1)}, u32[]{:S(2)}, u32[]{:S(2)}) collective-permute-start(f32[16,14,3]{2,0,1:T(8,128)S(1)} %get-tuple-element.65), channel_id=1, source_target_pairs={{1,0},{2,1},{3,2},{4,3},{5,4},{6,5},{7,6},{9,8},{10,9},{11,10},{12... | collective-permute-start | bytes 8072 | tf_op jit(solution)/shard_map/ppermute | solution.py:33
  148.5 4.0 %collective-permute-done.11 = f32[16,14,3]{2,0,1:T(8,128)S(1)} collective-permute-done((f32[16,14,3]{2,0,1:T(8,128)S(1)}, f32[16,14,3]{2,0,1:T(8,128)S(1)}, u32[]{:S(2)}, u32[]{:S(2)}) %collective-permute-start.11) | collective-permute-done | bytes 2720 | tf_op jit(solution)/shard_map/ppermute | solution.py:33
  158.3 5.9 %all-to-all-start.4 = ((f32[12,1,64]{2,1,0:T(1,128)}), f32[12,1,64]{2,1,0:T(1,128)S(1)}, u32[]{:S(2)}, u32[]{:S(2)}) async-start(f32[12,1,64]{2,1,0:T(1,128)} %broadcast_in_dim.195), calls=%async_computation.4 | async-start | bytes 12288 | tf_op jit(solution)/shard_map/all_to_all | solution.py:125
  167.5 5.7 %all-to-all-done.4 = f32[12,1,64]{2,1,0:T(1,128)S(1)} async-done(((f32[12,1,64]{2,1,0:T(1,128)}), f32[12,1,64]{2,1,0:T(1,128)S(1)}, u32[]{:S(2)}, u32[]{:S(2)}) %all-to-all-start.4) | async-done | bytes 3104 | tf_op jit(solution)/shard_map/all_to_all | solution.py:125
  173.9 3.3 %all-to-all-start.5 = ((f32[8,1,768]{2,1,0:T(1,128)}), f32[8,1,768]{2,1,0:T(1,128)S(1)}, u32[]{:S(2)}, u32[]{:S(2)}) async-start(f32[8,1,768]{2,1,0:T(1,128)} %broadcast_in_dim.197), calls=%async_computation.5 | async-start | bytes 49152 | tf_op jit(solution)/shard_map/all_to_all | solution.py:128
  179.1 4.8 %all-to-all-done.5 = f32[8,1,768]{2,1,0:T(1,128)S(1)} async-done(((f32[8,1,768]{2,1,0:T(1,128)}), f32[8,1,768]{2,1,0:T(1,128)S(1)}, u32[]{:S(2)}, u32[]{:S(2)}) %all-to-all-start.5) | async-done | bytes 24608 | tf_op jit(solution)/shard_map/all_to_all | solution.py:128
  186.3 2.2 %collective-permute-start.12 = (f32[16,1,128]{2,0,1:T(8,128)S(1)}, f32[16,1,128]{2,0,1:T(8,128)S(1)}, u32[]{:S(2)}, u32[]{:S(2)}) collective-permute-start(f32[16,1,128]{2,0,1:T(8,128)S(1)} %get-tuple-element.72), channel_id=1, source_target_pairs={{0,8},{8,16},{16,24},{24,32},{32,40},{40,48},{48,56},{56,64},{64,7... | collective-permute-start | bytes 24584 | tf_op jit(solution)/shard_map/ppermute | solution.py:32
  189.8 3.1 %collective-permute-done.13 = f32[16,1,128]{2,0,1:T(8,128)S(1)} collective-permute-done((f32[16,1,128]{2,0,1:T(8,128)S(1)}, f32[16,1,128]{2,0,1:T(8,128)S(1)}, u32[]{:S(2)}, u32[]{:S(2)}) %collective-permute-start.13) | collective-permute-done | bytes 8224 | tf_op jit(solution)/shard_map/ppermute | solution.py:33
  193.0 5.8 %collective-permute-start.14 = (f32[16,10,1]{2,0,1:T(8,128)S(1)}, f32[16,10,1]{2,0,1:T(8,128)S(1)}, u32[]{:S(2)}, u32[]{:S(2)}) collective-permute-start(f32[16,10,1]{2,0,1:T(8,128)S(1)} %get-tuple-element.68), channel_id=1, source_target_pairs={{0,1},{1,2},{2,3},{3,4},{4,5},{5,6},{6,7},{8,9},{9,10},{10,11},{11... | collective-permute-start | bytes 1928 | tf_op jit(solution)/shard_map/ppermute | solution.py:32
  198.8 1.9 collective-permute-start.15
  201.4 3.2 %collective-permute-done.15 = f32[16,10,1]{2,0,1:T(8,128)S(1)} collective-permute-done((f32[16,10,1]{2,0,1:T(8,128)S(1)}, f32[16,10,1]{2,0,1:T(8,128)S(1)}, u32[]{:S(2)}, u32[]{:S(2)}) %collective-permute-start.15) | collective-permute-done | bytes 672 | tf_op jit(solution)/shard_map/ppermute | solution.py:33
  (167 shorter events, 57.5 us)
Async XLA Ops:
  4.1 6.4 %collective-permute-start = (f32[3,16,3,128]{3,1,2,0:T(8,128)S(1)}, f32[3,16,3,128]{3,1,2,0:T(8,128)S(1)}, u32[]{:S(2)}, u32[]{:S(2)}) collective-permute-start(f32[3,16,3,128]{3,1,2,0:T(8,128)S(1)} %get-tuple-element.62), channel_id=1, source_target_pairs={{0,8},{8,16},{16,24},{24,32},{32,40},{40,48},{48,56},{56,64},{64,7... | collective-permute-start | bytes 221192 | tf_op jit(solution)/shard_map/ppermute | solution.py:32
  8.9 5.7 %collective-permute-start.1 = (f32[3,16,3,128]{3,1,2,0:T(8,128)S(1)}, f32[3,16,3,128]{3,1,2,0:T(8,128)S(1)}, u32[]{:S(2)}, u32[]{:S(2)}) collective-permute-start(f32[3,16,3,128]{3,1,2,0:T(8,128)S(1)} %get-tuple-element.63), channel_id=1, source_target_pairs={{8,0},{16,8},{24,16},{32,24},{40,32},{48,40},{56,48},{64,56},{72,6... | collective-permute-start | bytes 221192 | tf_op jit(solution)/shard_map/ppermute | solution.py:33
  10.3 22.7 %copy-start.5 = (f32[4]{0:T(128)}, f32[4]{0:T(128)S(1)}, u32[]{:S(2)}) copy-start(f32[4]{0:T(128)S(1)} %get-tuple-element.85) | copy-start | bytes 52
  10.3 22.7 %copy-start.8 = (f32[4]{0:T(128)}, f32[4]{0:T(128)S(1)}, u32[]{:S(2)}) copy-start(f32[4]{0:T(128)S(1)} %get-tuple-element.86) | copy-start | bytes 52
  10.3 22.9 %copy-start.12 = (f32[8]{0:T(128)}, f32[8]{0:T(128)S(1)}, u32[]{:S(2)}) copy-start(f32[8]{0:T(128)S(1)} %get-tuple-element.87) | copy-start | bytes 100
  10.3 22.9 %copy-start.16 = (f32[8]{0:T(128)}, f32[8]{0:T(128)S(1)}, u32[]{:S(2)}) copy-start(f32[8]{0:T(128)S(1)} %get-tuple-element.88) | copy-start | bytes 100
  10.5 22.5 %copy-start.20 = (f32[8]{0:T(128)}, f32[8]{0:T(128)S(1)}, u32[]{:S(2)}) copy-start(f32[8]{0:T(128)S(1)} %iota_add_fusion.1) | copy-start | bytes 100
  14.9 10.7 %collective-permute-start.2 = (f32[3,16,14,3]{3,1,2,0:T(8,128)S(1)}, f32[3,16,14,3]{3,1,2,0:T(8,128)S(1)}, u32[]{:S(2)}, u32[]{:S(2)}) collective-permute-start(f32[3,16,14,3]{3,1,2,0:T(8,128)S(1)} %get-tuple-element.36), channel_id=1, source_target_pairs={{0,1},{1,2},{2,3},{3,4},{4,5},{5,6},{6,7},{8,9},{9,10},{10,11},{11... | collective-permute-start | bytes 24200 | tf_op jit(solution)/shard_map/ppermute | solution.py:32
  19.7 8.6 %collective-permute-start.3 = (f32[3,16,14,3]{3,1,2,0:T(8,128)S(1)}, f32[3,16,14,3]{3,1,2,0:T(8,128)S(1)}, u32[]{:S(2)}, u32[]{:S(2)}) collective-permute-start(f32[3,16,14,3]{3,1,2,0:T(8,128)S(1)} %get-tuple-element.37), channel_id=1, source_target_pairs={{1,0},{2,1},{3,2},{4,3},{5,4},{6,5},{7,6},{9,8},{10,9},{11,10},{12... | collective-permute-start | bytes 24200 | tf_op jit(solution)/shard_map/ppermute | solution.py:33
  34.2 23.7 %all-to-all-start = ((f32[12,1,64]{2,1,0:T(1,128)}), f32[12,1,64]{2,1,0:T(1,128)}, u32[]{:S(2)}, u32[]{:S(2)}) async-start(f32[12,1,64]{2,1,0:T(1,128)} %broadcast_in_dim.187), calls=%async_computation | async-start | bytes 12288 | tf_op jit(solution)/shard_map/all_to_all | solution.py:125
  50.1 22.8 %copy-start = (f32[1,64,6144]{2,1,0:T(8,128)S(1)}, f32[1,64,6144]{2,1,0:T(8,128)}, u32[]{:S(2)}) copy-start(f32[1,64,6144]{2,1,0:T(8,128)} %param.9) | copy-start | bytes 4718596
  59.3 13.6 %all-to-all-start.1 = ((f32[8,1,768]{2,1,0:T(1,128)}), f32[8,1,768]{2,1,0:T(1,128)}, u32[]{:S(2)}, u32[]{:S(2)}) async-start(f32[8,1,768]{2,1,0:T(1,128)} %broadcast_in_dim.189), calls=%async_computation.1 | async-start | bytes 49152 | tf_op jit(solution)/shard_map/all_to_all | solution.py:128
  66.1 8.7 %copy-start.6 = (f32[4]{0:T(128)S(1)}, f32[4]{0:T(128)}, u32[]{:S(2)}) copy-start(f32[4]{0:T(128)} %copy-done.5) | copy-start | bytes 52
  77.3 19.4 %copy-start.3 = (f32[16,8,128]{2,0,1:T(8,128)}, f32[16,8,128]{2,0,1:T(8,128)S(1)}, u32[]{:S(2)}) copy-start(f32[16,8,128]{2,0,1:T(8,128)S(1)} %fusion.5) | copy-start | bytes 196612
  77.3 3.6 %collective-permute-start.4 = (f32[16,3,128]{2,0,1:T(8,128)S(1)}, f32[16,3,128]{2,0,1:T(8,128)S(1)}, u32[]{:S(2)}, u32[]{:S(2)}) collective-permute-start(f32[16,3,128]{2,0,1:T(8,128)S(1)} %get-tuple-element.76), channel_id=1, source_target_pairs={{0,8},{8,16},{16,24},{24,32},{32,40},{40,48},{48,56},{56,64},{64,7... | collective-permute-start | bytes 73736 | tf_op jit(solution)/shard_map/ppermute | solution.py:32
  79.6 4.6 %collective-permute-start.5 = (f32[16,3,128]{2,0,1:T(8,128)S(1)}, f32[16,3,128]{2,0,1:T(8,128)S(1)}, u32[]{:S(2)}, u32[]{:S(2)}) collective-permute-start(f32[16,3,128]{2,0,1:T(8,128)S(1)} %get-tuple-element.77), channel_id=1, source_target_pairs={{8,0},{16,8},{24,16},{32,24},{40,32},{48,40},{56,48},{64,56},{72,6... | collective-permute-start | bytes 73736 | tf_op jit(solution)/shard_map/ppermute | solution.py:33
  84.3 7.8 %collective-permute-start.6 = (f32[16,14,3]{2,0,1:T(8,128)S(1)}, f32[16,14,3]{2,0,1:T(8,128)S(1)}, u32[]{:S(2)}, u32[]{:S(2)}) collective-permute-start(f32[16,14,3]{2,0,1:T(8,128)S(1)} %get-tuple-element.66), channel_id=1, source_target_pairs={{0,1},{1,2},{2,3},{3,4},{4,5},{5,6},{6,7},{8,9},{9,10},{10,11},{11... | collective-permute-start | bytes 8072 | tf_op jit(solution)/shard_map/ppermute | solution.py:32
  90.2 6.1 %collective-permute-start.7 = (f32[16,14,3]{2,0,1:T(8,128)S(1)}, f32[16,14,3]{2,0,1:T(8,128)S(1)}, u32[]{:S(2)}, u32[]{:S(2)}) collective-permute-start(f32[16,14,3]{2,0,1:T(8,128)S(1)} %get-tuple-element.67), channel_id=1, source_target_pairs={{1,0},{2,1},{3,2},{4,3},{5,4},{6,5},{7,6},{9,8},{10,9},{11,10},{12... | collective-permute-start | bytes 8072 | tf_op jit(solution)/shard_map/ppermute | solution.py:33
  102.2 14.9 %all-to-all-start.2 = ((f32[12,1,64]{2,1,0:T(1,128)}), f32[12,1,64]{2,1,0:T(1,128)}, u32[]{:S(2)}, u32[]{:S(2)}) async-start(f32[12,1,64]{2,1,0:T(1,128)} %broadcast_in_dim.191), calls=%async_computation.2 | async-start | bytes 12288 | tf_op jit(solution)/shard_map/all_to_all | solution.py:125
  118.5 10.7 %all-to-all-start.3 = ((f32[8,1,768]{2,1,0:T(1,128)}), f32[8,1,768]{2,1,0:T(1,128)}, u32[]{:S(2)}, u32[]{:S(2)}) async-start(f32[8,1,768]{2,1,0:T(1,128)} %broadcast_in_dim.193), calls=%async_computation.3 | async-start | bytes 49152 | tf_op jit(solution)/shard_map/all_to_all | solution.py:128
  122.4 8.7 %copy-start.7 = (f32[4]{0:T(128)S(1)}, f32[4]{0:T(128)}, u32[]{:S(2)}) copy-start(f32[4]{0:T(128)} %copy-done.5) | copy-start | bytes 52
  133.6 19.2 %copy-start.1 = (f32[16,8,128]{2,0,1:T(8,128)}, f32[16,8,128]{2,0,1:T(8,128)S(1)}, u32[]{:S(2)}) copy-start(f32[16,8,128]{2,0,1:T(8,128)S(1)} %fusion.4) | copy-start | bytes 196612
  133.7 3.7 %collective-permute-start.8 = (f32[16,3,128]{2,0,1:T(8,128)S(1)}, f32[16,3,128]{2,0,1:T(8,128)S(1)}, u32[]{:S(2)}, u32[]{:S(2)}) collective-permute-start(f32[16,3,128]{2,0,1:T(8,128)S(1)} %get-tuple-element.74), channel_id=1, source_target_pairs={{0,8},{8,16},{16,24},{24,32},{32,40},{40,48},{48,56},{56,64},{64,7... | collective-permute-start | bytes 73736 | tf_op jit(solution)/shard_map/ppermute | solution.py:32
  136.0 4.6 %collective-permute-start.9 = (f32[16,3,128]{2,0,1:T(8,128)S(1)}, f32[16,3,128]{2,0,1:T(8,128)S(1)}, u32[]{:S(2)}, u32[]{:S(2)}) collective-permute-start(f32[16,3,128]{2,0,1:T(8,128)S(1)} %get-tuple-element.75), channel_id=1, source_target_pairs={{8,0},{16,8},{24,16},{32,24},{40,32},{48,40},{56,48},{64,56},{72,6... | collective-permute-start | bytes 73736 | tf_op jit(solution)/shard_map/ppermute | solution.py:33
  140.7 7.8 %collective-permute-start.10 = (f32[16,14,3]{2,0,1:T(8,128)S(1)}, f32[16,14,3]{2,0,1:T(8,128)S(1)}, u32[]{:S(2)}, u32[]{:S(2)}) collective-permute-start(f32[16,14,3]{2,0,1:T(8,128)S(1)} %get-tuple-element.64), channel_id=1, source_target_pairs={{0,1},{1,2},{2,3},{3,4},{4,5},{5,6},{6,7},{8,9},{9,10},{10,11},{11... | collective-permute-start | bytes 8072 | tf_op jit(solution)/shard_map/ppermute | solution.py:32
  146.4 6.1 %collective-permute-start.11 = (f32[16,14,3]{2,0,1:T(8,128)S(1)}, f32[16,14,3]{2,0,1:T(8,128)S(1)}, u32[]{:S(2)}, u32[]{:S(2)}) collective-permute-start(f32[16,14,3]{2,0,1:T(8,128)S(1)} %get-tuple-element.65), channel_id=1, source_target_pairs={{1,0},{2,1},{3,2},{4,3},{5,4},{6,5},{7,6},{9,8},{10,9},{11,10},{12... | collective-permute-start | bytes 8072 | tf_op jit(solution)/shard_map/ppermute | solution.py:33
  158.3 14.8 %all-to-all-start.4 = ((f32[12,1,64]{2,1,0:T(1,128)}), f32[12,1,64]{2,1,0:T(1,128)S(1)}, u32[]{:S(2)}, u32[]{:S(2)}) async-start(f32[12,1,64]{2,1,0:T(1,128)} %broadcast_in_dim.195), calls=%async_computation.4 | async-start | bytes 12288 | tf_op jit(solution)/shard_map/all_to_all | solution.py:125
  173.9 10.1 %all-to-all-start.5 = ((f32[8,1,768]{2,1,0:T(1,128)}), f32[8,1,768]{2,1,0:T(1,128)S(1)}, u32[]{:S(2)}, u32[]{:S(2)}) async-start(f32[8,1,768]{2,1,0:T(1,128)} %broadcast_in_dim.197), calls=%async_computation.5 | async-start | bytes 49152 | tf_op jit(solution)/shard_map/all_to_all | solution.py:128
  186.3 3.5 %collective-permute-start.12 = (f32[16,1,128]{2,0,1:T(8,128)S(1)}, f32[16,1,128]{2,0,1:T(8,128)S(1)}, u32[]{:S(2)}, u32[]{:S(2)}) collective-permute-start(f32[16,1,128]{2,0,1:T(8,128)S(1)} %get-tuple-element.72), channel_id=1, source_target_pairs={{0,8},{8,16},{16,24},{24,32},{32,40},{40,48},{48,56},{56,64},{64,7... | collective-permute-start | bytes 24584 | tf_op jit(solution)/shard_map/ppermute | solution.py:32
  188.5 4.4 %collective-permute-start.13 = (f32[16,1,128]{2,0,1:T(8,128)S(1)}, f32[16,1,128]{2,0,1:T(8,128)S(1)}, u32[]{:S(2)}, u32[]{:S(2)}) collective-permute-start(f32[16,1,128]{2,0,1:T(8,128)S(1)} %get-tuple-element.73), channel_id=1, source_target_pairs={{8,0},{16,8},{24,16},{32,24},{40,32},{48,40},{56,48},{64,56},{72,6... | collective-permute-start | bytes 24584 | tf_op jit(solution)/shard_map/ppermute | solution.py:33
  193.0 8.4 %collective-permute-start.14 = (f32[16,10,1]{2,0,1:T(8,128)S(1)}, f32[16,10,1]{2,0,1:T(8,128)S(1)}, u32[]{:S(2)}, u32[]{:S(2)}) collective-permute-start(f32[16,10,1]{2,0,1:T(8,128)S(1)} %get-tuple-element.68), channel_id=1, source_target_pairs={{0,1},{1,2},{2,3},{3,4},{4,5},{5,6},{6,7},{8,9},{9,10},{10,11},{11... | collective-permute-start | bytes 1928 | tf_op jit(solution)/shard_map/ppermute | solution.py:32
  198.8 5.8 %collective-permute-start.15 = (f32[16,10,1]{2,0,1:T(8,128)S(1)}, f32[16,10,1]{2,0,1:T(8,128)S(1)}, u32[]{:S(2)}, u32[]{:S(2)}) collective-permute-start(f32[16,10,1]{2,0,1:T(8,128)S(1)} %get-tuple-element.69), channel_id=1, source_target_pairs={{1,0},{2,1},{3,2},{4,3},{5,4},{6,5},{7,6},{9,8},{10,9},{11,10},{12... | collective-permute-start | bytes 1928 | tf_op jit(solution)/shard_map/ppermute | solution.py:33
  (18 other events, 99.3 us)

commit v2 on v0

v2 whole, which is shorter than its diff:
```python
import functools
import math

import jax
import jax.numpy as jnp
import numpy as np
from jax import lax
from jax.experimental import pallas as pl
from jax.experimental.pallas import tpu as pltpu
from jax.sharding import PartitionSpec as P

NZ = 16
CX = 8
CY = 128
OV = 2
SWEEPS = 3
CHEB = 4
MZ = 2
MX = 4
MY = 8
NB = 64
N_Z = 12
INVERSE_STEP = 0.004
CONTACT = 0.3
LOWER_BOUND = 0.1
UPPER_BOUND = 1.9

HALO = 13
ROWS = CX + 2 * HALO
FAR = HALO - CX
LANES = 256
STRIP = 16
WINDOW = 8
SPAN = 3
REACH = (8, 4, 0)
PACKS = 9


def cosine_table(mode_count, length):
    position = np.arange(length) + 0.5
    order = np.arange(mode_count)
    scaling = np.where(order == 0, math.sqrt(1.0 / length), math.sqrt(2.0 / length))
    return scaling[:, None] * np.cos(math.pi * order[:, None] * position[None, :] / length)


def tables():
    depth, first, second = cosine_table(MZ, NZ), cosine_table(MX, CX), cosine_table(MY, CY)
    flat = depth[0, 0]
    mix = np.zeros((NB, MZ * CX))
    rows = np.zeros((NB, CY))
    for s in range(MZ):
        for p in range(MX):
            for q in range(MY):
                n = (s * MX + p) * MY + q
                mix[n, s * CX : (s + 1) * CX] = first[p] * (flat if s == 0 else 1.0)
                rows[n] = second[q]
    half = np.zeros((2, CX, 2 * NB))
    spread = np.zeros((2 * NB, MZ, CY))
    for h in range(2):
        for s in range(MZ):
            for p in range(MX):
                for q in range(MY):
                    n = h * NB + (s * MX + p) * MY + q
                    half[h, :, n] = first[p]
                    spread[n, s] = second[q] * (flat if s == 0 else 1.0)
    own = np.zeros((2 * NB, MZ, LANES))
    own[:, :, :CY] = spread
    own[:, :, CY + 13 : CY + 16] = spread[:, :, 125:128]
    own[:, :, CY + 112 : CY + 115] = spread[:, :, 0:3]
    side = np.zeros((2, 2 * NB, MZ, CY))
    side[0, :, :, 96:112] = spread[:, :, 112:128]
    side[0, :, :, 125:128] = spread[:, :, 125:128]
    side[1, :, :, 16:32] = spread[:, :, 0:16]
    side[1, :, :, 0:3] = spread[:, :, 0:3]
    wave = np.broadcast_to(depth[1][:, None], (NZ, CY))
    mix = np.pad(mix, ((0, 0), (0, CY - MZ * CX)))
    parts = [own[:, s, k * CY : (k + 1) * CY] for s in range(MZ) for k in range(2)]
    parts += [side[:, :, s].reshape(4 * NB, CY) for s in range(MZ)]
    parts += [rows, mix, half.reshape(2 * CX, 2 * NB), wave]
    return np.concatenate(parts, axis=0).astype(np.float32)


OWN, SIDE, MOMENT, MIX, HALF, WAVE = 0, 512, 1024, 1088, 1152, 1168


def lane_shift(values, by):
    return pltpu.roll(values, by % values.shape[-1], axis=values.ndim - 1)


def depth_shift(values, by):
    return pltpu.roll(values, by % NZ, axis=0)


def lanes_in(shape, *ranges):
    lane = lax.broadcasted_iota(jnp.int32, shape, len(shape) - 1)
    inside = jnp.zeros(shape, jnp.bool_)
    for low, high in ranges:
        inside = inside | ((lane >= low) & (lane < high))
    return inside


def chebyshev():
    centre = (UPPER_BOUND + LOWER_BOUND) / 2.0
    radius = (UPPER_BOUND - LOWER_BOUND) / 2.0
    spread = centre / radius
    ratio = 1.0 / spread
    steps = []
    for _ in range(CHEB - 1):
        following = 1.0 / (2.0 * spread - ratio)
        steps.append((following * ratio, 2.0 * following / radius))
        ratio = following
    return 1.0 / centre, steps


def side_flux(values, south, below):
    across = south * (values - lane_shift(values, 1))
    upward = below * (values - depth_shift(values, 1))
    return (across - lane_shift(across, -1)) + (upward - depth_shift(upward, -1))


def spread_moments(r_row, table_ref, inv_ref, line_ref, out_ref):
    for x in range(CX):
        row = r_row(x)
        line_ref[x : x + 1, :] = jnp.sum(row, axis=0, keepdims=True)
        line_ref[CX + x : CX + x + 1, :] = jnp.sum(row * table_ref[WAVE : WAVE + NZ, :], axis=0, keepdims=True)
    mix = table_ref[MIX : MIX + NB, : MZ * CX]
    mixed = jnp.dot(mix, line_ref[...], precision=lax.Precision.HIGHEST, preferred_element_type=jnp.float32)
    moments = jnp.sum(mixed * table_ref[MOMENT : MOMENT + NB, :], axis=1, keepdims=True)
    column = jnp.broadcast_to(moments, (NB, CY))
    tiles = inv_ref.shape[1] // CY
    groups = tiles // 6
    out_ref[0, 0:1, :] = jnp.zeros((1, CY), jnp.float32)
    out_ref[groups - 1, WINDOW - 1 : WINDOW, :] = jnp.zeros((1, CY), jnp.float32)
    for t in range(tiles):
        total = jnp.sum(column * inv_ref[:, t * CY : (t + 1) * CY], axis=0, keepdims=True)
        for group in range(groups):
            place = t - (6 * group - 1)
            if 0 <= place < WINDOW:
                out_ref[group, place : place + 1, :] = total


def own_kernel(conc_ref, label_ref, out_ref, tail_ref, head_ref):
    for x in range(CX):
        for kind, values in enumerate((conc_ref[:, x, :], label_ref[:, x, :].astype(jnp.float32))):
            out_ref[kind, x] = values
            if x >= CX - FAR:
                tail_ref[kind, x - (CX - FAR)] = values
            if x < FAR:
                head_ref[kind, x] = values


def stage_kernel(_, scale_ref, slope_ref, inv_hbm, table_hbm, curve_ref, inv_ref, table_ref, sems):
    copies = [
        pltpu.make_async_copy(inv_hbm, inv_ref, sems.at[0]),
        pltpu.make_async_copy(table_hbm, table_ref, sems.at[1]),
    ]
    for copy in copies:
        copy.start()
    for n, ref in enumerate((scale_ref, slope_ref)):
        for k in range(8):
            curve_ref[8 * n + k : 8 * n + k + 1, :] = jnp.full((1, LANES), ref[k], jnp.float32)
    for copy in copies:
        copy.wait()


def pieces(refs):
    far_low, low, own, high, far_high = refs

    def at(kind, row):
        if row < FAR:
            return far_low[kind, row]
        if row < HALO:
            return low[kind, row - FAR]
        if row < HALO + CX:
            return own[kind, row - HALO]
        if row < HALO + 2 * CX:
            return high[kind, row - HALO - CX]
        return far_high[kind, row - HALO - 2 * CX]

    return at


def strip_kernel(far_low, low, own, high, far_high, up_ref, down_ref):
    at = pieces((far_low, low, own, high, far_high))
    for pack in range(PACKS):
        up = jnp.zeros((NZ, CY), jnp.float32)
        down = jnp.zeros((NZ, CY), jnp.float32)
        for slot in range(8):
            index = pack * 8 + slot
            if index < 2 * ROWS:
                values = at(index // ROWS, index % ROWS)
                mask = lanes_in((NZ, CY), (slot * STRIP, (slot + 1) * STRIP))
                up = jnp.where(mask, lane_shift(values, slot * STRIP - (CY - STRIP)), up)
                down = jnp.where(mask, lane_shift(values, slot * STRIP), down)
        up_ref[pack] = up
        down_ref[pack] = down


def setup_kernel(
    curve_ref, inv_ref, table_ref, far_low, low, own, high, far_high, left_ref, right_ref,
    west_out, south_out, below_out, inverse_out, source_out, out_ref,
    conc, label, coeff, line_ref,
):
    at = pieces((far_low, low, own, high, far_high))
    tile = (NZ, CY)
    m_right, m_right_own = lanes_in(tile, (16, 32)), lanes_in(tile, (0, 3))
    m_left, m_left_own = lanes_in(tile, (96, 112)), lanes_in(tile, (125, 128))
    m_end, m_start = lanes_in(tile, (13, 16)), lanes_in(tile, (112, 115))
    zero = jnp.zeros(tile, jnp.float32)
    for kind, target in ((0, conc), (1, label)):
        for row in range(ROWS):
            index = kind * ROWS + row
            values = at(kind, row)
            from_left, from_right = left_ref[index // 8], right_ref[index // 8]
            slot = (index % 8) * STRIP
            second = jnp.where(m_right, lane_shift(from_right, 16 - slot), zero)
            second = jnp.where(m_right_own, lane_shift(from_right, -slot), second)
            second = jnp.where(m_left, lane_shift(from_left, 96 - slot), second)
            second = jnp.where(m_left_own, lane_shift(from_left, 112 - slot), second)
            second = jnp.where(m_end, lane_shift(values, 16), second)
            second = jnp.where(m_start, lane_shift(values, -16), second)
            target[row, :, :CY] = values
            target[row, :, CY:] = second

    def diffusivity(row, _):
        kind = label[row].astype(jnp.int32) & 7
        bits = [(kind & (1 << b)) != 0 for b in range(3)]

        def pick(table):
            layer = [jnp.broadcast_to(curve_ref[table + k : table + k + 1, :], (NZ, LANES)) for k in range(8)]
            for bit in bits:
                layer = [jnp.where(bit, layer[2 * n + 1], layer[2 * n]) for n in range(len(layer) // 2)]
            return layer[0]

        coeff[row] = pick(0) * jnp.exp(pick(8) * conc[row])
        return 0

    lax.fori_loop(0, ROWS, diffusivity, 0)

    def pair(a, b, la, lb):
        weight = jnp.where(la == lb, 0.5, 0.5 * CONTACT)
        return jnp.where((la > 0.5) & (lb > 0.5), weight * (a + b), 0.0)

    not_bottom = lax.broadcasted_iota(jnp.int32, (NZ, LANES), 0) > 0
    west_out[0] = jnp.zeros((NZ, LANES), jnp.float32)

    def faces(row, _):
        a, la = coeff[row], label[row]

        @pl.when(row > 0)
        def _():
            west_out[row] = pair(a, coeff[row - 1], la, label[row - 1])

        south_out[row] = pair(a, lane_shift(a, 1), la, lane_shift(la, 1))
        below_out[row] = jnp.where(not_bottom, pair(a, depth_shift(a, 1), la, depth_shift(la, 1)), 0.0)
        return 0

    lax.fori_loop(0, ROWS, faces, 0)
    box = lanes_in((NZ, LANES), (0, 130), (142, 160), (224, 242), (254, 256))

    def operator(row, _):
        following = jnp.minimum(row + 1, ROWS - 1)
        before = jnp.maximum(row - 1, 0)
        west, east, south, below, c = west_out[row], west_out[following], south_out[row], below_out[row], conc[row]
        diagonal = INVERSE_STEP + west + east + south + lane_shift(south, -1) + below + depth_shift(below, -1)
        inverse_out[row] = jnp.where(box, 1.0 / diagonal, 0.0)
        flux = west * (c - conc[before]) - east * (conc[following] - c) + side_flux(c, south, below)
        source_out[row] = -flux
        return 0

    lax.fori_loop(0, ROWS, operator, 0)
    spread_moments(lambda x: source_out[HALO + x, :, :CY], table_ref, inv_ref, line_ref, out_ref)


def local_kernel(_, r_ref, west_ref, south_ref, below_ref, inverse_ref, out_ref, u_ref, q_ref, x_ref, *, wide):
    scaled, steps = chebyshev()
    plus = lanes_in((NZ, LANES), (253, 256), (141, 144))
    minus = lanes_in((NZ, LANES), (128, 131), (240, 243))
    for block in range(-2, 3):
        low, high = max(-wide, 8 * block), min(CX - 1 + wide, 8 * block + 7)
        if low > high:
            continue
        box_low, box_high = max(8 * block - OV, -HALO), min(8 * block + 7 + OV, CX - 1 + HALO)

        def start(row):
            if not box_low <= row <= box_high:
                return None
            return scaled * inverse_ref[row + HALO] * r_ref[row + HALO]

        for number, (keep, gain) in enumerate(steps):
            more = len(steps) - 1 - number
            first, last = max(low - more, box_low), min(high + more, box_high)

            def held(row):
                if not box_low <= row <= box_high:
                    return None
                return u_ref[row - box_low]

            fetch = start if number == 0 else held
            now, before = fetch(first), fetch(first - 1)
            flow = west_ref[first + HALO] * (now if before is None else now - before)
            for row in range(first, last + 1):
                following = fetch(row + 1)
                if row + 1 + HALO < ROWS:
                    gate = west_ref[row + 1 + HALO]
                    onward = gate * (-now if following is None else following - now)
                else:
                    onward = jnp.zeros_like(now)
                place = row - box_low
                applied = INVERSE_STEP * now + (flow - onward)
                applied = applied + side_flux(now, south_ref[row + HALO], below_ref[row + HALO])
                remain = (r_ref[row + HALO] if number == 0 else q_ref[place]) - applied
                step = keep * now + gain * (inverse_ref[row + HALO] * remain)
                result = (now if number == 0 else x_ref[place]) + step
                if more:
                    u_ref[place] = step
                    q_ref[place] = remain
                    x_ref[place] = result
                else:
                    merged = jnp.where(plus, lane_shift(result, 16), result)
                    out_ref[row + HALO] = jnp.where(minus, lane_shift(result, -16), merged)
                now, flow = following, onward


def turn_kernel(in_ref, out_ref):
    total = in_ref[0]
    for peer in range(1, in_ref.shape[0]):
        total = total + in_ref[peer]
    for z in range(N_Z):
        out_ref[z] = total[z // 2 : z // 2 + SPAN, :]


def answer_kernel(in_ref, out_ref):
    total = in_ref[0]
    for peer in range(1, N_Z):
        total = total + in_ref[peer]
    out_ref[...] = total


def coarse_rows(odd, answers, table_ref, flat_ref, wavy_ref):
    def weighted(answer):
        blocks = []
        for block in range(5):
            choice = []
            for index in (block, block + 1):
                row = jnp.broadcast_to(answer[index // 2 : index // 2 + 1, :], (CX, 2 * NB))
                choice.append(row * table_ref[HALF + (index % 2) * CX : HALF + (index % 2 + 1) * CX, :])
            blocks.append(jnp.where(odd, choice[1], choice[0]))
        return jnp.concatenate(blocks, axis=0)

    left, own, right = (weighted(a[...]) for a in answers)
    dot = functools.partial(jnp.dot, precision=lax.Precision.HIGHEST, preferred_element_type=jnp.float32)
    own_at = lambda n: dot(own, table_ref[OWN + n * CY : OWN + (n + 1) * CY, :])
    for s, target in enumerate((flat_ref, wavy_ref)):
        first = SIDE + s * 4 * NB
        beside = dot(left, table_ref[first : first + CY, :]) + dot(right, table_ref[first + CY : first + 2 * CY, :])
        target[:, :CY] = own_at(2 * s)
        target[:, CY:] = own_at(2 * s + 1) + beside


def update_kernel(*refs, reach, first):
    refs = list(refs)
    take = lambda count: [refs.pop(0) for _ in range(count)]
    odd_ref, left_ref, own_ref, right_ref = take(4)
    x_ref, source_ref, west_ref, south_ref, below_ref = take(5)
    (table_ref,) = take(1)
    (old_ref,) = take(0 if first else 1) or (None,)
    if reach:
        (inv_ref,) = take(1)
        u_ref, r_ref, out_ref = take(3)
        flat_ref, wavy_ref, line_ref = take(3)
    else:
        (packed_ref,) = take(1)
        updated_ref, residual_ref = take(2)
        flat_ref, wavy_ref = take(2)
        u_ref = None
    coarse_rows(odd_ref[0] == 1, (left_ref, own_ref, right_ref), table_ref, flat_ref, wavy_ref)
    wave = table_ref[WAVE : WAVE + NZ, :]
    wave = jnp.concatenate([wave, wave], axis=1)

    def fresh(row):
        place = row + 2 * CX
        field = jnp.broadcast_to(flat_ref[place : place + 1, :], (NZ, LANES))
        field = field + wave * jnp.broadcast_to(wavy_ref[place : place + 1, :], (NZ, LANES))
        value = x_ref[row + HALO] + field
        if not first:
            value = old_ref[row + HALO] + value
        if u_ref is not None:
            u_ref[row + HALO] = value
        return value

    before, now = fresh(-reach - 1), fresh(-reach)
    flow = west_ref[HALO - reach] * (now - before)
    for row in range(-reach, CX + reach):
        following = fresh(row + 1)
        onward = west_ref[row + 1 + HALO] * (following - now)
        applied = INVERSE_STEP * now + (flow - onward)
        applied = applied + side_flux(now, south_ref[row + HALO], below_ref[row + HALO])
        remain = source_ref[row + HALO] - applied
        if reach:
            r_ref[row + HALO] = remain
        else:
            updated_ref[:, row, :] = packed_ref[0, row] + now[:, :CY]
            residual_ref[:, row, :] = remain[:, :CY]
        now, flow = following, onward
    if reach:
        spread_moments(lambda x: r_ref[HALO + x, :, :CY], table_ref, inv_ref, line_ref, out_ref)


def vmem(count):
    return [pl.BlockSpec(memory_space=pltpu.VMEM)] * count


def shaped(*shape):
    return jax.ShapeDtypeStruct(shape, jnp.float32)


def moved(array, axis, by):
    size = lax.axis_size(axis)
    pairs = [(i, i + by) for i in range(size) if 0 <= i + by < size]
    return lax.ppermute(array, axis, pairs)


def room(mebibytes):
    return pltpu.CompilerParams(vmem_limit_bytes=mebibytes * 2**20)


def cost(flops):
    return pl.CostEstimate(flops=flops, bytes_accessed=4_000_000, transcendentals=0)


def on_device(concentration, labels, curve_scale, curve_slope, coarse_inv):
    size = lax.axis_size("gx")
    n_y = size // N_Z
    along_z = [[y * N_Z + z for z in range(N_Z)] for y in range(n_y)]
    along_y = [[y * N_Z + z for y in range(n_y)] for z in range(N_Z)]
    odd = (lax.axis_index("gx") & 1).astype(jnp.int32).reshape(1)
    odd, concentration = lax.optimization_barrier((odd, concentration))
    frame = shaped(ROWS, NZ, LANES)
    smem, anywhere = pl.BlockSpec(memory_space=pltpu.SMEM), pl.BlockSpec(memory_space=pl.ANY)
    hbm = pl.BlockSpec(memory_space=pltpu.HBM)
    scratch = lambda *shape: pltpu.VMEM(shape, jnp.float32)
    line_scratch = scratch(MZ * CX, CY)
    table_scratch = [scratch(5 * CX, LANES)] * 2

    own, tail, head = pl.pallas_call(
        own_kernel,
        out_shape=[shaped(2, CX, NZ, CY), shaped(2, FAR, NZ, CY), shaped(2, FAR, NZ, CY)],
        in_specs=vmem(2),
        out_specs=vmem(3),
        compiler_params=room(4),
        name="own",
    )(concentration, labels)
    low, high = moved(own, "gx", 1), moved(own, "gx", -1)
    far_low, far_high = moved(tail, "gx", 2), moved(head, "gx", -2)
    curve, inverse_rows, table = pl.pallas_call(
        stage_kernel,
        out_shape=[shaped(16, LANES), shaped(NB, NB * size), shaped(WAVE + NZ, CY)],
        in_specs=[anywhere, smem, smem, hbm, hbm],
        out_specs=vmem(3),
        scratch_shapes=[pltpu.SemaphoreType.DMA((2,))],
        compiler_params=room(4),
        cost_estimate=cost(1_000_000),
        name="stage",
    )(own, curve_scale, curve_slope, coarse_inv[0], jnp.asarray(tables()))
    parts = (far_low, low, own, high, far_high)
    up, down = pl.pallas_call(
        strip_kernel,
        out_shape=[shaped(PACKS, NZ, CY)] * 2,
        in_specs=vmem(5),
        out_specs=vmem(2),
        compiler_params=room(4),
        name="strips",
    )(*parts)
    left, right = moved(up, "gy", 1), moved(down, "gy", -1)
    west, south, below, inverse, source, partial = pl.pallas_call(
        setup_kernel,
        out_shape=[frame] * 5 + [shaped(n_y, WINDOW, CY)],
        in_specs=vmem(10),
        out_specs=vmem(6),
        scratch_shapes=[scratch(ROWS, NZ, LANES)] * 3 + [line_scratch],
        compiler_params=room(8),
        name="setup",
    )(curve, inverse_rows, table, *parts, left, right)

    residual, update = source, None
    for sweep, reach in enumerate(REACH):
        through = lax.all_to_all(partial, "gx", 0, 0, tiled=True, axis_index_groups=along_y)
        turned = pl.pallas_call(
            turn_kernel,
            out_shape=shaped(N_Z, SPAN, CY),
            in_specs=vmem(1),
            out_specs=vmem(1)[0],
            compiler_params=room(4),
            name="turn",
        )(through)
        arrived = lax.all_to_all(turned, "gx", 0, 0, tiled=True, axis_index_groups=along_z)
        answer = pl.pallas_call(
            answer_kernel,
            out_shape=shaped(SPAN, CY),
            in_specs=vmem(1),
            out_specs=vmem(1)[0],
            compiler_params=room(4),
            name="answer",
        )(arrived)
        answers = (moved(answer, "gy", 1), answer, moved(answer, "gy", -1))
        local = pl.pallas_call(
            functools.partial(local_kernel, wide=reach + 1),
            out_shape=frame,
            in_specs=[anywhere] + vmem(5),
            out_specs=vmem(1)[0],
            scratch_shapes=[scratch(CX + 2 * OV, NZ, LANES)] * 3,
            compiler_params=room(8),
            cost_estimate=cost(20_000_000),
            name="local",
        )(answer, residual, west, south, below, inverse)
        operands = [odd, *answers, local, source, west, south, below, table]
        operands += [] if sweep == 0 else [update]
        kernel = functools.partial(update_kernel, reach=reach, first=sweep == 0)
        if reach:
            operands += [inverse_rows]
            update, residual, partial = pl.pallas_call(
                kernel,
                out_shape=[frame, frame, shaped(n_y, WINDOW, CY)],
                in_specs=[smem] + vmem(len(operands) - 1),
                out_specs=vmem(3),
                scratch_shapes=table_scratch + [line_scratch],
                compiler_params=room(8),
                name="update",
            )(*operands)
        else:
            operands += [own]
            return pl.pallas_call(
                kernel,
                out_shape=[shaped(NZ, CX, CY)] * 2,
                in_specs=[smem] + vmem(len(operands) - 1),
                out_specs=vmem(2),
                scratch_shapes=table_scratch,
                compiler_params=room(8),
                name="final",
            )(*operands)


def solution(mesh):
    return jax.shard_map(
        on_device,
        mesh=mesh,
        in_specs=(P(None, "gx", "gy"), P(None, "gx", "gy"), P(), P(), P("gy", "gx", None)),
        out_specs=(P(None, "gx", "gy"), P(None, "gx", "gy")),
        check_vma=False,
    )
```

time: 1430 us -> 163 us (0.11); the launches traced: 1410 us -> 162 us
  blocking collectives: 1000 us -> 76.9 us
  starting transfers between devices: 298 us -> 43.4 us
  matrix products: 43.5 us -> 0 us
  Pallas kernels: 0 us -> 27.5 us
  waiting for transfers between devices: 32.3 us -> 7.57 us
  other arithmetic: 15 us -> 0 us
    unnamed x3 -> x0, blocking collectives: 1000 us -> none
    ppermute x24 -> x12, starting transfers between devices: 298 us -> 43.4 us  [moved(): return lax.ppermute(array, axis, pairs)]
    all_to_all x0 -> x6, blocking collectives: none -> 76.9 us  [the longest x3 38.5 us: on_device(): lax.all_to_all(partial, 'gx', 0, 0, tiled=True, axis_index_groups=along_y)]
    dot_general x21 -> x0, matrix products: 43.5 us -> none  [the longest x3 31.2 us: coarse_part(): jnp.dot(own_rows, lax.all_gather(moments, 'gx', axis=0, tiled=True), prec...]
    pallas_call x0 -> x16, Pallas kernels: none -> 27.5 us  [the longest x3 11.8 us: on_device(): pl.pallas_call(functools.partial(local_kernel, wide=reach + 1), out_shape...]
    ppermute x24 -> x12, waiting for transfers between devices: 32.3 us -> 7.57 us  [moved(): return lax.ppermute(array, axis, pairs)]
  transfers between devices with their start and end apart: 24 -> 12, of which waited for: 10 -> 2; matrix products, arithmetic and copies ran while one was open for 2% -> 0% of each run, Pallas kernels for 0% -> 8%
where the time goes in v2:
time: 163 us; the launch traced here: 162 us
  blocking collectives  76.9 us (47%)
  starting transfers between devices  43.4 us (27%)
  Pallas kernels  27.5 us (17%)
  waiting for transfers between devices  7.57 us (5%)
  local copies, waits for them, and re-layouts  5.45 us (3%)
    ppermute x12, starting transfers between devices, moved(): return lax.ppermute(array, axis, pairs)  43.4 us
    all_to_all x3, blocking collectives, on_device(): lax.all_to_all(partial, 'gx', 0, 0, tiled=True, axis_index_groups=along_y)  38.5 us
    all_to_all x3, blocking collectives, on_device(): lax.all_to_all(turned, 'gx', 0, 0, tiled=True, axis_index_groups=along_z)  38.5 us
    pallas_call x3, Pallas kernels, on_device(): pl.pallas_call(functools.partial(local_kernel, wide=reach + 1), out_shape...  11.8 us
    pallas_call x1, Pallas kernels, on_device(): pl.pallas_call(setup_kernel, out_shape=[frame] * 5 + [shaped(n_y, WINDOW,...  10.2 us
    ppermute x12, waiting for transfers between devices, moved(): return lax.ppermute(array, axis, pairs)  7.57 us
    unnamed x12, local copies, waits for them, and re-layouts  5.45 us
  transfers between devices with their start and end apart: 12, of which 2 were waited for; matrix products, arithmetic and copies ran while one was open for 0% of the time, Pallas kernels for 8%

profile of v2, /device:TPU:1, one launch (start us, length us, event | category | flops | bytes accessed | tf_op | source)
XLA Modules:
  0.0 161.8 jit_solution(740795096676938482)
XLA Ops:
  0.6 0.8 copy-done.2
  1.5 0.8 copy-done.3
  2.4 1.3 collective-permute-start.2
  3.7 5.5 %collective-permute-start.1 = (f32[2,8,16,128]{3,2,1,0:T(8,128)S(1)}, f32[2,8,16,128]{3,2,1,0:T(8,128)S(1)}, u32[]{:S(2)}, u32[]{:S(2)}) collective-permute-start(f32[2,8,16,128]{3,2,1,0:T(8,128)S(1)} %get-tuple-element.26._.own.refs_11_), channel_id=1, source_target_pairs={{0,8},{8,16},{16,24},{24,32},{32,40},{40,48},{48,56},{56,64},{64,7... | collective-permute-start | bytes 393224 | tf_op jit(solution)/shard_map/ppermute | solution.py:421
  9.2 5.8 %collective-permute-start = (f32[2,5,16,128]{3,2,1,0:T(8,128)S(1)}, f32[2,5,16,128]{3,2,1,0:T(8,128)S(1)}, u32[]{:S(2)}, u32[]{:S(2)}) collective-permute-start(f32[2,5,16,128]{3,2,1,0:T(8,128)S(1)} %get-tuple-element.30), channel_id=1, source_target_pairs={{0,16},{8,24},{16,32},{24,40},{32,48},{40,56},{48,64},{56,72},{64,... | collective-permute-start | bytes 245768 | tf_op jit(solution)/shard_map/ppermute | solution.py:421
  15.0 1.3 collective-permute-start.3
  16.4 7.4 %collective-permute-done.3.far_high = f32[2,5,16,128]{3,2,1,0:T(8,128)S(1)} collective-permute-done((f32[2,5,16,128]{3,2,1,0:T(8,128)S(1)}, f32[2,5,16,128]{3,2,1,0:T(8,128)S(1)}, u32[]{:S(2)}, u32[]{:S(2)}) %collective-permute-start.3) | collective-permute-done | bytes 81952 | tf_op jit(solution)/shard_map/ppermute | solution.py:421
  24.1 6.0 %collective-permute-start.4 = (f32[9,16,128]{2,1,0:T(8,128)S(1)}, f32[9,16,128]{2,1,0:T(8,128)S(1)}, u32[]{:S(2)}, u32[]{:S(2)}) collective-permute-start(f32[9,16,128]{2,1,0:T(8,128)S(1)} %get-tuple-element.32), channel_id=1, source_target_pairs={{0,1},{1,2},{2,3},{3,4},{4,5},{5,6},{6,7},{8,9},{9,10},{10,11},{11... | collective-permute-start | bytes 221192 | tf_op jit(solution)/shard_map/ppermute | solution.py:421
  30.1 1.9 %collective-permute-start.5 = (f32[9,16,128]{2,1,0:T(8,128)S(1)}, f32[9,16,128]{2,1,0:T(8,128)S(1)}, u32[]{:S(2)}, u32[]{:S(2)}) collective-permute-start(f32[9,16,128]{2,1,0:T(8,128)S(1)} %get-tuple-element.33), channel_id=1, source_target_pairs={{1,0},{2,1},{3,2},{4,3},{5,4},{6,5},{7,6},{9,8},{10,9},{11,10},{12... | collective-permute-start | bytes 221192 | tf_op jit(solution)/shard_map/ppermute | solution.py:421
  32.1 1.4 copy-done
  33.5 1.1 copy-done.1
  34.6 0.7 copy-done.4
  35.9 0.8 stage.1
  36.7 10.2 %setup.1 = (f32[34,16,256]{2,1,0:T(8,128)S(1)}, f32[34,16,256]{2,1,0:T(8,128)S(1)}, f32[34,16,256]{2,1,0:T(8,128)S(1)}, f32[34,16,256]{2,1,0:T(8,128)S(1)}, f32[...) custom-call(f32[16,256]{1,0:T(8,128)S(1)} %get-tuple-element.27.curve_ref, ...), custom_call_target="tpu_custom_call" | custom-call | tf_op jit(solution)/shard_map/setup/pallas_call | solution.py:476
  46.9 20.0 %all_to_all.30.in_ref = f32[8,8,128]{2,1,0:T(8,128)S(1)} all-to-all(f32[8,8,128]{2,1,0:T(8,128)S(1)} %get-tuple-element.34), channel_id=1, replica_groups={{0,96,192,288,384,480,576,672},{8,104,200,296,392,488,584,680},{16,112,..., dimensions={0} | all-to-all | bytes 65536 | tf_op jit(solution)/shard_map/all_to_all | solution.py:488
  66.9 14.9 %all_to_all.31.in_ref = f32[12,3,128]{2,1,0:T(4,128)S(1)} all-to-all(f32[12,3,128]{2,1,0:T(4,128)S(1)} %turn.3), channel_id=1, replica_groups={{0,8,16,24,32,40,48,56,64,72,80,88},{96,104,112,120,128,136,144,152,160..., dimensions={0} | all-to-all | bytes 36864 | tf_op jit(solution)/shard_map/all_to_all | solution.py:497
  81.8 1.9 %collective-permute-start.7 = (f32[3,128]{1,0:T(4,128)S(1)}, f32[3,128]{1,0:T(4,128)S(1)}, u32[]{:S(2)}, u32[]{:S(2)}) collective-permute-start(f32[3,128]{1,0:T(4,128)S(1)} %answer.3._.refs_2_), channel_id=1, source_target_pairs={{1,0},{2,1},{3,2},{4,3},{5,4},{6,5},{7,6},{9,8},{10,9},{11,10},{12... | collective-permute-start | bytes 4616 | tf_op jit(solution)/shard_map/ppermute | solution.py:421
  83.7 6.2 %collective-permute-start.6 = (f32[3,128]{1,0:T(4,128)S(1)}, f32[3,128]{1,0:T(4,128)S(1)}, u32[]{:S(2)}, u32[]{:S(2)}) collective-permute-start(f32[3,128]{1,0:T(4,128)S(1)} %answer.3._.refs_2_), channel_id=1, source_target_pairs={{0,1},{1,2},{2,3},{3,4},{4,5},{5,6},{6,7},{8,9},{9,10},{10,11},{11... | collective-permute-start | bytes 4616 | tf_op jit(solution)/shard_map/ppermute | solution.py:421
  90.0 6.8 %local.3.refs_4_ = f32[34,16,256]{2,1,0:T(8,128)S(1)} custom-call(f32[3,128]{1,0:T(4,128)S(1)} %answer.3._.refs_2_, f32[34,16,256]{2,1,0:T(8,128)S(1)} %get-tuple-element.35.r_ref.refs_5_, f32[34,16,256]{2,1,0:T(8,128)S(1)} %get-tuple-element.36.west_ref.refs_6_, f32[34,16,256]{2,1,0:T(8,128)S(1)} %get-tuple-element.37.south_ref.refs_7_, ...), custom_call_target="tpu_custom_call" | custom-call | flops 20000000 | bytes 4000000 | tf_op jit(solution)/shard_map/local/pallas_call | solution.py:507
  96.8 1.7 %update.2 = (f32[34,16,256]{2,1,0:T(8,128)S(1)}, f32[34,16,256]{2,1,0:T(8,128)S(1)}, f32[8,8,128]{2,1,0:T(8,128)S(1)}) custom-call(s32[1]{0:T(128)} %bitcast.refs_0_, f32[3,128]{1,0:T(4,128)S(1)} %collective-permute-done.6.refs_1_, f32[3,128]{1,0:T(4,128)S(1)} %answer.3._.refs_2_, f32[3,128]{1,0:T(4,128)S(1)} %collective-permute-done.7.refs_3_, ...), custom_call_target="tpu_custom_call" | custom-call | tf_op jit(solution)/shard_map/update/pallas_call | solution.py:522
  98.5 9.2 %all_to_all.32.in_ref = f32[8,8,128]{2,1,0:T(8,128)S(1)} all-to-all(f32[8,8,128]{2,1,0:T(8,128)S(1)} %get-tuple-element.40), channel_id=1, replica_groups={{0,96,192,288,384,480,576,672},{8,104,200,296,392,488,584,680},{16,112,..., dimensions={0} | all-to-all | bytes 65536 | tf_op jit(solution)/shard_map/all_to_all | solution.py:488
  107.8 11.8 %all_to_all.33.in_ref = f32[12,3,128]{2,1,0:T(4,128)S(1)} all-to-all(f32[12,3,128]{2,1,0:T(4,128)S(1)} %turn.4), channel_id=1, replica_groups={{0,8,16,24,32,40,48,56,64,72,80,88},{96,104,112,120,128,136,144,152,160..., dimensions={0} | all-to-all | bytes 36864 | tf_op jit(solution)/shard_map/all_to_all | solution.py:497
  119.6 1.9 %collective-permute-start.9 = (f32[3,128]{1,0:T(4,128)S(1)}, f32[3,128]{1,0:T(4,128)S(1)}, u32[]{:S(2)}, u32[]{:S(2)}) collective-permute-start(f32[3,128]{1,0:T(4,128)S(1)} %answer.4._.refs_2_), channel_id=1, source_target_pairs={{1,0},{2,1},{3,2},{4,3},{5,4},{6,5},{7,6},{9,8},{10,9},{11,10},{12... | collective-permute-start | bytes 4616 | tf_op jit(solution)/shard_map/ppermute | solution.py:421
  121.5 4.8 %collective-permute-start.8 = (f32[3,128]{1,0:T(4,128)S(1)}, f32[3,128]{1,0:T(4,128)S(1)}, u32[]{:S(2)}, u32[]{:S(2)}) collective-permute-start(f32[3,128]{1,0:T(4,128)S(1)} %answer.4._.refs_2_), channel_id=1, source_target_pairs={{0,1},{1,2},{2,3},{3,4},{4,5},{5,6},{6,7},{8,9},{9,10},{10,11},{11... | collective-permute-start | bytes 4616 | tf_op jit(solution)/shard_map/ppermute | solution.py:421
  126.3 3.4 %local.4.refs_4_ = f32[34,16,256]{2,1,0:T(8,128)S(1)} custom-call(f32[3,128]{1,0:T(4,128)S(1)} %answer.4._.refs_2_, f32[34,16,256]{2,1,0:T(8,128)S(1)} %get-tuple-element.41.r_ref, f32[34,16,256]{2,1,0:T(8,128)S(1)} %get-tuple-element.36.west_ref.refs_6_, f32[34,16,256]{2,1,0:T(8,128)S(1)} %get-tuple-element.37.south_ref.refs_7_, ...), custom_call_target="tpu_custom_call" | custom-call | flops 20000000 | bytes 4000000 | tf_op jit(solution)/shard_map/local/pallas_call | solution.py:507
  129.7 1.2 update.3
  130.9 9.2 %all_to_all.34.in_ref = f32[8,8,128]{2,1,0:T(8,128)S(1)} all-to-all(f32[8,8,128]{2,1,0:T(8,128)S(1)} %get-tuple-element.43), channel_id=1, replica_groups={{0,96,192,288,384,480,576,672},{8,104,200,296,392,488,584,680},{16,112,..., dimensions={0} | all-to-all | bytes 65536 | tf_op jit(solution)/shard_map/all_to_all | solution.py:488
  140.2 11.8 %all_to_all.35.in_ref = f32[12,3,128]{2,1,0:T(4,128)S(1)} all-to-all(f32[12,3,128]{2,1,0:T(4,128)S(1)} %turn.5), channel_id=1, replica_groups={{0,8,16,24,32,40,48,56,64,72,80,88},{96,104,112,120,128,136,144,152,160..., dimensions={0} | all-to-all | bytes 36864 | tf_op jit(solution)/shard_map/all_to_all | solution.py:497
  152.0 1.9 %collective-permute-start.11 = (f32[3,128]{1,0:T(4,128)S(1)}, f32[3,128]{1,0:T(4,128)S(1)}, u32[]{:S(2)}, u32[]{:S(2)}) collective-permute-start(f32[3,128]{1,0:T(4,128)S(1)} %answer.5._.refs_2_), channel_id=1, source_target_pairs={{1,0},{2,1},{3,2},{4,3},{5,4},{6,5},{7,6},{9,8},{10,9},{11,10},{12... | collective-permute-start | bytes 4616 | tf_op jit(solution)/shard_map/ppermute | solution.py:421
  153.9 4.8 %collective-permute-start.10 = (f32[3,128]{1,0:T(4,128)S(1)}, f32[3,128]{1,0:T(4,128)S(1)}, u32[]{:S(2)}, u32[]{:S(2)}) collective-permute-start(f32[3,128]{1,0:T(4,128)S(1)} %answer.5._.refs_2_), channel_id=1, source_target_pairs={{0,1},{1,2},{2,3},{3,4},{4,5},{5,6},{6,7},{8,9},{9,10},{10,11},{11... | collective-permute-start | bytes 4616 | tf_op jit(solution)/shard_map/ppermute | solution.py:421
  158.7 1.7 %local.5.refs_4_ = f32[34,16,256]{2,1,0:T(8,128)S(1)} custom-call(f32[3,128]{1,0:T(4,128)S(1)} %answer.5._.refs_2_, f32[34,16,256]{2,1,0:T(8,128)S(1)} %get-tuple-element.44.r_ref, f32[34,16,256]{2,1,0:T(8,128)S(1)} %get-tuple-element.36.west_ref.refs_6_, f32[34,16,256]{2,1,0:T(8,128)S(1)} %get-tuple-element.37.south_ref.refs_7_, ...), custom_call_target="tpu_custom_call" | custom-call | flops 20000000 | bytes 4000000 | tf_op jit(solution)/shard_map/local/pallas_call | solution.py:507
  160.4 1.4 final.1
  (26 shorter events, 1.3 us)
Async XLA Ops:
  0.6 0.8 copy-start.2
  1.5 0.8 copy-start.3
  2.4 21.4 %collective-permute-start.2 = (f32[2,8,16,128]{3,2,1,0:T(8,128)S(1)}, f32[2,8,16,128]{3,2,1,0:T(8,128)S(1)}, u32[]{:S(2)}, u32[]{:S(2)}) collective-permute-start(f32[2,8,16,128]{3,2,1,0:T(8,128)S(1)} %get-tuple-element.26._.own.refs_11_), channel_id=1, source_target_pairs={{8,0},{16,8},{24,16},{32,24},{40,32},{48,40},{56,48},{64,56},{72,6... | collective-permute-start | bytes 393224 | tf_op jit(solution)/shard_map/ppermute | solution.py:421
  3.7 20.1 %collective-permute-start.1 = (f32[2,8,16,128]{3,2,1,0:T(8,128)S(1)}, f32[2,8,16,128]{3,2,1,0:T(8,128)S(1)}, u32[]{:S(2)}, u32[]{:S(2)}) collective-permute-start(f32[2,8,16,128]{3,2,1,0:T(8,128)S(1)} %get-tuple-element.26._.own.refs_11_), channel_id=1, source_target_pairs={{0,8},{8,16},{16,24},{24,32},{32,40},{40,48},{48,56},{56,64},{64,7... | collective-permute-start | bytes 393224 | tf_op jit(solution)/shard_map/ppermute | solution.py:421
  9.2 7.3 %collective-permute-start = (f32[2,5,16,128]{3,2,1,0:T(8,128)S(1)}, f32[2,5,16,128]{3,2,1,0:T(8,128)S(1)}, u32[]{:S(2)}, u32[]{:S(2)}) collective-permute-start(f32[2,5,16,128]{3,2,1,0:T(8,128)S(1)} %get-tuple-element.30), channel_id=1, source_target_pairs={{0,16},{8,24},{16,32},{24,40},{32,48},{40,56},{48,64},{56,72},{64,... | collective-permute-start | bytes 245768 | tf_op jit(solution)/shard_map/ppermute | solution.py:421
  15.0 8.8 %collective-permute-start.3 = (f32[2,5,16,128]{3,2,1,0:T(8,128)S(1)}, f32[2,5,16,128]{3,2,1,0:T(8,128)S(1)}, u32[]{:S(2)}, u32[]{:S(2)}) collective-permute-start(f32[2,5,16,128]{3,2,1,0:T(8,128)S(1)} %get-tuple-element.31), channel_id=1, source_target_pairs={{16,0},{24,8},{32,16},{40,24},{48,32},{56,40},{64,48},{72,56},{80,... | collective-permute-start | bytes 245768 | tf_op jit(solution)/shard_map/ppermute | solution.py:421
  24.1 12.5 %collective-permute-start.4 = (f32[9,16,128]{2,1,0:T(8,128)S(1)}, f32[9,16,128]{2,1,0:T(8,128)S(1)}, u32[]{:S(2)}, u32[]{:S(2)}) collective-permute-start(f32[9,16,128]{2,1,0:T(8,128)S(1)} %get-tuple-element.32), channel_id=1, source_target_pairs={{0,1},{1,2},{2,3},{3,4},{4,5},{5,6},{6,7},{8,9},{9,10},{10,11},{11... | collective-permute-start | bytes 221192 | tf_op jit(solution)/shard_map/ppermute | solution.py:421
  30.1 6.6 %collective-permute-start.5 = (f32[9,16,128]{2,1,0:T(8,128)S(1)}, f32[9,16,128]{2,1,0:T(8,128)S(1)}, u32[]{:S(2)}, u32[]{:S(2)}) collective-permute-start(f32[9,16,128]{2,1,0:T(8,128)S(1)} %get-tuple-element.33), channel_id=1, source_target_pairs={{1,0},{2,1},{3,2},{4,3},{5,4},{6,5},{7,6},{9,8},{10,9},{11,10},{12... | collective-permute-start | bytes 221192 | tf_op jit(solution)/shard_map/ppermute | solution.py:421
  32.1 1.4 copy-start
  33.5 1.1 copy-start.1
  34.6 0.7 copy-start.4
  35.2 0.7 copy-start.5
  81.8 15.0 %collective-permute-start.7 = (f32[3,128]{1,0:T(4,128)S(1)}, f32[3,128]{1,0:T(4,128)S(1)}, u32[]{:S(2)}, u32[]{:S(2)}) collective-permute-start(f32[3,128]{1,0:T(4,128)S(1)} %answer.3._.refs_2_), channel_id=1, source_target_pairs={{1,0},{2,1},{3,2},{4,3},{5,4},{6,5},{7,6},{9,8},{10,9},{11,10},{12... | collective-permute-start | bytes 4616 | tf_op jit(solution)/shard_map/ppermute | solution.py:421
  83.7 13.1 %collective-permute-start.6 = (f32[3,128]{1,0:T(4,128)S(1)}, f32[3,128]{1,0:T(4,128)S(1)}, u32[]{:S(2)}, u32[]{:S(2)}) collective-permute-start(f32[3,128]{1,0:T(4,128)S(1)} %answer.3._.refs_2_), channel_id=1, source_target_pairs={{0,1},{1,2},{2,3},{3,4},{4,5},{5,6},{6,7},{8,9},{9,10},{10,11},{11... | collective-permute-start | bytes 4616 | tf_op jit(solution)/shard_map/ppermute | solution.py:421
  119.6 10.1 %collective-permute-start.9 = (f32[3,128]{1,0:T(4,128)S(1)}, f32[3,128]{1,0:T(4,128)S(1)}, u32[]{:S(2)}, u32[]{:S(2)}) collective-permute-start(f32[3,128]{1,0:T(4,128)S(1)} %answer.4._.refs_2_), channel_id=1, source_target_pairs={{1,0},{2,1},{3,2},{4,3},{5,4},{6,5},{7,6},{9,8},{10,9},{11,10},{12... | collective-permute-start | bytes 4616 | tf_op jit(solution)/shard_map/ppermute | solution.py:421
  121.5 8.2 %collective-permute-start.8 = (f32[3,128]{1,0:T(4,128)S(1)}, f32[3,128]{1,0:T(4,128)S(1)}, u32[]{:S(2)}, u32[]{:S(2)}) collective-permute-start(f32[3,128]{1,0:T(4,128)S(1)} %answer.4._.refs_2_), channel_id=1, source_target_pairs={{0,1},{1,2},{2,3},{3,4},{4,5},{5,6},{6,7},{8,9},{9,10},{10,11},{11... | collective-permute-start | bytes 4616 | tf_op jit(solution)/shard_map/ppermute | solution.py:421
  152.0 8.4 %collective-permute-start.11 = (f32[3,128]{1,0:T(4,128)S(1)}, f32[3,128]{1,0:T(4,128)S(1)}, u32[]{:S(2)}, u32[]{:S(2)}) collective-permute-start(f32[3,128]{1,0:T(4,128)S(1)} %answer.5._.refs_2_), channel_id=1, source_target_pairs={{1,0},{2,1},{3,2},{4,3},{5,4},{6,5},{7,6},{9,8},{10,9},{11,10},{12... | collective-permute-start | bytes 4616 | tf_op jit(solution)/shard_map/ppermute | solution.py:421
  153.9 6.5 %collective-permute-start.10 = (f32[3,128]{1,0:T(4,128)S(1)}, f32[3,128]{1,0:T(4,128)S(1)}, u32[]{:S(2)}, u32[]{:S(2)}) collective-permute-start(f32[3,128]{1,0:T(4,128)S(1)} %answer.5._.refs_2_), channel_id=1, source_target_pairs={{0,1},{1,2},{2,3},{3,4},{4,5},{5,6},{6,7},{8,9},{9,10},{10,11},{11... | collective-permute-start | bytes 4616 | tf_op jit(solution)/shard_map/ppermute | solution.py:421

commit v3 on v2

--- a/solution.py
+++ b/solution.py
@@ -158,7 +158,7 @@
         copy.start()
     for n, ref in enumerate((scale_ref, slope_ref)):
         for k in range(8):
-            curve_ref[8 * n + k : 8 * n + k + 1, :] = jnp.full((1, LANES), ref[k], jnp.float32)
+            curve_ref[8 * n + k : 8 * n + k + 1, :] = jnp.full((1, CY), ref[k], jnp.float32)
     for copy in copies:
         copy.wait()
 
@@ -180,7 +180,7 @@
     return at
 
 
-def strip_kernel(far_low, low, own, high, far_high, up_ref, down_ref):
+def strip_kernel(_, far_low, low, own, high, far_high, up_ref, down_ref):
     at = pieces((far_low, low, own, high, far_high))
     for pack in range(PACKS):
         up = jnp.zeros((NZ, CY), jnp.float32)
@@ -196,130 +196,182 @@
         down_ref[pack] = down
 
 
+class Beside:
+    def __init__(self, first, second):
+        self.first, self.second = first, second
+
+    def __getitem__(self, row):
+        return jnp.concatenate([self.first[row], self.second[row]], axis=1)
+
+
+def rows_in_pairs(step):
+    def both(pair, _):
+        step(2 * pair)
+        step(2 * pair + 1)
+        return 0
+
+    lax.fori_loop(0, ROWS // 2, both, 0)
+
+
+def diffusivity(conc, label, curve_ref):
+    kind = label.astype(jnp.int32) & 7
+    bits = [(kind & (1 << b)) != 0 for b in range(3)]
+
+    def pick(table):
+        layer = [jnp.broadcast_to(curve_ref[table + k : table + k + 1, :], conc.shape) for k in range(8)]
+        for bit in bits:
+            layer = [jnp.where(bit, layer[2 * n + 1], layer[2 * n]) for n in range(len(layer) // 2)]
+        return layer[0]
+
+    return pick(0) * jnp.exp(pick(8) * conc)
+
+
+def pair_weight(a, b, la, lb):
+    weight = jnp.where(la == lb, 0.5, 0.5 * CONTACT)
+    return jnp.where(jnp.minimum(la, lb) > 0.5, weight * (a + b), 0.0)
+
+
+def tile_faces(row, coeff, label, west, below):
+    a, la = coeff[row], label[row]
+    before = jnp.maximum(row - 1, 0)
+    west[row] = pair_weight(a, coeff[before], la, label[before])
+    not_bottom = lax.broadcasted_iota(jnp.int32, a.shape, 0) > 0
+    below[row] = jnp.where(not_bottom, pair_weight(a, depth_shift(a, 1), la, depth_shift(la, 1)), 0.0)
+
+
+def tile_kernel(curve_ref, far_low, low, own, high, far_high, conc, label, coeff, west, below):
+    at = pieces((far_low, low, own, high, far_high))
+    for row in range(ROWS):
+        conc[row] = at(0, row)
+        label[row] = at(1, row)
+
+    def fill(row):
+        coeff[row] = diffusivity(conc[row], label[row], curve_ref)
+
+    rows_in_pairs(fill)
+    rows_in_pairs(lambda row: tile_faces(row, coeff, label, west, below))
+
+
 def setup_kernel(
-    curve_ref, inv_ref, table_ref, far_low, low, own, high, far_high, left_ref, right_ref,
-    west_out, south_out, below_out, inverse_out, source_out, out_ref,
-    conc, label, coeff, line_ref,
+    curve_ref, inv_ref, table_ref, conc0, label0, coeff0, west0, below0, left_ref, right_ref,
+    west1, below1, south_out, inverse_out, source_out, out_ref,
+    conc1, label1, coeff1, line_ref,
 ):
-    at = pieces((far_low, low, own, high, far_high))
     tile = (NZ, CY)
     m_right, m_right_own = lanes_in(tile, (16, 32)), lanes_in(tile, (0, 3))
     m_left, m_left_own = lanes_in(tile, (96, 112)), lanes_in(tile, (125, 128))
     m_end, m_start = lanes_in(tile, (13, 16)), lanes_in(tile, (112, 115))
     zero = jnp.zeros(tile, jnp.float32)
-    for kind, target in ((0, conc), (1, label)):
-        for row in range(ROWS):
-            index = kind * ROWS + row
-            values = at(kind, row)
-            from_left, from_right = left_ref[index // 8], right_ref[index // 8]
-            slot = (index % 8) * STRIP
-            second = jnp.where(m_right, lane_shift(from_right, 16 - slot), zero)
-            second = jnp.where(m_right_own, lane_shift(from_right, -slot), second)
-            second = jnp.where(m_left, lane_shift(from_left, 96 - slot), second)
-            second = jnp.where(m_left_own, lane_shift(from_left, 112 - slot), second)
-            second = jnp.where(m_end, lane_shift(values, 16), second)
-            second = jnp.where(m_start, lane_shift(values, -16), second)
-            target[row, :, :CY] = values
-            target[row, :, CY:] = second
-
-    def diffusivity(row, _):
-        kind = label[row].astype(jnp.int32) & 7
-        bits = [(kind & (1 << b)) != 0 for b in range(3)]
-
-        def pick(table):
-            layer = [jnp.broadcast_to(curve_ref[table + k : table + k + 1, :], (NZ, LANES)) for k in range(8)]
-            for bit in bits:
-                layer = [jnp.where(bit, layer[2 * n + 1], layer[2 * n]) for n in range(len(layer) // 2)]
-            return layer[0]
-
-        coeff[row] = pick(0) * jnp.exp(pick(8) * conc[row])
-        return 0
-
-    lax.fori_loop(0, ROWS, diffusivity, 0)
-
-    def pair(a, b, la, lb):
-        weight = jnp.where(la == lb, 0.5, 0.5 * CONTACT)
-        return jnp.where((la > 0.5) & (lb > 0.5), weight * (a + b), 0.0)
-
-    not_bottom = lax.broadcasted_iota(jnp.int32, (NZ, LANES), 0) > 0
-    west_out[0] = jnp.zeros((NZ, LANES), jnp.float32)
-
-    def faces(row, _):
+    for pack in range(PACKS):
+        from_left, from_right = left_ref[pack], right_ref[pack]
+        for part in range(8):
+            index = pack * 8 + part
+            if index >= 2 * ROWS:
+                continue
+            kind, row = index // ROWS, index % ROWS
+            first, second = ((conc0, conc1), (label0, label1))[kind]
+            values, slot = first[row], part * STRIP
+            merged = jnp.where(m_right, lane_shift(from_right, 16 - slot), zero)
+            merged = jnp.where(m_right_own, lane_shift(from_right, -slot), merged)
+            merged = jnp.where(m_left, lane_shift(from_left, 96 - slot), merged)
+            merged = jnp.where(m_left_own, lane_shift(from_left, 112 - slot), merged)
+            merged = jnp.where(m_end, lane_shift(values, 16), merged)
+            second[row] = jnp.where(m_start, lane_shift(values, -16), merged)
+
+    def fill(row):
+        coeff1[row] = diffusivity(conc1[row], label1[row], curve_ref)
+
+    rows_in_pairs(fill)
+    coeff, label, conc = Beside(coeff0, coeff1), Beside(label0, label1), Beside(conc0, conc1)
+
+    def faces(row):
+        tile_faces(row, coeff1, label1, west1, below1)
         a, la = coeff[row], label[row]
-
-        @pl.when(row > 0)
-        def _():
-            west_out[row] = pair(a, coeff[row - 1], la, label[row - 1])
-
-        south_out[row] = pair(a, lane_shift(a, 1), la, lane_shift(la, 1))
-        below_out[row] = jnp.where(not_bottom, pair(a, depth_shift(a, 1), la, depth_shift(la, 1)), 0.0)
-        return 0
-
-    lax.fori_loop(0, ROWS, faces, 0)
+        south_out[row] = pair_weight(a, lane_shift(a, 1), la, lane_shift(la, 1))
+
+    rows_in_pairs(faces)
+    west_all, below_all = Beside(west0, west1), Beside(below0, below1)
     box = lanes_in((NZ, LANES), (0, 130), (142, 160), (224, 242), (254, 256))
 
-    def operator(row, _):
+    def operator(row):
         following = jnp.minimum(row + 1, ROWS - 1)
         before = jnp.maximum(row - 1, 0)
-        west, east, south, below, c = west_out[row], west_out[following], south_out[row], below_out[row], conc[row]
+        west, east, south, below = west_all[row], west_all[following], south_out[row], below_all[row]
+        c = conc[row]
         diagonal = INVERSE_STEP + west + east + south + lane_shift(south, -1) + below + depth_shift(below, -1)
         inverse_out[row] = jnp.where(box, 1.0 / diagonal, 0.0)
-        flux = west * (c - conc[before]) - east * (conc[following] - c) + side_flux(c, south, below)
-        source_out[row] = -flux
-        return 0
-
-    lax.fori_loop(0, ROWS, operator, 0)
+        flux = east * (conc[following] - c) - west * (c - conc[before])
+        source_out[row] = flux - side_flux(c, south, below)
+
+    rows_in_pairs(operator)
     spread_moments(lambda x: source_out[HALO + x, :, :CY], table_ref, inv_ref, line_ref, out_ref)
 
 
-def local_kernel(_, r_ref, west_ref, south_ref, below_ref, inverse_ref, out_ref, u_ref, q_ref, x_ref, *, wide):
+def local_kernel(
+    _, r_ref, west0, west1, south_ref, below0, below1, inverse_ref, out_ref, u_ref, q_ref, x_ref, *, wide
+):
+    west_ref, below_ref = Beside(west0, west1), Beside(below0, below1)
     scaled, steps = chebyshev()
     plus = lanes_in((NZ, LANES), (253, 256), (141, 144))
     minus = lanes_in((NZ, LANES), (128, 131), (240, 243))
-    for block in range(-2, 3):
-        low, high = max(-wide, 8 * block), min(CX - 1 + wide, 8 * block + 7)
-        if low > high:
-            continue
-        box_low, box_high = max(8 * block - OV, -HALO), min(8 * block + 7 + OV, CX - 1 + HALO)
-
+
+    def solve(base, low, high, box_low, box_high, limit):
         def start(row):
             if not box_low <= row <= box_high:
                 return None
-            return scaled * inverse_ref[row + HALO] * r_ref[row + HALO]
+            return scaled * inverse_ref[base + row] * r_ref[base + row]
+
+        def held(row):
+            if not box_low <= row <= box_high:
+                return None
+            return u_ref[row - box_low]
 
         for number, (keep, gain) in enumerate(steps):
             more = len(steps) - 1 - number
             first, last = max(low - more, box_low), min(high + more, box_high)
-
-            def held(row):
-                if not box_low <= row <= box_high:
-                    return None
-                return u_ref[row - box_low]
-
             fetch = start if number == 0 else held
             now, before = fetch(first), fetch(first - 1)
-            flow = west_ref[first + HALO] * (now if before is None else now - before)
+            flow = west_ref[base + first] * (now if before is None else now - before)
             for row in range(first, last + 1):
                 following = fetch(row + 1)
-                if row + 1 + HALO < ROWS:
-                    gate = west_ref[row + 1 + HALO]
+                if row + 1 < limit:
+                    gate = west_ref[base + row + 1]
                     onward = gate * (-now if following is None else following - now)
                 else:
                     onward = jnp.zeros_like(now)
                 place = row - box_low
                 applied = INVERSE_STEP * now + (flow - onward)
-                applied = applied + side_flux(now, south_ref[row + HALO], below_ref[row + HALO])
-                remain = (r_ref[row + HALO] if number == 0 else q_ref[place]) - applied
-                step = keep * now + gain * (inverse_ref[row + HALO] * remain)
-                result = (now if number == 0 else x_ref[place]) + step
+                applied = applied + side_flux(now, south_ref[base + row], below_ref[base + row])
+                remain = (r_ref[base + row] if number == 0 else q_ref[place]) - applied
+                step = keep * now + gain * (inverse_ref[base + row] * remain)
                 if more:
                     u_ref[place] = step
                     q_ref[place] = remain
-                    x_ref[place] = result
-                else:
-                    merged = jnp.where(plus, lane_shift(result, 16), result)
-                    out_ref[row + HALO] = jnp.where(minus, lane_shift(result, -16), merged)
+                if low <= row <= high:
+                    result = (now if number == 0 else x_ref[place]) + step
+                    if more:
+                        x_ref[place] = result
+                    else:
+                        merged = jnp.where(plus, lane_shift(result, 16), result)
+                        out_ref[base + row] = jnp.where(minus, lane_shift(result, -16), merged)
                 now, flow = following, onward
+
+    whole = [block for block in range(-2, 3) if -wide <= 8 * block and 8 * block + 7 <= CX - 1 + wide]
+    for block in range(-2, 3):
+        low, high = max(-wide, 8 * block), min(CX - 1 + wide, 8 * block + 7)
+        if low > high or (block in whole and len(whole) > 1):
+            continue
+        base = HALO + 8 * block
+        box_low, box_high = max(8 * block - OV, -HALO), min(8 * block + 7 + OV, CX - 1 + HALO)
+        at = lambda row: row - 8 * block
+        solve(base, at(low), at(high), at(box_low), at(box_high), ROWS - base)
+    if len(whole) > 1:
+
+        def body(number, _):
+            solve(HALO + 8 * (number + whole[0]), 0, CX - 1, -OV, CX - 1 + OV, CX + OV + 1)
+            return 0
+
+        lax.fori_loop(0, len(whole), body, 0)
 
 
 def turn_kernel(in_ref, out_ref):
@@ -362,7 +414,8 @@
     refs = list(refs)
     take = lambda count: [refs.pop(0) for _ in range(count)]
     odd_ref, left_ref, own_ref, right_ref = take(4)
-    x_ref, source_ref, west_ref, south_ref, below_ref = take(5)
+    x_ref, source_ref, west0, west1, south_ref, below0, below1 = take(7)
+    west_ref, below_ref = Beside(west0, west1), Beside(below0, below1)
     (table_ref,) = take(1)
     (old_ref,) = take(0 if first else 1) or (None,)
     if reach:
@@ -455,7 +508,7 @@
     far_low, far_high = moved(tail, "gx", 2), moved(head, "gx", -2)
     curve, inverse_rows, table = pl.pallas_call(
         stage_kernel,
-        out_shape=[shaped(16, LANES), shaped(NB, NB * size), shaped(WAVE + NZ, CY)],
+        out_shape=[shaped(16, CY), shaped(NB, NB * size), shaped(WAVE + NZ, CY)],
         in_specs=[anywhere, smem, smem, hbm, hbm],
         out_specs=vmem(3),
         scratch_shapes=[pltpu.SemaphoreType.DMA((2,))],
@@ -467,21 +520,33 @@
     up, down = pl.pallas_call(
         strip_kernel,
         out_shape=[shaped(PACKS, NZ, CY)] * 2,
-        in_specs=vmem(5),
+        in_specs=[anywhere] + vmem(5),
         out_specs=vmem(2),
         compiler_params=room(4),
         name="strips",
-    )(*parts)
+    )(curve, *parts)
     left, right = moved(up, "gy", 1), moved(down, "gy", -1)
-    west, south, below, inverse, source, partial = pl.pallas_call(
+    half_frame = shaped(ROWS, NZ, CY)
+    tiled = pl.pallas_call(
+        tile_kernel,
+        out_shape=[half_frame] * 5,
+        in_specs=vmem(6),
+        out_specs=vmem(5),
+        compiler_params=room(4),
+        cost_estimate=cost(10_000_000),
+        name="tile",
+    )(curve, *parts)
+    west0, below0 = tiled[3:]
+    west1, below1, south, inverse, source, partial = pl.pallas_call(
         setup_kernel,
-        out_shape=[frame] * 5 + [shaped(n_y, WINDOW, CY)],
+        out_shape=[half_frame] * 2 + [frame] * 3 + [shaped(n_y, WINDOW, CY)],
         in_specs=vmem(10),
         out_specs=vmem(6),
-        scratch_shapes=[scratch(ROWS, NZ, LANES)] * 3 + [line_scratch],
+        scratch_shapes=[scratch(ROWS, NZ, CY)] * 3 + [line_scratch],
         compiler_params=room(8),
         name="setup",
-    )(curve, inverse_rows, table, *parts, left, right)
+    )(curve, inverse_rows, table, *tiled, left, right)
+    faces = (west0, west1, south, below0, below1)
 
     residual, update = source, None
     for sweep, reach in enumerate(REACH):
@@ -507,14 +572,14 @@
         local = pl.pallas_call(
             functools.partial(local_kernel, wide=reach + 1),
             out_shape=frame,
-            in_specs=[anywhere] + vmem(5),
+            in_specs=[anywhere] + vmem(7),
             out_specs=vmem(1)[0],
             scratch_shapes=[scratch(CX + 2 * OV, NZ, LANES)] * 3,
             compiler_params=room(8),
             cost_estimate=cost(20_000_000),
             name="local",
-        )(answer, residual, west, south, below, inverse)
-        operands = [odd, *answers, local, source, west, south, below, table]
+        )(answer, residual, *faces, inverse)
+        operands = [odd, *answers, local, source, *faces, table]
         operands += [] if sweep == 0 else [update]
         kernel = functools.partial(update_kernel, reach=reach, first=sweep == 0)
         if reach:

time: 163 us -> 151 us (0.926)
  Pallas kernels: 27.5 us -> 19.8 us
  starting transfers between devices: 43.4 us -> 41.3 us
  waiting for transfers between devices: 7.57 us -> 5.93 us
    pallas_call x3, Pallas kernels: 11.8 us -> 7.97 us  [on_device(): pl.pallas_call(functools.partial(local_kernel, wide=reach + 1), out_shape...]
    pallas_call x2 -> x3, Pallas kernels: 11 us -> 7.15 us  [the longest x1 5.6 us: on_device(): pl.pallas_call(setup_kernel, out_shape=[half_frame] * 2 + [frame] * 3 + [...]
    ppermute x12, starting transfers between devices: 43.4 us -> 41.3 us  [moved(): return lax.ppermute(array, axis, pairs)]
    all_to_all x3, blocking collectives: 38.5 us -> 40.2 us  [on_device(): lax.all_to_all(partial, 'gx', 0, 0, tiled=True, axis_index_groups=along_y)]
    all_to_all x3, blocking collectives: 38.5 us -> 36.7 us  [on_device(): lax.all_to_all(turned, 'gx', 0, 0, tiled=True, axis_index_groups=along_z)]
    ppermute x12, waiting for transfers between devices: 7.57 us -> 5.93 us  [moved(): return lax.ppermute(array, axis, pairs)]
  transfers between devices with their start and end apart: 12 -> 12, of which waited for: 2 -> 2; matrix products, arithmetic and copies ran while one was open for 0% -> 0% of each run, Pallas kernels for 8% -> 6%
where the time goes in v3:
time: 151 us; the launch traced here: 150 us
  blocking collectives  77 us (51%)
  starting transfers between devices  41.3 us (27%)
  Pallas kernels  19.8 us (13%)
  waiting for transfers between devices  5.93 us (4%)
  local copies, waits for them, and re-layouts  5.45 us (4%)
    ppermute x12, starting transfers between devices, moved(): return lax.ppermute(array, axis, pairs)  41.3 us
    all_to_all x3, blocking collectives, on_device(): lax.all_to_all(partial, 'gx', 0, 0, tiled=True, axis_index_groups=along_y)  40.2 us
    all_to_all x3, blocking collectives, on_device(): lax.all_to_all(turned, 'gx', 0, 0, tiled=True, axis_index_groups=along_z)  36.7 us
    pallas_call x3, Pallas kernels, on_device(): pl.pallas_call(functools.partial(local_kernel, wide=reach + 1), out_shape...  7.97 us
    ppermute x12, waiting for transfers between devices, moved(): return lax.ppermute(array, axis, pairs)  5.93 us
    pallas_call x1, Pallas kernels, on_device(): pl.pallas_call(setup_kernel, out_shape=[half_frame] * 2 + [frame] * 3 + [...  5.6 us
    unnamed x12, local copies, waits for them, and re-layouts  5.45 us
  transfers between devices with their start and end apart: 12, of which 2 were waited for; matrix products, arithmetic and copies ran while one was open for 0% of the time, Pallas kernels for 6%

profile of v3, /device:TPU:1, one launch (start us, length us, event | category | flops | bytes accessed | tf_op | source)
XLA Modules:
  0.0 150.4 jit_solution(4768148426423525158)
XLA Ops:
  0.6 0.8 copy-done.2
  1.5 0.8 copy-done.3
  2.4 1.3 collective-permute-start.2
  3.7 5.5 %collective-permute-start.1 = (f32[2,8,16,128]{3,2,1,0:T(8,128)S(1)}, f32[2,8,16,128]{3,2,1,0:T(8,128)S(1)}, u32[]{:S(2)}, u32[]{:S(2)}) collective-permute-start(f32[2,8,16,128]{3,2,1,0:T(8,128)S(1)} %get-tuple-element.31._.own.refs_13_), channel_id=1, source_target_pairs={{0,8},{8,16},{16,24},{24,32},{32,40},{40,48},{48,56},{56,64},{64,7... | collective-permute-start | bytes 393224 | tf_op jit(solution)/shard_map/ppermute | solution.py:474
  9.2 5.8 %collective-permute-start = (f32[2,5,16,128]{3,2,1,0:T(8,128)S(1)}, f32[2,5,16,128]{3,2,1,0:T(8,128)S(1)}, u32[]{:S(2)}, u32[]{:S(2)}) collective-permute-start(f32[2,5,16,128]{3,2,1,0:T(8,128)S(1)} %get-tuple-element.35), channel_id=1, source_target_pairs={{0,16},{8,24},{16,32},{24,40},{32,48},{40,56},{48,64},{56,72},{64,... | collective-permute-start | bytes 245768 | tf_op jit(solution)/shard_map/ppermute | solution.py:474
  15.0 1.3 collective-permute-start.3
  16.3 1.4 copy-done
  17.7 1.1 copy-done.1
  20.1 0.8 stage.1
  20.9 2.9 %collective-permute-done.3.far_high = f32[2,5,16,128]{3,2,1,0:T(8,128)S(1)} collective-permute-done((f32[2,5,16,128]{3,2,1,0:T(8,128)S(1)}, f32[2,5,16,128]{3,2,1,0:T(8,128)S(1)}, u32[]{:S(2)}, u32[]{:S(2)}) %collective-permute-start.3) | collective-permute-done | bytes 81952 | tf_op jit(solution)/shard_map/ppermute | solution.py:474
  24.1 6.0 %collective-permute-start.4 = (f32[9,16,128]{2,1,0:T(8,128)S(1)}, f32[9,16,128]{2,1,0:T(8,128)S(1)}, u32[]{:S(2)}, u32[]{:S(2)}) collective-permute-start(f32[9,16,128]{2,1,0:T(8,128)S(1)} %get-tuple-element.42), channel_id=1, source_target_pairs={{0,1},{1,2},{2,3},{3,4},{4,5},{5,6},{6,7},{8,9},{9,10},{10,11},{11... | collective-permute-start | bytes 221192 | tf_op jit(solution)/shard_map/ppermute | solution.py:474
  30.1 1.9 %collective-permute-start.5 = (f32[9,16,128]{2,1,0:T(8,128)S(1)}, f32[9,16,128]{2,1,0:T(8,128)S(1)}, u32[]{:S(2)}, u32[]{:S(2)}) collective-permute-start(f32[9,16,128]{2,1,0:T(8,128)S(1)} %get-tuple-element.43), channel_id=1, source_target_pairs={{1,0},{2,1},{3,2},{4,3},{5,4},{6,5},{7,6},{9,8},{10,9},{11,10},{12... | collective-permute-start | bytes 221192 | tf_op jit(solution)/shard_map/ppermute | solution.py:474
  32.8 3.0 %collective-permute-done.5.right_ref = f32[9,16,128]{2,1,0:T(8,128)S(1)} collective-permute-done((f32[9,16,128]{2,1,0:T(8,128)S(1)}, f32[9,16,128]{2,1,0:T(8,128)S(1)}, u32[]{:S(2)}, u32[]{:S(2)}) %collective-permute-start.5) | collective-permute-done | bytes 73760 | tf_op jit(solution)/shard_map/ppermute | solution.py:474
  35.8 5.6 %setup.1 = (f32[34,16,128]{2,1,0:T(8,128)S(1)}, f32[34,16,128]{2,1,0:T(8,128)S(1)}, f32[34,16,256]{2,1,0:T(8,128)S(1)}, f32[34,16,256]{2,1,0:T(8,128)S(1)}, f32[...) custom-call(f32[16,128]{1,0:T(8,128)S(1)} %get-tuple-element.32.curve_ref._, ...), custom_call_target="tpu_custom_call" | custom-call | tf_op jit(solution)/shard_map/setup/pallas_call | solution.py:540
  41.4 21.7 %all_to_all.30.in_ref = f32[8,8,128]{2,1,0:T(8,128)S(1)} all-to-all(f32[8,8,128]{2,1,0:T(8,128)S(1)} %get-tuple-element.44), channel_id=1, replica_groups={{0,96,192,288,384,480,576,672},{8,104,200,296,392,488,584,680},{16,112,..., dimensions={0} | all-to-all | bytes 65536 | tf_op jit(solution)/shard_map/all_to_all | solution.py:553
  63.2 13.0 %all_to_all.31.in_ref = f32[12,3,128]{2,1,0:T(4,128)S(1)} all-to-all(f32[12,3,128]{2,1,0:T(4,128)S(1)} %turn.3), channel_id=1, replica_groups={{0,8,16,24,32,40,48,56,64,72,80,88},{96,104,112,120,128,136,144,152,160..., dimensions={0} | all-to-all | bytes 36864 | tf_op jit(solution)/shard_map/all_to_all | solution.py:562
  76.2 2.2 %collective-permute-start.7 = (f32[3,128]{1,0:T(4,128)S(1)}, f32[3,128]{1,0:T(4,128)S(1)}, u32[]{:S(2)}, u32[]{:S(2)}) collective-permute-start(f32[3,128]{1,0:T(4,128)S(1)} %answer.3._.refs_2_), channel_id=1, source_target_pairs={{1,0},{2,1},{3,2},{4,3},{5,4},{6,5},{7,6},{9,8},{10,9},{11,10},{12... | collective-permute-start | bytes 4616 | tf_op jit(solution)/shard_map/ppermute | solution.py:474
  78.4 4.3 %collective-permute-start.6 = (f32[3,128]{1,0:T(4,128)S(1)}, f32[3,128]{1,0:T(4,128)S(1)}, u32[]{:S(2)}, u32[]{:S(2)}) collective-permute-start(f32[3,128]{1,0:T(4,128)S(1)} %answer.3._.refs_2_), channel_id=1, source_target_pairs={{0,1},{1,2},{2,3},{3,4},{4,5},{5,6},{6,7},{8,9},{9,10},{10,11},{11... | collective-permute-start | bytes 4616 | tf_op jit(solution)/shard_map/ppermute | solution.py:474
  82.7 2.9 %local.3.refs_4_ = f32[34,16,256]{2,1,0:T(8,128)S(1)} custom-call(f32[3,128]{1,0:T(4,128)S(1)} %answer.3._.refs_2_, f32[34,16,256]{2,1,0:T(8,128)S(1)} %get-tuple-element.45.r_ref.refs_5_, f32[34,16,128]{2,1,0:T(8,128)S(1)} %get-tuple-element.40.west0.refs_6_, f32[34,16,128]{2,1,0:T(8,128)S(1)} %get-tuple-element.46.west1.refs_7_, ...), custom_call_target="tpu_custom_call" | custom-call | flops 20000000 | bytes 4000000 | tf_op jit(solution)/shard_map/local/pallas_call | solution.py:572
  85.6 1.7 %update.2 = (f32[34,16,256]{2,1,0:T(8,128)S(1)}, f32[34,16,256]{2,1,0:T(8,128)S(1)}, f32[8,8,128]{2,1,0:T(8,128)S(1)}) custom-call(s32[1]{0:T(128)} %bitcast.refs_0_, f32[3,128]{1,0:T(4,128)S(1)} %collective-permute-done.6.refs_1_, f32[3,128]{1,0:T(4,128)S(1)} %answer.3._.refs_2_, f32[3,128]{1,0:T(4,128)S(1)} %collective-permute-done.7.refs_3_, ...), custom_call_target="tpu_custom_call" | custom-call | tf_op jit(solution)/shard_map/update/pallas_call | solution.py:587
  87.3 9.2 %all_to_all.32.in_ref = f32[8,8,128]{2,1,0:T(8,128)S(1)} all-to-all(f32[8,8,128]{2,1,0:T(8,128)S(1)} %get-tuple-element.50), channel_id=1, replica_groups={{0,96,192,288,384,480,576,672},{8,104,200,296,392,488,584,680},{16,112,..., dimensions={0} | all-to-all | bytes 65536 | tf_op jit(solution)/shard_map/all_to_all | solution.py:553
  96.6 11.9 %all_to_all.33.in_ref = f32[12,3,128]{2,1,0:T(4,128)S(1)} all-to-all(f32[12,3,128]{2,1,0:T(4,128)S(1)} %turn.4), channel_id=1, replica_groups={{0,8,16,24,32,40,48,56,64,72,80,88},{96,104,112,120,128,136,144,152,160..., dimensions={0} | all-to-all | bytes 36864 | tf_op jit(solution)/shard_map/all_to_all | solution.py:562
  108.5 2.2 %collective-permute-start.9 = (f32[3,128]{1,0:T(4,128)S(1)}, f32[3,128]{1,0:T(4,128)S(1)}, u32[]{:S(2)}, u32[]{:S(2)}) collective-permute-start(f32[3,128]{1,0:T(4,128)S(1)} %answer.4._.refs_2_), channel_id=1, source_target_pairs={{1,0},{2,1},{3,2},{4,3},{5,4},{6,5},{7,6},{9,8},{10,9},{11,10},{12... | collective-permute-start | bytes 4616 | tf_op jit(solution)/shard_map/ppermute | solution.py:474
  110.7 4.3 %collective-permute-start.8 = (f32[3,128]{1,0:T(4,128)S(1)}, f32[3,128]{1,0:T(4,128)S(1)}, u32[]{:S(2)}, u32[]{:S(2)}) collective-permute-start(f32[3,128]{1,0:T(4,128)S(1)} %answer.4._.refs_2_), channel_id=1, source_target_pairs={{0,1},{1,2},{2,3},{3,4},{4,5},{5,6},{6,7},{8,9},{9,10},{10,11},{11... | collective-permute-start | bytes 4616 | tf_op jit(solution)/shard_map/ppermute | solution.py:474
  115.0 3.4 %local.4.refs_4_ = f32[34,16,256]{2,1,0:T(8,128)S(1)} custom-call(f32[3,128]{1,0:T(4,128)S(1)} %answer.4._.refs_2_, f32[34,16,256]{2,1,0:T(8,128)S(1)} %get-tuple-element.51.r_ref, f32[34,16,128]{2,1,0:T(8,128)S(1)} %get-tuple-element.40.west0.refs_6_, f32[34,16,128]{2,1,0:T(8,128)S(1)} %get-tuple-element.46.west1.refs_7_, ...), custom_call_target="tpu_custom_call" | custom-call | flops 20000000 | bytes 4000000 | tf_op jit(solution)/shard_map/local/pallas_call | solution.py:572
  118.5 1.2 update.3
  119.6 9.2 %all_to_all.34.in_ref = f32[8,8,128]{2,1,0:T(8,128)S(1)} all-to-all(f32[8,8,128]{2,1,0:T(8,128)S(1)} %get-tuple-element.53), channel_id=1, replica_groups={{0,96,192,288,384,480,576,672},{8,104,200,296,392,488,584,680},{16,112,..., dimensions={0} | all-to-all | bytes 65536 | tf_op jit(solution)/shard_map/all_to_all | solution.py:553
  128.9 11.9 %all_to_all.35.in_ref = f32[12,3,128]{2,1,0:T(4,128)S(1)} all-to-all(f32[12,3,128]{2,1,0:T(4,128)S(1)} %turn.5), channel_id=1, replica_groups={{0,8,16,24,32,40,48,56,64,72,80,88},{96,104,112,120,128,136,144,152,160..., dimensions={0} | all-to-all | bytes 36864 | tf_op jit(solution)/shard_map/all_to_all | solution.py:562
  140.8 2.2 %collective-permute-start.11 = (f32[3,128]{1,0:T(4,128)S(1)}, f32[3,128]{1,0:T(4,128)S(1)}, u32[]{:S(2)}, u32[]{:S(2)}) collective-permute-start(f32[3,128]{1,0:T(4,128)S(1)} %answer.5._.refs_2_), channel_id=1, source_target_pairs={{1,0},{2,1},{3,2},{4,3},{5,4},{6,5},{7,6},{9,8},{10,9},{11,10},{12... | collective-permute-start | bytes 4616 | tf_op jit(solution)/shard_map/ppermute | solution.py:474
  143.0 4.3 %collective-permute-start.10 = (f32[3,128]{1,0:T(4,128)S(1)}, f32[3,128]{1,0:T(4,128)S(1)}, u32[]{:S(2)}, u32[]{:S(2)}) collective-permute-start(f32[3,128]{1,0:T(4,128)S(1)} %answer.5._.refs_2_), channel_id=1, source_target_pairs={{0,1},{1,2},{2,3},{3,4},{4,5},{5,6},{6,7},{8,9},{9,10},{10,11},{11... | collective-permute-start | bytes 4616 | tf_op jit(solution)/shard_map/ppermute | solution.py:474
  147.3 1.7 %local.5.refs_4_ = f32[34,16,256]{2,1,0:T(8,128)S(1)} custom-call(f32[3,128]{1,0:T(4,128)S(1)} %answer.5._.refs_2_, f32[34,16,256]{2,1,0:T(8,128)S(1)} %get-tuple-element.54.r_ref, f32[34,16,128]{2,1,0:T(8,128)S(1)} %get-tuple-element.40.west0.refs_6_, f32[34,16,128]{2,1,0:T(8,128)S(1)} %get-tuple-element.46.west1.refs_7_, ...), custom_call_target="tpu_custom_call" | custom-call | flops 20000000 | bytes 4000000 | tf_op jit(solution)/shard_map/local/pallas_call | solution.py:572
  149.0 1.4 final.1
  (27 shorter events, 2.5 us)
Async XLA Ops:
  0.6 0.8 copy-start.2
  1.5 0.8 copy-start.3
  2.4 21.4 %collective-permute-start.2 = (f32[2,8,16,128]{3,2,1,0:T(8,128)S(1)}, f32[2,8,16,128]{3,2,1,0:T(8,128)S(1)}, u32[]{:S(2)}, u32[]{:S(2)}) collective-permute-start(f32[2,8,16,128]{3,2,1,0:T(8,128)S(1)} %get-tuple-element.31._.own.refs_13_), channel_id=1, source_target_pairs={{8,0},{16,8},{24,16},{32,24},{40,32},{48,40},{56,48},{64,56},{72,6... | collective-permute-start | bytes 393224 | tf_op jit(solution)/shard_map/ppermute | solution.py:474
  3.7 20.1 %collective-permute-start.1 = (f32[2,8,16,128]{3,2,1,0:T(8,128)S(1)}, f32[2,8,16,128]{3,2,1,0:T(8,128)S(1)}, u32[]{:S(2)}, u32[]{:S(2)}) collective-permute-start(f32[2,8,16,128]{3,2,1,0:T(8,128)S(1)} %get-tuple-element.31._.own.refs_13_), channel_id=1, source_target_pairs={{0,8},{8,16},{16,24},{24,32},{32,40},{40,48},{48,56},{56,64},{64,7... | collective-permute-start | bytes 393224 | tf_op jit(solution)/shard_map/ppermute | solution.py:474
  9.2 11.7 %collective-permute-start = (f32[2,5,16,128]{3,2,1,0:T(8,128)S(1)}, f32[2,5,16,128]{3,2,1,0:T(8,128)S(1)}, u32[]{:S(2)}, u32[]{:S(2)}) collective-permute-start(f32[2,5,16,128]{3,2,1,0:T(8,128)S(1)} %get-tuple-element.35), channel_id=1, source_target_pairs={{0,16},{8,24},{16,32},{24,40},{32,48},{40,56},{48,64},{56,72},{64,... | collective-permute-start | bytes 245768 | tf_op jit(solution)/shard_map/ppermute | solution.py:474
  15.0 8.8 %collective-permute-start.3 = (f32[2,5,16,128]{3,2,1,0:T(8,128)S(1)}, f32[2,5,16,128]{3,2,1,0:T(8,128)S(1)}, u32[]{:S(2)}, u32[]{:S(2)}) collective-permute-start(f32[2,5,16,128]{3,2,1,0:T(8,128)S(1)} %get-tuple-element.36), channel_id=1, source_target_pairs={{16,0},{24,8},{32,16},{40,24},{48,32},{56,40},{64,48},{72,56},{80,... | collective-permute-start | bytes 245768 | tf_op jit(solution)/shard_map/ppermute | solution.py:474
  16.3 1.4 copy-start
  17.7 1.1 copy-start.1
  18.8 0.7 copy-start.4
  19.4 0.7 copy-start.5
  24.1 8.7 %collective-permute-start.4 = (f32[9,16,128]{2,1,0:T(8,128)S(1)}, f32[9,16,128]{2,1,0:T(8,128)S(1)}, u32[]{:S(2)}, u32[]{:S(2)}) collective-permute-start(f32[9,16,128]{2,1,0:T(8,128)S(1)} %get-tuple-element.42), channel_id=1, source_target_pairs={{0,1},{1,2},{2,3},{3,4},{4,5},{5,6},{6,7},{8,9},{9,10},{10,11},{11... | collective-permute-start | bytes 221192 | tf_op jit(solution)/shard_map/ppermute | solution.py:474
  30.1 5.7 %collective-permute-start.5 = (f32[9,16,128]{2,1,0:T(8,128)S(1)}, f32[9,16,128]{2,1,0:T(8,128)S(1)}, u32[]{:S(2)}, u32[]{:S(2)}) collective-permute-start(f32[9,16,128]{2,1,0:T(8,128)S(1)} %get-tuple-element.43), channel_id=1, source_target_pairs={{1,0},{2,1},{3,2},{4,3},{5,4},{6,5},{7,6},{9,8},{10,9},{11,10},{12... | collective-permute-start | bytes 221192 | tf_op jit(solution)/shard_map/ppermute | solution.py:474
  76.2 9.4 %collective-permute-start.7 = (f32[3,128]{1,0:T(4,128)S(1)}, f32[3,128]{1,0:T(4,128)S(1)}, u32[]{:S(2)}, u32[]{:S(2)}) collective-permute-start(f32[3,128]{1,0:T(4,128)S(1)} %answer.3._.refs_2_), channel_id=1, source_target_pairs={{1,0},{2,1},{3,2},{4,3},{5,4},{6,5},{7,6},{9,8},{10,9},{11,10},{12... | collective-permute-start | bytes 4616 | tf_op jit(solution)/shard_map/ppermute | solution.py:474
  78.4 7.2 %collective-permute-start.6 = (f32[3,128]{1,0:T(4,128)S(1)}, f32[3,128]{1,0:T(4,128)S(1)}, u32[]{:S(2)}, u32[]{:S(2)}) collective-permute-start(f32[3,128]{1,0:T(4,128)S(1)} %answer.3._.refs_2_), channel_id=1, source_target_pairs={{0,1},{1,2},{2,3},{3,4},{4,5},{5,6},{6,7},{8,9},{9,10},{10,11},{11... | collective-permute-start | bytes 4616 | tf_op jit(solution)/shard_map/ppermute | solution.py:474
  108.5 10.0 %collective-permute-start.9 = (f32[3,128]{1,0:T(4,128)S(1)}, f32[3,128]{1,0:T(4,128)S(1)}, u32[]{:S(2)}, u32[]{:S(2)}) collective-permute-start(f32[3,128]{1,0:T(4,128)S(1)} %answer.4._.refs_2_), channel_id=1, source_target_pairs={{1,0},{2,1},{3,2},{4,3},{5,4},{6,5},{7,6},{9,8},{10,9},{11,10},{12... | collective-permute-start | bytes 4616 | tf_op jit(solution)/shard_map/ppermute | solution.py:474
  110.7 7.8 %collective-permute-start.8 = (f32[3,128]{1,0:T(4,128)S(1)}, f32[3,128]{1,0:T(4,128)S(1)}, u32[]{:S(2)}, u32[]{:S(2)}) collective-permute-start(f32[3,128]{1,0:T(4,128)S(1)} %answer.4._.refs_2_), channel_id=1, source_target_pairs={{0,1},{1,2},{2,3},{3,4},{4,5},{5,6},{6,7},{8,9},{9,10},{10,11},{11... | collective-permute-start | bytes 4616 | tf_op jit(solution)/shard_map/ppermute | solution.py:474
  140.8 8.2 %collective-permute-start.11 = (f32[3,128]{1,0:T(4,128)S(1)}, f32[3,128]{1,0:T(4,128)S(1)}, u32[]{:S(2)}, u32[]{:S(2)}) collective-permute-start(f32[3,128]{1,0:T(4,128)S(1)} %answer.5._.refs_2_), channel_id=1, source_target_pairs={{1,0},{2,1},{3,2},{4,3},{5,4},{6,5},{7,6},{9,8},{10,9},{11,10},{12... | collective-permute-start | bytes 4616 | tf_op jit(solution)/shard_map/ppermute | solution.py:474
  143.0 6.0 %collective-permute-start.10 = (f32[3,128]{1,0:T(4,128)S(1)}, f32[3,128]{1,0:T(4,128)S(1)}, u32[]{:S(2)}, u32[]{:S(2)}) collective-permute-start(f32[3,128]{1,0:T(4,128)S(1)} %answer.5._.refs_2_), channel_id=1, source_target_pairs={{0,1},{1,2},{2,3},{3,4},{4,5},{5,6},{6,7},{8,9},{9,10},{10,11},{11... | collective-permute-start | bytes 4616 | tf_op jit(solution)/shard_map/ppermute | solution.py:474

commit v4 on v3

--- a/solution.py
+++ b/solution.py
@@ -139,14 +139,16 @@
                 out_ref[group, place : place + 1, :] = total
 
 
-def own_kernel(conc_ref, label_ref, out_ref, tail_ref, head_ref):
+def own_kernel(place_ref, conc_ref, label_ref, out_ref, one_ref, two_ref):
+    upper = bit(place_ref, 4)
     for x in range(CX):
         for kind, values in enumerate((conc_ref[:, x, :], label_ref[:, x, :].astype(jnp.float32))):
             out_ref[kind, x] = values
-            if x >= CX - FAR:
-                tail_ref[kind, x - (CX - FAR)] = values
-            if x < FAR:
-                head_ref[kind, x] = values
+    for kind in range(2):
+        for row in range(FAR):
+            head, tail = out_ref[kind, row], out_ref[kind, CX - FAR + row]
+            one_ref[kind, row] = jnp.where(upper, head, tail)
+            two_ref[kind, row] = jnp.where(upper, tail, head)
 
 
 def stage_kernel(_, scale_ref, slope_ref, inv_hbm, table_hbm, curve_ref, inv_ref, table_ref, sems):
@@ -163,25 +165,33 @@
         copy.wait()
 
 
-def pieces(refs):
-    far_low, low, own, high, far_high = refs
+def bit(place_ref, which):
+    return ((place_ref[0] >> which) & 1) == 1
+
+
+def pieces(place_ref, refs):
+    near_one, near_two, far_one, far_two, own = refs
+    odd, upper = bit(place_ref, 3), bit(place_ref, 4)
 
     def at(kind, row):
-        if row < FAR:
-            return far_low[kind, row]
-        if row < HALO:
-            return low[kind, row - FAR]
-        if row < HALO + CX:
+        if HALO <= row < HALO + CX:
             return own[kind, row - HALO]
-        if row < HALO + 2 * CX:
-            return high[kind, row - HALO - CX]
-        return far_high[kind, row - HALO - 2 * CX]
+        below = row < HALO
+        if FAR <= row < HALO + 2 * CX:
+            place = row - FAR if below else row - HALO - CX
+            flag, one, two = odd, near_one, near_two
+        else:
+            place = row if below else row - HALO - 2 * CX
+            flag, one, two = upper, far_one, far_two
+        first, second = one[kind, place], two[kind, place]
+        return jnp.where(flag, first, second) if below else jnp.where(flag, second, first)
 
     return at
 
 
-def strip_kernel(_, far_low, low, own, high, far_high, up_ref, down_ref):
-    at = pieces((far_low, low, own, high, far_high))
+def strip_kernel(place_ref, _, near_one, near_two, far_one, far_two, own, one_ref, two_ref):
+    at = pieces(place_ref, (near_one, near_two, far_one, far_two, own))
+    odd = bit(place_ref, 0)
     for pack in range(PACKS):
         up = jnp.zeros((NZ, CY), jnp.float32)
         down = jnp.zeros((NZ, CY), jnp.float32)
@@ -192,8 +202,8 @@
                 mask = lanes_in((NZ, CY), (slot * STRIP, (slot + 1) * STRIP))
                 up = jnp.where(mask, lane_shift(values, slot * STRIP - (CY - STRIP)), up)
                 down = jnp.where(mask, lane_shift(values, slot * STRIP), down)
-        up_ref[pack] = up
-        down_ref[pack] = down
+        one_ref[pack] = jnp.where(odd, down, up)
+        two_ref[pack] = jnp.where(odd, up, down)
 
 
 class Beside:
@@ -239,8 +249,8 @@
     below[row] = jnp.where(not_bottom, pair_weight(a, depth_shift(a, 1), la, depth_shift(la, 1)), 0.0)
 
 
-def tile_kernel(curve_ref, far_low, low, own, high, far_high, conc, label, coeff, west, below):
-    at = pieces((far_low, low, own, high, far_high))
+def tile_kernel(place_ref, curve_ref, near_one, near_two, far_one, far_two, own, conc, label, coeff, west, below):
+    at = pieces(place_ref, (near_one, near_two, far_one, far_two, own))
     for row in range(ROWS):
         conc[row] = at(0, row)
         label[row] = at(1, row)
@@ -253,7 +263,7 @@
 
 
 def setup_kernel(
-    curve_ref, inv_ref, table_ref, conc0, label0, coeff0, west0, below0, left_ref, right_ref,
+    place_ref, curve_ref, inv_ref, table_ref, conc0, label0, coeff0, west0, below0, one_ref, two_ref,
     west1, below1, south_out, inverse_out, source_out, out_ref,
     conc1, label1, coeff1, line_ref,
 ):
@@ -262,8 +272,10 @@
     m_left, m_left_own = lanes_in(tile, (96, 112)), lanes_in(tile, (125, 128))
     m_end, m_start = lanes_in(tile, (13, 16)), lanes_in(tile, (112, 115))
     zero = jnp.zeros(tile, jnp.float32)
+    odd = bit(place_ref, 0)
     for pack in range(PACKS):
-        from_left, from_right = left_ref[pack], right_ref[pack]
+        one, two = one_ref[pack], two_ref[pack]
+        from_left, from_right = jnp.where(odd, one, two), jnp.where(odd, two, one)
         for part in range(8):
             index = pack * 8 + part
             if index >= 2 * ROWS:
@@ -356,16 +368,16 @@
                         out_ref[base + row] = jnp.where(minus, lane_shift(result, -16), merged)
                 now, flow = following, onward
 
-    whole = [block for block in range(-2, 3) if -wide <= 8 * block and 8 * block + 7 <= CX - 1 + wide]
+    whole = [-1, 0, 1] if wide >= 5 else []
     for block in range(-2, 3):
         low, high = max(-wide, 8 * block), min(CX - 1 + wide, 8 * block + 7)
-        if low > high or (block in whole and len(whole) > 1):
+        if low > high or block in whole:
             continue
         base = HALO + 8 * block
         box_low, box_high = max(8 * block - OV, -HALO), min(8 * block + 7 + OV, CX - 1 + HALO)
         at = lambda row: row - 8 * block
         solve(base, at(low), at(high), at(box_low), at(box_high), ROWS - base)
-    if len(whole) > 1:
+    if whole:
 
         def body(number, _):
             solve(HALO + 8 * (number + whole[0]), 0, CX - 1, -OV, CX - 1 + OV, CX + OV + 1)
@@ -400,7 +412,7 @@
             blocks.append(jnp.where(odd, choice[1], choice[0]))
         return jnp.concatenate(blocks, axis=0)
 
-    left, own, right = (weighted(a[...]) for a in answers)
+    left, own, right = (weighted(a) for a in answers)
     dot = functools.partial(jnp.dot, precision=lax.Precision.HIGHEST, preferred_element_type=jnp.float32)
     own_at = lambda n: dot(own, table_ref[OWN + n * CY : OWN + (n + 1) * CY, :])
     for s, target in enumerate((flat_ref, wavy_ref)):
@@ -413,7 +425,10 @@
 def update_kernel(*refs, reach, first):
     refs = list(refs)
     take = lambda count: [refs.pop(0) for _ in range(count)]
-    odd_ref, left_ref, own_ref, right_ref = take(4)
+    place_ref, one_ref, own_ref, two_ref = take(4)
+    right_column = bit(place_ref, 0)
+    one, two = one_ref[...], two_ref[...]
+    answers = (jnp.where(right_column, one, two), own_ref[...], jnp.where(right_column, two, one))
     x_ref, source_ref, west0, west1, south_ref, below0, below1 = take(7)
     west_ref, below_ref = Beside(west0, west1), Beside(below0, below1)
     (table_ref,) = take(1)
@@ -427,7 +442,7 @@
         updated_ref, residual_ref = take(2)
         flat_ref, wavy_ref = take(2)
         u_ref = None
-    coarse_rows(odd_ref[0] == 1, (left_ref, own_ref, right_ref), table_ref, flat_ref, wavy_ref)
+    coarse_rows(bit(place_ref, 3), answers, table_ref, flat_ref, wavy_ref)
     wave = table_ref[WAVE : WAVE + NZ, :]
     wave = jnp.concatenate([wave, wave], axis=1)
 
@@ -442,6 +457,9 @@
             u_ref[row + HALO] = value
         return value
 
+    if reach:
+        for row in (-reach - 2, -reach - 1, CX + reach, CX + reach + 1):
+            r_ref[row + HALO] = jnp.zeros((NZ, LANES), jnp.float32)
     before, now = fresh(-reach - 1), fresh(-reach)
     flow = west_ref[HALO - reach] * (now - before)
     for row in range(-reach, CX + reach):
@@ -468,10 +486,17 @@
     return jax.ShapeDtypeStruct(shape, jnp.float32)
 
 
-def moved(array, axis, by):
+def swapped(array, axis, apart):
     size = lax.axis_size(axis)
-    pairs = [(i, i + by) for i in range(size) if 0 <= i + by < size]
-    return lax.ppermute(array, axis, pairs)
+    arrays = array if isinstance(array, (list, tuple)) else (array, array)
+    results = []
+    for offset, values in zip((0, apart), arrays):
+        pairs = []
+        for low in range(size - apart):
+            if (low - offset) % (2 * apart) < apart:
+                pairs += [(low, low + apart), (low + apart, low)]
+        results.append(lax.ppermute(values, axis, pairs))
+    return results
 
 
 def room(mebibytes):
@@ -487,8 +512,8 @@
     n_y = size // N_Z
     along_z = [[y * N_Z + z for z in range(N_Z)] for y in range(n_y)]
     along_y = [[y * N_Z + z for y in range(n_y)] for z in range(N_Z)]
-    odd = (lax.axis_index("gx") & 1).astype(jnp.int32).reshape(1)
-    odd, concentration = lax.optimization_barrier((odd, concentration))
+    place = (8 * lax.axis_index("gx") + lax.axis_index("gy")).astype(jnp.int32).reshape(1)
+    place, concentration = lax.optimization_barrier((place, concentration))
     frame = shaped(ROWS, NZ, LANES)
     smem, anywhere = pl.BlockSpec(memory_space=pltpu.SMEM), pl.BlockSpec(memory_space=pl.ANY)
     hbm = pl.BlockSpec(memory_space=pltpu.HBM)
@@ -496,16 +521,15 @@
     line_scratch = scratch(MZ * CX, CY)
     table_scratch = [scratch(5 * CX, LANES)] * 2
 
-    own, tail, head = pl.pallas_call(
+    own, far_one, far_two = pl.pallas_call(
         own_kernel,
         out_shape=[shaped(2, CX, NZ, CY), shaped(2, FAR, NZ, CY), shaped(2, FAR, NZ, CY)],
-        in_specs=vmem(2),
+        in_specs=[smem] + vmem(2),
         out_specs=vmem(3),
         compiler_params=room(4),
         name="own",
-    )(concentration, labels)
-    low, high = moved(own, "gx", 1), moved(own, "gx", -1)
-    far_low, far_high = moved(tail, "gx", 2), moved(head, "gx", -2)
+    )(place, concentration, labels)
+    parts = (*swapped(own, "gx", 1), *swapped((far_one, far_two), "gx", 2), own)
     curve, inverse_rows, table = pl.pallas_call(
         stage_kernel,
         out_shape=[shaped(16, CY), shaped(NB, NB * size), shaped(WAVE + NZ, CY)],
@@ -516,36 +540,35 @@
         cost_estimate=cost(1_000_000),
         name="stage",
     )(own, curve_scale, curve_slope, coarse_inv[0], jnp.asarray(tables()))
-    parts = (far_low, low, own, high, far_high)
-    up, down = pl.pallas_call(
+    strips = pl.pallas_call(
         strip_kernel,
         out_shape=[shaped(PACKS, NZ, CY)] * 2,
-        in_specs=[anywhere] + vmem(5),
+        in_specs=[smem, anywhere] + vmem(5),
         out_specs=vmem(2),
         compiler_params=room(4),
         name="strips",
-    )(curve, *parts)
-    left, right = moved(up, "gy", 1), moved(down, "gy", -1)
+    )(place, curve, *parts)
+    strips = swapped(strips, "gy", 1)
     half_frame = shaped(ROWS, NZ, CY)
     tiled = pl.pallas_call(
         tile_kernel,
         out_shape=[half_frame] * 5,
-        in_specs=vmem(6),
+        in_specs=[smem] + vmem(6),
         out_specs=vmem(5),
         compiler_params=room(4),
         cost_estimate=cost(10_000_000),
         name="tile",
-    )(curve, *parts)
+    )(place, curve, *parts)
     west0, below0 = tiled[3:]
     west1, below1, south, inverse, source, partial = pl.pallas_call(
         setup_kernel,
         out_shape=[half_frame] * 2 + [frame] * 3 + [shaped(n_y, WINDOW, CY)],
-        in_specs=vmem(10),
+        in_specs=[smem] + vmem(10),
         out_specs=vmem(6),
         scratch_shapes=[scratch(ROWS, NZ, CY)] * 3 + [line_scratch],
         compiler_params=room(8),
         name="setup",
-    )(curve, inverse_rows, table, *tiled, left, right)
+    )(place, curve, inverse_rows, table, *tiled, *strips)
     faces = (west0, west1, south, below0, below1)
 
     residual, update = source, None
@@ -568,7 +591,7 @@
             compiler_params=room(4),
             name="answer",
         )(arrived)
-        answers = (moved(answer, "gy", 1), answer, moved(answer, "gy", -1))
+        one, two = swapped(answer, "gy", 1)
         local = pl.pallas_call(
             functools.partial(local_kernel, wide=reach + 1),
             out_shape=frame,
@@ -579,7 +602,7 @@
             cost_estimate=cost(20_000_000),
             name="local",
         )(answer, residual, *faces, inverse)
-        operands = [odd, *answers, local, source, *faces, table]
+        operands = [place, one, answer, two, local, source, *faces, table]
         operands += [] if sweep == 0 else [update]
         kernel = functools.partial(update_kernel, reach=reach, first=sweep == 0)
         if reach:

time: 151 us -> 151 us (level)
  starting transfers between devices: 41.3 us -> 45.9 us
  waiting for transfers between devices: 5.93 us -> 1.91 us
    ppermute x12, starting transfers between devices: 41.3 us -> 45.9 us  [swapped(): results.append(lax.ppermute(values, axis, pairs))]
    ppermute x12, waiting for transfers between devices: 5.93 us -> 1.91 us  [swapped(): results.append(lax.ppermute(values, axis, pairs))]
  transfers between devices with their start and end apart: 12 -> 12, of which waited for: 2 -> 1; matrix products, arithmetic and copies ran while one was open for 0% -> 0% of each run, Pallas kernels for 6% -> 6%
where the time goes in v4:
time: 151 us; the launch traced here: 150 us
  blocking collectives  77.4 us (51%)
  starting transfers between devices  45.9 us (30%)
  Pallas kernels  18.8 us (12%)
  local copies, waits for them, and re-layouts  5.45 us (4%)
  waiting for transfers between devices  1.91 us (1%)
    ppermute x12, starting transfers between devices, swapped(): results.append(lax.ppermute(values, axis, pairs))  45.9 us
    all_to_all x3, blocking collectives, on_device(): lax.all_to_all(partial, 'gx', 0, 0, tiled=True, axis_index_groups=along_y)  39.7 us
    all_to_all x3, blocking collectives, on_device(): lax.all_to_all(turned, 'gx', 0, 0, tiled=True, axis_index_groups=along_z)  37.8 us
    pallas_call x3, Pallas kernels, on_device(): pl.pallas_call(functools.partial(local_kernel, wide=reach + 1), out_shape...  6.86 us
    pallas_call x1, Pallas kernels, on_device(): pl.pallas_call(setup_kernel, out_shape=[half_frame] * 2 + [frame] * 3 + [...  5.63 us
    unnamed x12, local copies, waits for them, and re-layouts  5.45 us
  transfers between devices with their start and end apart: 12, of which 1 were waited for; matrix products, arithmetic and copies ran while one was open for 0% of the time, Pallas kernels for 6%

profile of v4, /device:TPU:1, one launch (start us, length us, event | category | flops | bytes accessed | tf_op | source)
XLA Modules:
  0.0 150.4 jit_solution(10715765845108171915)
XLA Ops:
  0.7 0.8 copy-done.2
  1.5 0.8 copy-done.3
  2.4 0.7 collective-permute-start.1
  3.1 8.2 %collective-permute-start = (f32[2,8,16,128]{3,2,1,0:T(8,128)S(1)}, f32[2,8,16,128]{3,2,1,0:T(8,128)S(1)}, u32[]{:S(2)}, u32[]{:S(2)}) collective-permute-start(f32[2,8,16,128]{3,2,1,0:T(8,128)S(1)} %get-tuple-element.31._.own.refs_13_), channel_id=1, source_target_pairs={{0,8},{8,0},{16,24},{24,16},{32,40},{40,32},{48,56},{56,48},{64,72... | collective-permute-start | bytes 393224 | tf_op jit(solution)/shard_map/ppermute | solution.py:498
  11.3 7.0 %collective-permute-start.2 = (f32[2,5,16,128]{3,2,1,0:T(8,128)S(1)}, f32[2,5,16,128]{3,2,1,0:T(8,128)S(1)}, u32[]{:S(2)}, u32[]{:S(2)}) collective-permute-start(f32[2,5,16,128]{3,2,1,0:T(8,128)S(1)} %get-tuple-element.35), channel_id=1, source_target_pairs={{0,16},{16,0},{8,24},{24,8},{32,48},{48,32},{40,56},{56,40},{64,80... | collective-permute-start | bytes 245768 | tf_op jit(solution)/shard_map/ppermute | solution.py:498
  18.3 0.7 collective-permute-start.3
  19.0 1.4 copy-done
  20.4 1.1 copy-done.1
  22.7 0.8 stage.1
  23.9 3.4 %collective-permute-start.4 = (f32[9,16,128]{2,1,0:T(8,128)S(1)}, f32[9,16,128]{2,1,0:T(8,128)S(1)}, u32[]{:S(2)}, u32[]{:S(2)}) collective-permute-start(f32[9,16,128]{2,1,0:T(8,128)S(1)} %get-tuple-element.42), channel_id=1, source_target_pairs={{0,1},{1,0},{2,3},{3,2},{4,5},{5,4},{6,7},{7,6},{8,9},{9,8},{10,11... | collective-permute-start | bytes 221192 | tf_op jit(solution)/shard_map/ppermute | solution.py:498
  27.4 3.0 %collective-permute-start.5 = (f32[9,16,128]{2,1,0:T(8,128)S(1)}, f32[9,16,128]{2,1,0:T(8,128)S(1)}, u32[]{:S(2)}, u32[]{:S(2)}) collective-permute-start(f32[9,16,128]{2,1,0:T(8,128)S(1)} %get-tuple-element.43), channel_id=1, source_target_pairs={{1,2},{2,1},{3,4},{4,3},{5,6},{6,5},{9,10},{10,9},{11,12},{12,11},... | collective-permute-start | bytes 221192 | tf_op jit(solution)/shard_map/ppermute | solution.py:498
  30.4 0.7 tile.1
  31.2 1.9 %collective-permute-done.5.two_ref = f32[9,16,128]{2,1,0:T(8,128)S(1)} collective-permute-done((f32[9,16,128]{2,1,0:T(8,128)S(1)}, f32[9,16,128]{2,1,0:T(8,128)S(1)}, u32[]{:S(2)}, u32[]{:S(2)}) %collective-permute-start.5) | collective-permute-done | bytes 73760 | tf_op jit(solution)/shard_map/ppermute | solution.py:498
  33.0 5.6 %setup.1 = (f32[34,16,128]{2,1,0:T(8,128)S(1)}, f32[34,16,128]{2,1,0:T(8,128)S(1)}, f32[34,16,256]{2,1,0:T(8,128)S(1)}, f32[34,16,256]{2,1,0:T(8,128)S(1)}, f32[...) custom-call(s32[1]{0:T(128)} %bitcast.place_ref.refs_0_, f32[16,128]{1,0:T(8,128)S(1)} %get-tuple-element.32.curve_ref._, ...), custom_call_target="tpu_custom_call" | custom-call | tf_op jit(solution)/shard_map/setup/pallas_call | solution.py:563
  38.7 21.2 %all_to_all.30.in_ref = f32[8,8,128]{2,1,0:T(8,128)S(1)} all-to-all(f32[8,8,128]{2,1,0:T(8,128)S(1)} %get-tuple-element.44), channel_id=1, replica_groups={{0,96,192,288,384,480,576,672},{8,104,200,296,392,488,584,680},{16,112,..., dimensions={0} | all-to-all | bytes 65536 | tf_op jit(solution)/shard_map/all_to_all | solution.py:576
  59.9 14.2 %all_to_all.31.in_ref = f32[12,3,128]{2,1,0:T(4,128)S(1)} all-to-all(f32[12,3,128]{2,1,0:T(4,128)S(1)} %turn.3), channel_id=1, replica_groups={{0,8,16,24,32,40,48,56,64,72,80,88},{96,104,112,120,128,136,144,152,160..., dimensions={0} | all-to-all | bytes 36864 | tf_op jit(solution)/shard_map/all_to_all | solution.py:585
  74.1 5.6 %collective-permute-start.7 = (f32[3,128]{1,0:T(4,128)S(1)}, f32[3,128]{1,0:T(4,128)S(1)}, u32[]{:S(2)}, u32[]{:S(2)}) collective-permute-start(f32[3,128]{1,0:T(4,128)S(1)} %answer.3._.refs_2_), channel_id=1, source_target_pairs={{1,2},{2,1},{3,4},{4,3},{5,6},{6,5},{9,10},{10,9},{11,12},{12,11},... | collective-permute-start | bytes 4616 | tf_op jit(solution)/shard_map/ppermute | solution.py:498
  79.7 1.9 %collective-permute-start.6 = (f32[3,128]{1,0:T(4,128)S(1)}, f32[3,128]{1,0:T(4,128)S(1)}, u32[]{:S(2)}, u32[]{:S(2)}) collective-permute-start(f32[3,128]{1,0:T(4,128)S(1)} %answer.3._.refs_2_), channel_id=1, source_target_pairs={{0,1},{1,0},{2,3},{3,2},{4,5},{5,4},{6,7},{7,6},{8,9},{9,8},{10,11... | collective-permute-start | bytes 4616 | tf_op jit(solution)/shard_map/ppermute | solution.py:498
  81.6 2.9 %local.3.refs_4_ = f32[34,16,256]{2,1,0:T(8,128)S(1)} custom-call(f32[3,128]{1,0:T(4,128)S(1)} %answer.3._.refs_2_, f32[34,16,256]{2,1,0:T(8,128)S(1)} %get-tuple-element.45.r_ref.refs_5_, f32[34,16,128]{2,1,0:T(8,128)S(1)} %get-tuple-element.40.west0.refs_6_, f32[34,16,128]{2,1,0:T(8,128)S(1)} %get-tuple-element.46.west1.refs_7_, ...), custom_call_target="tpu_custom_call" | custom-call | flops 20000000 | bytes 4000000 | tf_op jit(solution)/shard_map/local/pallas_call | solution.py:595
  84.6 1.7 %update.2 = (f32[34,16,256]{2,1,0:T(8,128)S(1)}, f32[34,16,256]{2,1,0:T(8,128)S(1)}, f32[8,8,128]{2,1,0:T(8,128)S(1)}) custom-call(s32[1]{0:T(128)} %bitcast.place_ref.refs_0_, f32[3,128]{1,0:T(4,128)S(1)} %collective-permute-done.6.refs_1_, f32[3,128]{1,0:T(4,128)S(1)} %answer.3._.refs_2_, f32[3,128]{1,0:T(4,128)S(1)} %collective-permute-done.7.refs_3_, ...), custom_call_target="tpu_custom_call" | custom-call | tf_op jit(solution)/shard_map/update/pallas_call | solution.py:610
  86.3 9.2 %all_to_all.32.in_ref = f32[8,8,128]{2,1,0:T(8,128)S(1)} all-to-all(f32[8,8,128]{2,1,0:T(8,128)S(1)} %get-tuple-element.50), channel_id=1, replica_groups={{0,96,192,288,384,480,576,672},{8,104,200,296,392,488,584,680},{16,112,..., dimensions={0} | all-to-all | bytes 65536 | tf_op jit(solution)/shard_map/all_to_all | solution.py:576
  95.5 11.8 %all_to_all.33.in_ref = f32[12,3,128]{2,1,0:T(4,128)S(1)} all-to-all(f32[12,3,128]{2,1,0:T(4,128)S(1)} %turn.4), channel_id=1, replica_groups={{0,8,16,24,32,40,48,56,64,72,80,88},{96,104,112,120,128,136,144,152,160..., dimensions={0} | all-to-all | bytes 36864 | tf_op jit(solution)/shard_map/all_to_all | solution.py:585
  107.3 5.8 %collective-permute-start.9 = (f32[3,128]{1,0:T(4,128)S(1)}, f32[3,128]{1,0:T(4,128)S(1)}, u32[]{:S(2)}, u32[]{:S(2)}) collective-permute-start(f32[3,128]{1,0:T(4,128)S(1)} %answer.4._.refs_2_), channel_id=1, source_target_pairs={{1,2},{2,1},{3,4},{4,3},{5,6},{6,5},{9,10},{10,9},{11,12},{12,11},... | collective-permute-start | bytes 4616 | tf_op jit(solution)/shard_map/ppermute | solution.py:498
  113.1 1.9 %collective-permute-start.8 = (f32[3,128]{1,0:T(4,128)S(1)}, f32[3,128]{1,0:T(4,128)S(1)}, u32[]{:S(2)}, u32[]{:S(2)}) collective-permute-start(f32[3,128]{1,0:T(4,128)S(1)} %answer.4._.refs_2_), channel_id=1, source_target_pairs={{0,1},{1,0},{2,3},{3,2},{4,5},{5,4},{6,7},{7,6},{8,9},{9,8},{10,11... | collective-permute-start | bytes 4616 | tf_op jit(solution)/shard_map/ppermute | solution.py:498
  115.1 2.3 %local.4.refs_4_ = f32[34,16,256]{2,1,0:T(8,128)S(1)} custom-call(f32[3,128]{1,0:T(4,128)S(1)} %answer.4._.refs_2_, f32[34,16,256]{2,1,0:T(8,128)S(1)} %get-tuple-element.51.r_ref, f32[34,16,128]{2,1,0:T(8,128)S(1)} %get-tuple-element.40.west0.refs_6_, f32[34,16,128]{2,1,0:T(8,128)S(1)} %get-tuple-element.46.west1.refs_7_, ...), custom_call_target="tpu_custom_call" | custom-call | flops 20000000 | bytes 4000000 | tf_op jit(solution)/shard_map/local/pallas_call | solution.py:595
  117.4 1.2 update.3
  118.6 9.2 %all_to_all.34.in_ref = f32[8,8,128]{2,1,0:T(8,128)S(1)} all-to-all(f32[8,8,128]{2,1,0:T(8,128)S(1)} %get-tuple-element.53), channel_id=1, replica_groups={{0,96,192,288,384,480,576,672},{8,104,200,296,392,488,584,680},{16,112,..., dimensions={0} | all-to-all | bytes 65536 | tf_op jit(solution)/shard_map/all_to_all | solution.py:576
  127.8 11.8 %all_to_all.35.in_ref = f32[12,3,128]{2,1,0:T(4,128)S(1)} all-to-all(f32[12,3,128]{2,1,0:T(4,128)S(1)} %turn.5), channel_id=1, replica_groups={{0,8,16,24,32,40,48,56,64,72,80,88},{96,104,112,120,128,136,144,152,160..., dimensions={0} | all-to-all | bytes 36864 | tf_op jit(solution)/shard_map/all_to_all | solution.py:585
  139.6 5.7 %collective-permute-start.11 = (f32[3,128]{1,0:T(4,128)S(1)}, f32[3,128]{1,0:T(4,128)S(1)}, u32[]{:S(2)}, u32[]{:S(2)}) collective-permute-start(f32[3,128]{1,0:T(4,128)S(1)} %answer.5._.refs_2_), channel_id=1, source_target_pairs={{1,2},{2,1},{3,4},{4,3},{5,6},{6,5},{9,10},{10,9},{11,12},{12,11},... | collective-permute-start | bytes 4616 | tf_op jit(solution)/shard_map/ppermute | solution.py:498
  145.4 1.9 %collective-permute-start.10 = (f32[3,128]{1,0:T(4,128)S(1)}, f32[3,128]{1,0:T(4,128)S(1)}, u32[]{:S(2)}, u32[]{:S(2)}) collective-permute-start(f32[3,128]{1,0:T(4,128)S(1)} %answer.5._.refs_2_), channel_id=1, source_target_pairs={{0,1},{1,0},{2,3},{3,2},{4,5},{5,4},{6,7},{7,6},{8,9},{9,8},{10,11... | collective-permute-start | bytes 4616 | tf_op jit(solution)/shard_map/ppermute | solution.py:498
  147.3 1.6 %local.5.refs_4_ = f32[34,16,256]{2,1,0:T(8,128)S(1)} custom-call(f32[3,128]{1,0:T(4,128)S(1)} %answer.5._.refs_2_, f32[34,16,256]{2,1,0:T(8,128)S(1)} %get-tuple-element.54.r_ref, f32[34,16,128]{2,1,0:T(8,128)S(1)} %get-tuple-element.40.west0.refs_6_, f32[34,16,128]{2,1,0:T(8,128)S(1)} %get-tuple-element.46.west1.refs_7_, ...), custom_call_target="tpu_custom_call" | custom-call | flops 20000000 | bytes 4000000 | tf_op jit(solution)/shard_map/local/pallas_call | solution.py:595
  149.0 1.4 final.1
  (27 shorter events, 1.8 us)
Async XLA Ops:
  0.6 0.8 copy-start.2
  1.5 0.8 copy-start.3
  2.4 21.2 %collective-permute-start.1 = (f32[2,8,16,128]{3,2,1,0:T(8,128)S(1)}, f32[2,8,16,128]{3,2,1,0:T(8,128)S(1)}, u32[]{:S(2)}, u32[]{:S(2)}) collective-permute-start(f32[2,8,16,128]{3,2,1,0:T(8,128)S(1)} %get-tuple-element.31._.own.refs_13_), channel_id=1, source_target_pairs={{8,16},{16,8},{24,32},{32,24},{40,48},{48,40},{56,64},{64,56},{72,... | collective-permute-start | bytes 393224 | tf_op jit(solution)/shard_map/ppermute | solution.py:498
  3.1 20.5 %collective-permute-start = (f32[2,8,16,128]{3,2,1,0:T(8,128)S(1)}, f32[2,8,16,128]{3,2,1,0:T(8,128)S(1)}, u32[]{:S(2)}, u32[]{:S(2)}) collective-permute-start(f32[2,8,16,128]{3,2,1,0:T(8,128)S(1)} %get-tuple-element.31._.own.refs_13_), channel_id=1, source_target_pairs={{0,8},{8,0},{16,24},{24,16},{32,40},{40,32},{48,56},{56,48},{64,72... | collective-permute-start | bytes 393224 | tf_op jit(solution)/shard_map/ppermute | solution.py:498
  11.3 12.3 %collective-permute-start.2 = (f32[2,5,16,128]{3,2,1,0:T(8,128)S(1)}, f32[2,5,16,128]{3,2,1,0:T(8,128)S(1)}, u32[]{:S(2)}, u32[]{:S(2)}) collective-permute-start(f32[2,5,16,128]{3,2,1,0:T(8,128)S(1)} %get-tuple-element.35), channel_id=1, source_target_pairs={{0,16},{16,0},{8,24},{24,8},{32,48},{48,32},{40,56},{56,40},{64,80... | collective-permute-start | bytes 245768 | tf_op jit(solution)/shard_map/ppermute | solution.py:498
  18.3 5.3 %collective-permute-start.3 = (f32[2,5,16,128]{3,2,1,0:T(8,128)S(1)}, f32[2,5,16,128]{3,2,1,0:T(8,128)S(1)}, u32[]{:S(2)}, u32[]{:S(2)}) collective-permute-start(f32[2,5,16,128]{3,2,1,0:T(8,128)S(1)} %get-tuple-element.36), channel_id=1, source_target_pairs={{16,32},{32,16},{24,40},{40,24},{48,64},{64,48},{56,72},{72,56},{8... | collective-permute-start | bytes 245768 | tf_op jit(solution)/shard_map/ppermute | solution.py:498
  19.0 1.4 copy-start
  20.4 1.1 copy-start.1
  21.4 0.7 copy-start.4
  22.1 0.7 copy-start.5
  23.9 7.2 %collective-permute-start.4 = (f32[9,16,128]{2,1,0:T(8,128)S(1)}, f32[9,16,128]{2,1,0:T(8,128)S(1)}, u32[]{:S(2)}, u32[]{:S(2)}) collective-permute-start(f32[9,16,128]{2,1,0:T(8,128)S(1)} %get-tuple-element.42), channel_id=1, source_target_pairs={{0,1},{1,0},{2,3},{3,2},{4,5},{5,4},{6,7},{7,6},{8,9},{9,8},{10,11... | collective-permute-start | bytes 221192 | tf_op jit(solution)/shard_map/ppermute | solution.py:498
  27.4 5.7 %collective-permute-start.5 = (f32[9,16,128]{2,1,0:T(8,128)S(1)}, f32[9,16,128]{2,1,0:T(8,128)S(1)}, u32[]{:S(2)}, u32[]{:S(2)}) collective-permute-start(f32[9,16,128]{2,1,0:T(8,128)S(1)} %get-tuple-element.43), channel_id=1, source_target_pairs={{1,2},{2,1},{3,4},{4,3},{5,6},{6,5},{9,10},{10,9},{11,12},{12,11},... | collective-permute-start | bytes 221192 | tf_op jit(solution)/shard_map/ppermute | solution.py:498
  74.1 10.5 %collective-permute-start.7 = (f32[3,128]{1,0:T(4,128)S(1)}, f32[3,128]{1,0:T(4,128)S(1)}, u32[]{:S(2)}, u32[]{:S(2)}) collective-permute-start(f32[3,128]{1,0:T(4,128)S(1)} %answer.3._.refs_2_), channel_id=1, source_target_pairs={{1,2},{2,1},{3,4},{4,3},{5,6},{6,5},{9,10},{10,9},{11,12},{12,11},... | collective-permute-start | bytes 4616 | tf_op jit(solution)/shard_map/ppermute | solution.py:498
  79.7 4.9 %collective-permute-start.6 = (f32[3,128]{1,0:T(4,128)S(1)}, f32[3,128]{1,0:T(4,128)S(1)}, u32[]{:S(2)}, u32[]{:S(2)}) collective-permute-start(f32[3,128]{1,0:T(4,128)S(1)} %answer.3._.refs_2_), channel_id=1, source_target_pairs={{0,1},{1,0},{2,3},{3,2},{4,5},{5,4},{6,7},{7,6},{8,9},{9,8},{10,11... | collective-permute-start | bytes 4616 | tf_op jit(solution)/shard_map/ppermute | solution.py:498
  107.3 10.1 %collective-permute-start.9 = (f32[3,128]{1,0:T(4,128)S(1)}, f32[3,128]{1,0:T(4,128)S(1)}, u32[]{:S(2)}, u32[]{:S(2)}) collective-permute-start(f32[3,128]{1,0:T(4,128)S(1)} %answer.4._.refs_2_), channel_id=1, source_target_pairs={{1,2},{2,1},{3,4},{4,3},{5,6},{6,5},{9,10},{10,9},{11,12},{12,11},... | collective-permute-start | bytes 4616 | tf_op jit(solution)/shard_map/ppermute | solution.py:498
  113.1 4.2 %collective-permute-start.8 = (f32[3,128]{1,0:T(4,128)S(1)}, f32[3,128]{1,0:T(4,128)S(1)}, u32[]{:S(2)}, u32[]{:S(2)}) collective-permute-start(f32[3,128]{1,0:T(4,128)S(1)} %answer.4._.refs_2_), channel_id=1, source_target_pairs={{0,1},{1,0},{2,3},{3,2},{4,5},{5,4},{6,7},{7,6},{8,9},{9,8},{10,11... | collective-permute-start | bytes 4616 | tf_op jit(solution)/shard_map/ppermute | solution.py:498
  139.6 9.3 %collective-permute-start.11 = (f32[3,128]{1,0:T(4,128)S(1)}, f32[3,128]{1,0:T(4,128)S(1)}, u32[]{:S(2)}, u32[]{:S(2)}) collective-permute-start(f32[3,128]{1,0:T(4,128)S(1)} %answer.5._.refs_2_), channel_id=1, source_target_pairs={{1,2},{2,1},{3,4},{4,3},{5,6},{6,5},{9,10},{10,9},{11,12},{12,11},... | collective-permute-start | bytes 4616 | tf_op jit(solution)/shard_map/ppermute | solution.py:498
  145.4 3.6 %collective-permute-start.10 = (f32[3,128]{1,0:T(4,128)S(1)}, f32[3,128]{1,0:T(4,128)S(1)}, u32[]{:S(2)}, u32[]{:S(2)}) collective-permute-start(f32[3,128]{1,0:T(4,128)S(1)} %answer.5._.refs_2_), channel_id=1, source_target_pairs={{0,1},{1,0},{2,3},{3,2},{4,5},{5,4},{6,7},{7,6},{8,9},{9,8},{10,11... | collective-permute-start | bytes 4616 | tf_op jit(solution)/shard_map/ppermute | solution.py:498

commit v5 on v4

--- a/solution.py
+++ b/solution.py
@@ -139,11 +139,22 @@
                 out_ref[group, place : place + 1, :] = total
 
 
-def own_kernel(place_ref, conc_ref, label_ref, out_ref, one_ref, two_ref):
+def bit(place_ref, which):
+    return ((place_ref[0] >> which) & 1) == 1
+
+
+def own_kernel(place_ref, conc_hbm, label_hbm, out_ref, one_ref, two_ref, conc_ref, label_ref, sems):
+    copies = [
+        pltpu.make_async_copy(conc_hbm, conc_ref, sems.at[0]),
+        pltpu.make_async_copy(label_hbm, label_ref, sems.at[1]),
+    ]
+    for copy in copies:
+        copy.start()
     upper = bit(place_ref, 4)
-    for x in range(CX):
-        for kind, values in enumerate((conc_ref[:, x, :], label_ref[:, x, :].astype(jnp.float32))):
-            out_ref[kind, x] = values
+    for kind, copy in enumerate(copies):
+        copy.wait()
+        for x in range(CX):
+            out_ref[kind, x] = conc_ref[:, x, :] if kind == 0 else label_ref[:, x, :].astype(jnp.float32)
     for kind in range(2):
         for row in range(FAR):
             head, tail = out_ref[kind, row], out_ref[kind, CX - FAR + row]
@@ -151,22 +162,10 @@
             two_ref[kind, row] = jnp.where(upper, tail, head)
 
 
-def stage_kernel(_, scale_ref, slope_ref, inv_hbm, table_hbm, curve_ref, inv_ref, table_ref, sems):
-    copies = [
-        pltpu.make_async_copy(inv_hbm, inv_ref, sems.at[0]),
-        pltpu.make_async_copy(table_hbm, table_ref, sems.at[1]),
-    ]
-    for copy in copies:
-        copy.start()
+def curve_rows(scale_ref, slope_ref, curve_ref):
     for n, ref in enumerate((scale_ref, slope_ref)):
         for k in range(8):
             curve_ref[8 * n + k : 8 * n + k + 1, :] = jnp.full((1, CY), ref[k], jnp.float32)
-    for copy in copies:
-        copy.wait()
-
-
-def bit(place_ref, which):
-    return ((place_ref[0] >> which) & 1) == 1
 
 
 def pieces(place_ref, refs):
@@ -189,7 +188,7 @@
     return at
 
 
-def strip_kernel(place_ref, _, near_one, near_two, far_one, far_two, own, one_ref, two_ref):
+def strip_kernel(place_ref, near_one, near_two, far_one, far_two, own, one_ref, two_ref):
     at = pieces(place_ref, (near_one, near_two, far_one, far_two, own))
     odd = bit(place_ref, 0)
     for pack in range(PACKS):
@@ -249,11 +248,35 @@
     below[row] = jnp.where(not_bottom, pair_weight(a, depth_shift(a, 1), la, depth_shift(la, 1)), 0.0)
 
 
-def tile_kernel(place_ref, curve_ref, near_one, near_two, far_one, far_two, own, conc, label, coeff, west, below):
+def tile_sums(row, conc, west, below):
+    following, before = jnp.minimum(row + 1, ROWS - 1), jnp.maximum(row - 1, 0)
+    c, w, e, b = conc[row], west[row], west[following], below[row]
+    upward = b * (c - depth_shift(c, 1))
+    flux = e * (conc[following] - c) - w * (c - conc[before]) - (upward - depth_shift(upward, -1))
+    return INVERSE_STEP + w + e + b + depth_shift(b, -1), flux
+
+
+def tile_kernel(
+    place_ref, scale_hbm, slope_hbm, inv_hbm, table_hbm, near_one, near_two, far_one, far_two, own,
+    conc, label, coeff, west, below, diagonal, source, conc_edge, label_edge, curve_ref, inv_ref, table_ref,
+    scale_ref, slope_ref, sems,
+):
+    sources = (scale_hbm, slope_hbm, inv_hbm, table_hbm)
+    targets = (scale_ref, slope_ref, inv_ref, table_ref)
+    copies = [pltpu.make_async_copy(a, b, sems.at[n]) for n, (a, b) in enumerate(zip(sources, targets))]
+    for copy in copies:
+        copy.start()
     at = pieces(place_ref, (near_one, near_two, far_one, far_two, own))
-    for row in range(ROWS):
-        conc[row] = at(0, row)
-        label[row] = at(1, row)
+    end, start = lanes_in((NZ, CY), (13, 16)), lanes_in((NZ, CY), (112, 115))
+    for kind, (target, edge) in enumerate(((conc, conc_edge), (label, label_edge))):
+        for row in range(ROWS):
+            values = at(kind, row)
+            target[row] = values
+            beside = jnp.where(end, lane_shift(values, 16), 0.0)
+            edge[row] = jnp.where(start, lane_shift(values, -16), beside)
+    copies[0].wait()
+    copies[1].wait()
+    curve_rows(scale_ref, slope_ref, curve_ref)
 
     def fill(row):
         coeff[row] = diffusivity(conc[row], label[row], curve_ref)
@@ -261,17 +284,24 @@
     rows_in_pairs(fill)
     rows_in_pairs(lambda row: tile_faces(row, coeff, label, west, below))
 
+    def sums(row):
+        diagonal[row], source[row] = tile_sums(row, conc, west, below)
+
+    rows_in_pairs(sums)
+    copies[2].wait()
+    copies[3].wait()
+
 
 def setup_kernel(
-    place_ref, curve_ref, inv_ref, table_ref, conc0, label0, coeff0, west0, below0, one_ref, two_ref,
+    place_ref,
+    conc0, label0, coeff0, west0, below0, diagonal0, source0, conc_edge, label_edge, curve_ref, inv_ref, table_ref,
+    one_ref, two_ref,
     west1, below1, south_out, inverse_out, source_out, out_ref,
     conc1, label1, coeff1, line_ref,
 ):
     tile = (NZ, CY)
     m_right, m_right_own = lanes_in(tile, (16, 32)), lanes_in(tile, (0, 3))
     m_left, m_left_own = lanes_in(tile, (96, 112)), lanes_in(tile, (125, 128))
-    m_end, m_start = lanes_in(tile, (13, 16)), lanes_in(tile, (112, 115))
-    zero = jnp.zeros(tile, jnp.float32)
     odd = bit(place_ref, 0)
     for pack in range(PACKS):
         one, two = one_ref[pack], two_ref[pack]
@@ -281,39 +311,30 @@
             if index >= 2 * ROWS:
                 continue
             kind, row = index // ROWS, index % ROWS
-            first, second = ((conc0, conc1), (label0, label1))[kind]
-            values, slot = first[row], part * STRIP
-            merged = jnp.where(m_right, lane_shift(from_right, 16 - slot), zero)
+            edge, second = ((conc_edge, conc1), (label_edge, label1))[kind]
+            slot = part * STRIP
+            merged = jnp.where(m_right, lane_shift(from_right, 16 - slot), edge[row])
             merged = jnp.where(m_right_own, lane_shift(from_right, -slot), merged)
             merged = jnp.where(m_left, lane_shift(from_left, 96 - slot), merged)
-            merged = jnp.where(m_left_own, lane_shift(from_left, 112 - slot), merged)
-            merged = jnp.where(m_end, lane_shift(values, 16), merged)
-            second[row] = jnp.where(m_start, lane_shift(values, -16), merged)
+            second[row] = jnp.where(m_left_own, lane_shift(from_left, 112 - slot), merged)
 
     def fill(row):
         coeff1[row] = diffusivity(conc1[row], label1[row], curve_ref)
 
     rows_in_pairs(fill)
+    rows_in_pairs(lambda row: tile_faces(row, coeff1, label1, west1, below1))
     coeff, label, conc = Beside(coeff0, coeff1), Beside(label0, label1), Beside(conc0, conc1)
-
-    def faces(row):
-        tile_faces(row, coeff1, label1, west1, below1)
-        a, la = coeff[row], label[row]
-        south_out[row] = pair_weight(a, lane_shift(a, 1), la, lane_shift(la, 1))
-
-    rows_in_pairs(faces)
-    west_all, below_all = Beside(west0, west1), Beside(below0, below1)
     box = lanes_in((NZ, LANES), (0, 130), (142, 160), (224, 242), (254, 256))
 
     def operator(row):
-        following = jnp.minimum(row + 1, ROWS - 1)
-        before = jnp.maximum(row - 1, 0)
-        west, east, south, below = west_all[row], west_all[following], south_out[row], below_all[row]
-        c = conc[row]
-        diagonal = INVERSE_STEP + west + east + south + lane_shift(south, -1) + below + depth_shift(below, -1)
+        a, la, c = coeff[row], label[row], conc[row]
+        south = pair_weight(a, lane_shift(a, 1), la, lane_shift(la, 1))
+        south_out[row] = south
+        diagonal1, source1 = tile_sums(row, conc1, west1, below1)
+        diagonal = jnp.concatenate([diagonal0[row], diagonal1], axis=1) + south + lane_shift(south, -1)
         inverse_out[row] = jnp.where(box, 1.0 / diagonal, 0.0)
-        flux = east * (conc[following] - c) - west * (c - conc[before])
-        source_out[row] = flux - side_flux(c, south, below)
+        across = south * (c - lane_shift(c, 1))
+        source_out[row] = jnp.concatenate([source0[row], source1], axis=1) - (across - lane_shift(across, -1))
 
     rows_in_pairs(operator)
     spread_moments(lambda x: source_out[HALO + x, :, :CY], table_ref, inv_ref, line_ref, out_ref)
@@ -503,8 +524,8 @@
     return pltpu.CompilerParams(vmem_limit_bytes=mebibytes * 2**20)
 
 
-def cost(flops):
-    return pl.CostEstimate(flops=flops, bytes_accessed=4_000_000, transcendentals=0)
+def cost(flops, accessed=4_000_000):
+    return pl.CostEstimate(flops=flops, bytes_accessed=accessed, transcendentals=0)
 
 
 def on_device(concentration, labels, curve_scale, curve_slope, coarse_inv):
@@ -516,59 +537,54 @@
     place, concentration = lax.optimization_barrier((place, concentration))
     frame = shaped(ROWS, NZ, LANES)
     smem, anywhere = pl.BlockSpec(memory_space=pltpu.SMEM), pl.BlockSpec(memory_space=pl.ANY)
-    hbm = pl.BlockSpec(memory_space=pltpu.HBM)
     scratch = lambda *shape: pltpu.VMEM(shape, jnp.float32)
     line_scratch = scratch(MZ * CX, CY)
     table_scratch = [scratch(5 * CX, LANES)] * 2
 
-    own, far_one, far_two = pl.pallas_call(
+    kept = lambda array: pltpu.with_memory_space_constraint(array, pltpu.HBM)
+    hbm = pl.BlockSpec(memory_space=pltpu.HBM)
+    own, *far = pl.pallas_call(
         own_kernel,
-        out_shape=[shaped(2, CX, NZ, CY), shaped(2, FAR, NZ, CY), shaped(2, FAR, NZ, CY)],
-        in_specs=[smem] + vmem(2),
+        out_shape=[shaped(2, CX, NZ, CY)] + [shaped(2, FAR, NZ, CY)] * 2,
+        in_specs=[smem, hbm, hbm],
         out_specs=vmem(3),
+        scratch_shapes=[scratch(NZ, CX, CY), pltpu.VMEM((NZ, CX, CY), jnp.int32), pltpu.SemaphoreType.DMA((2,))],
         compiler_params=room(4),
         name="own",
-    )(place, concentration, labels)
-    parts = (*swapped(own, "gx", 1), *swapped((far_one, far_two), "gx", 2), own)
-    curve, inverse_rows, table = pl.pallas_call(
-        stage_kernel,
-        out_shape=[shaped(16, CY), shaped(NB, NB * size), shaped(WAVE + NZ, CY)],
-        in_specs=[anywhere, smem, smem, hbm, hbm],
-        out_specs=vmem(3),
-        scratch_shapes=[pltpu.SemaphoreType.DMA((2,))],
-        compiler_params=room(4),
-        cost_estimate=cost(1_000_000),
-        name="stage",
-    )(own, curve_scale, curve_slope, coarse_inv[0], jnp.asarray(tables()))
+    )(place, kept(concentration), kept(labels))
+    parts = (*swapped(own, "gx", 1), *swapped(far, "gx", 2), own)
     strips = pl.pallas_call(
         strip_kernel,
         out_shape=[shaped(PACKS, NZ, CY)] * 2,
-        in_specs=[smem, anywhere] + vmem(5),
+        in_specs=[smem] + vmem(5),
         out_specs=vmem(2),
         compiler_params=room(4),
         name="strips",
-    )(place, curve, *parts)
+    )(place, *parts)
     strips = swapped(strips, "gy", 1)
     half_frame = shaped(ROWS, NZ, CY)
+    table = tables()
     tiled = pl.pallas_call(
         tile_kernel,
-        out_shape=[half_frame] * 5,
-        in_specs=[smem] + vmem(6),
-        out_specs=vmem(5),
+        out_shape=[half_frame] * 9 + [shaped(16, CY), shaped(NB, NB * size), shaped(*table.shape)],
+        in_specs=[smem] + [hbm] * 4 + vmem(5),
+        out_specs=vmem(12),
+        scratch_shapes=[pltpu.SMEM((8,), jnp.float32)] * 2 + [pltpu.SemaphoreType.DMA((4,))],
         compiler_params=room(4),
         cost_estimate=cost(10_000_000),
         name="tile",
-    )(place, curve, *parts)
-    west0, below0 = tiled[3:]
+    )(place, *(kept(a) for a in (curve_scale, curve_slope, coarse_inv[0], jnp.asarray(table))), *parts)
+    west0, below0 = tiled[3:5]
+    inverse_rows, table = tiled[10:]
     west1, below1, south, inverse, source, partial = pl.pallas_call(
         setup_kernel,
         out_shape=[half_frame] * 2 + [frame] * 3 + [shaped(n_y, WINDOW, CY)],
-        in_specs=[smem] + vmem(10),
+        in_specs=[smem] + vmem(14),
         out_specs=vmem(6),
         scratch_shapes=[scratch(ROWS, NZ, CY)] * 3 + [line_scratch],
         compiler_params=room(8),
         name="setup",
-    )(place, curve, inverse_rows, table, *tiled, *strips)
+    )(place, *tiled, *strips)
     faces = (west0, west1, south, below0, below1)
 
     residual, update = source, None

time: 151 us -> 148 us (0.980)
  local copies, waits for them, and re-layouts: 5.45 us -> 0 us
  blocking collectives: 77.4 us -> 79 us
    unnamed x12 -> x0, local copies, waits for them, and re-layouts: 5.45 us -> none
    all_to_all x3, blocking collectives: 39.7 us -> 42 us  [on_device(): lax.all_to_all(partial, 'gx', 0, 0, tiled=True, axis_index_groups=along_y)]
  transfers between devices with their start and end apart: 12 -> 12, of which waited for: 1 -> 2; matrix products, arithmetic and copies ran while one was open for 0% -> 0% of each run, Pallas kernels for 6% -> 6%
where the time goes in v5:
time: 148 us
  blocking collectives  79 us (53%)
  starting transfers between devices  46.8 us (32%)
  Pallas kernels  18.7 us (13%)
  waiting for transfers between devices  2.23 us (2%)
    ppermute x12, starting transfers between devices, swapped(): results.append(lax.ppermute(values, axis, pairs))  46.8 us
    all_to_all x3, blocking collectives, on_device(): lax.all_to_all(partial, 'gx', 0, 0, tiled=True, axis_index_groups=along_y)  42 us
    all_to_all x3, blocking collectives, on_device(): lax.all_to_all(turned, 'gx', 0, 0, tiled=True, axis_index_groups=along_z)  36.9 us
    pallas_call x3, Pallas kernels, on_device(): pl.pallas_call(functools.partial(local_kernel, wide=reach + 1), out_shape...  7.02 us
    pallas_call x1, Pallas kernels, on_device(): pl.pallas_call(setup_kernel, out_shape=[half_frame] * 2 + [frame] * 3 + [...  4.32 us
  transfers between devices with their start and end apart: 12, of which 2 were waited for; matrix products, arithmetic and copies ran while one was open for 0% of the time, Pallas kernels for 6%

profile of v5, /device:TPU:1, one launch (start us, length us, event | category | flops | bytes accessed | tf_op | source)
XLA Modules:
  0.0 147.6 jit_solution(12795338220935290057)
XLA Ops:
  0.6 1.0 own.1
  1.6 0.7 collective-permute-start.1
  2.3 8.2 %collective-permute-start = (f32[2,8,16,128]{3,2,1,0:T(8,128)S(1)}, f32[2,8,16,128]{3,2,1,0:T(8,128)S(1)}, u32[]{:S(2)}, u32[]{:S(2)}) collective-permute-start(f32[2,8,16,128]{3,2,1,0:T(8,128)S(1)} %get-tuple-element.35.own.refs_13_), channel_id=1, source_target_pairs={{0,8},{8,0},{16,24},{24,16},{32,40},{40,32},{48,56},{56,48},{64,72... | collective-permute-start | bytes 393224 | tf_op jit(solution)/shard_map/ppermute | solution.py:519
  10.4 7.0 %collective-permute-start.2 = (f32[2,5,16,128]{3,2,1,0:T(8,128)S(1)}, f32[2,5,16,128]{3,2,1,0:T(8,128)S(1)}, u32[]{:S(2)}, u32[]{:S(2)}) collective-permute-start(f32[2,5,16,128]{3,2,1,0:T(8,128)S(1)} %get-tuple-element.36), channel_id=1, source_target_pairs={{0,16},{16,0},{8,24},{24,8},{32,48},{48,32},{40,56},{56,40},{64,80... | collective-permute-start | bytes 245768 | tf_op jit(solution)/shard_map/ppermute | solution.py:519
  17.5 0.7 collective-permute-start.3
  18.1 1.9 %collective-permute-done.2.far_one = f32[2,5,16,128]{3,2,1,0:T(8,128)S(1)} collective-permute-done((f32[2,5,16,128]{3,2,1,0:T(8,128)S(1)}, f32[2,5,16,128]{3,2,1,0:T(8,128)S(1)}, u32[]{:S(2)}, u32[]{:S(2)}) %collective-permute-start.2) | collective-permute-done | bytes 81952 | tf_op jit(solution)/shard_map/ppermute | solution.py:519
  20.0 0.3 strips.1
  20.4 3.8 %collective-permute-start.4 = (f32[9,16,128]{2,1,0:T(8,128)S(1)}, f32[9,16,128]{2,1,0:T(8,128)S(1)}, u32[]{:S(2)}, u32[]{:S(2)}) collective-permute-start(f32[9,16,128]{2,1,0:T(8,128)S(1)} %get-tuple-element.50), channel_id=1, source_target_pairs={{0,1},{1,0},{2,3},{3,2},{4,5},{5,4},{6,7},{7,6},{8,9},{9,8},{10,11... | collective-permute-start | bytes 221192 | tf_op jit(solution)/shard_map/ppermute | solution.py:519
  24.2 3.6 %collective-permute-start.5 = (f32[9,16,128]{2,1,0:T(8,128)S(1)}, f32[9,16,128]{2,1,0:T(8,128)S(1)}, u32[]{:S(2)}, u32[]{:S(2)}) collective-permute-start(f32[9,16,128]{2,1,0:T(8,128)S(1)} %get-tuple-element.51), channel_id=1, source_target_pairs={{1,2},{2,1},{3,4},{4,3},{5,6},{6,5},{9,10},{10,9},{11,12},{12,11},... | collective-permute-start | bytes 221192 | tf_op jit(solution)/shard_map/ppermute | solution.py:519
  27.7 1.8 %tile.1 = (f32[34,16,128]{2,1,0:T(8,128)S(1)}, f32[34,16,128]{2,1,0:T(8,128)S(1)}, f32[34,16,128]{2,1,0:T(8,128)S(1)}, f32[34,16,128]{2,1,0:T(8,128)S(1)}, f32[3...) custom-call(s32[1]{0:T(128)} %bitcast.place_ref.refs_0_, ...), custom_call_target="tpu_custom_call" | custom-call | flops 10000000 | bytes 4000000 | tf_op jit(solution)/shard_map/tile/pallas_call | solution.py:567
  29.5 0.0 collective-permute-done.4.one_ref
  29.5 0.3 collective-permute-done.5.two_ref
  29.8 4.3 %setup.1 = (f32[34,16,128]{2,1,0:T(8,128)S(1)}, f32[34,16,128]{2,1,0:T(8,128)S(1)}, f32[34,16,256]{2,1,0:T(8,128)S(1)}, f32[34,16,256]{2,1,0:T(8,128)S(1)}, f32[...) custom-call(s32[1]{0:T(128)} %bitcast.place_ref.refs_0_, f32[34,16,128]{2,1,0:T(8,128)S(1)} %get-tuple-element.38.conc0, ...), custom_call_target="tpu_custom_call" | custom-call | tf_op jit(solution)/shard_map/setup/pallas_call | solution.py:579
  34.2 23.6 %all_to_all.30.in_ref = f32[8,8,128]{2,1,0:T(8,128)S(1)} all-to-all(f32[8,8,128]{2,1,0:T(8,128)S(1)} %get-tuple-element.52), channel_id=1, replica_groups={{0,96,192,288,384,480,576,672},{8,104,200,296,392,488,584,680},{16,112,..., dimensions={0} | all-to-all | bytes 65536 | tf_op jit(solution)/shard_map/all_to_all | solution.py:592
  57.7 13.4 %all_to_all.31.in_ref = f32[12,3,128]{2,1,0:T(4,128)S(1)} all-to-all(f32[12,3,128]{2,1,0:T(4,128)S(1)} %turn.3), channel_id=1, replica_groups={{0,8,16,24,32,40,48,56,64,72,80,88},{96,104,112,120,128,136,144,152,160..., dimensions={0} | all-to-all | bytes 36864 | tf_op jit(solution)/shard_map/all_to_all | solution.py:601
  71.1 5.6 %collective-permute-start.7 = (f32[3,128]{1,0:T(4,128)S(1)}, f32[3,128]{1,0:T(4,128)S(1)}, u32[]{:S(2)}, u32[]{:S(2)}) collective-permute-start(f32[3,128]{1,0:T(4,128)S(1)} %answer.3._.refs_2_), channel_id=1, source_target_pairs={{1,2},{2,1},{3,4},{4,3},{5,6},{6,5},{9,10},{10,9},{11,12},{12,11},... | collective-permute-start | bytes 4616 | tf_op jit(solution)/shard_map/ppermute | solution.py:519
  76.7 1.9 %collective-permute-start.6 = (f32[3,128]{1,0:T(4,128)S(1)}, f32[3,128]{1,0:T(4,128)S(1)}, u32[]{:S(2)}, u32[]{:S(2)}) collective-permute-start(f32[3,128]{1,0:T(4,128)S(1)} %answer.3._.refs_2_), channel_id=1, source_target_pairs={{0,1},{1,0},{2,3},{3,2},{4,5},{5,4},{6,7},{7,6},{8,9},{9,8},{10,11... | collective-permute-start | bytes 4616 | tf_op jit(solution)/shard_map/ppermute | solution.py:519
  78.7 3.0 %local.3.refs_4_ = f32[34,16,256]{2,1,0:T(8,128)S(1)} custom-call(f32[3,128]{1,0:T(4,128)S(1)} %answer.3._.refs_2_, f32[34,16,256]{2,1,0:T(8,128)S(1)} %get-tuple-element.53.r_ref.refs_5_, f32[34,16,128]{2,1,0:T(8,128)S(1)} %get-tuple-element.41.west0.refs_6_, f32[34,16,128]{2,1,0:T(8,128)S(1)} %get-tuple-element.54.west1.refs_7_, ...), custom_call_target="tpu_custom_call" | custom-call | flops 20000000 | bytes 4000000 | tf_op jit(solution)/shard_map/local/pallas_call | solution.py:611
  81.7 1.7 %update.2 = (f32[34,16,256]{2,1,0:T(8,128)S(1)}, f32[34,16,256]{2,1,0:T(8,128)S(1)}, f32[8,8,128]{2,1,0:T(8,128)S(1)}) custom-call(s32[1]{0:T(128)} %bitcast.place_ref.refs_0_, f32[3,128]{1,0:T(4,128)S(1)} %collective-permute-done.6.refs_1_, f32[3,128]{1,0:T(4,128)S(1)} %answer.3._.refs_2_, f32[3,128]{1,0:T(4,128)S(1)} %collective-permute-done.7.refs_3_, ...), custom_call_target="tpu_custom_call" | custom-call | tf_op jit(solution)/shard_map/update/pallas_call | solution.py:626
  83.4 9.2 %all_to_all.32.in_ref = f32[8,8,128]{2,1,0:T(8,128)S(1)} all-to-all(f32[8,8,128]{2,1,0:T(8,128)S(1)} %get-tuple-element.58), channel_id=1, replica_groups={{0,96,192,288,384,480,576,672},{8,104,200,296,392,488,584,680},{16,112,..., dimensions={0} | all-to-all | bytes 65536 | tf_op jit(solution)/shard_map/all_to_all | solution.py:592
  92.6 11.8 %all_to_all.33.in_ref = f32[12,3,128]{2,1,0:T(4,128)S(1)} all-to-all(f32[12,3,128]{2,1,0:T(4,128)S(1)} %turn.4), channel_id=1, replica_groups={{0,8,16,24,32,40,48,56,64,72,80,88},{96,104,112,120,128,136,144,152,160..., dimensions={0} | all-to-all | bytes 36864 | tf_op jit(solution)/shard_map/all_to_all | solution.py:601
  104.4 5.8 %collective-permute-start.9 = (f32[3,128]{1,0:T(4,128)S(1)}, f32[3,128]{1,0:T(4,128)S(1)}, u32[]{:S(2)}, u32[]{:S(2)}) collective-permute-start(f32[3,128]{1,0:T(4,128)S(1)} %answer.4._.refs_2_), channel_id=1, source_target_pairs={{1,2},{2,1},{3,4},{4,3},{5,6},{6,5},{9,10},{10,9},{11,12},{12,11},... | collective-permute-start | bytes 4616 | tf_op jit(solution)/shard_map/ppermute | solution.py:519
  110.3 1.9 %collective-permute-start.8 = (f32[3,128]{1,0:T(4,128)S(1)}, f32[3,128]{1,0:T(4,128)S(1)}, u32[]{:S(2)}, u32[]{:S(2)}) collective-permute-start(f32[3,128]{1,0:T(4,128)S(1)} %answer.4._.refs_2_), channel_id=1, source_target_pairs={{0,1},{1,0},{2,3},{3,2},{4,5},{5,4},{6,7},{7,6},{8,9},{9,8},{10,11... | collective-permute-start | bytes 4616 | tf_op jit(solution)/shard_map/ppermute | solution.py:519
  112.2 2.4 %local.4.refs_4_ = f32[34,16,256]{2,1,0:T(8,128)S(1)} custom-call(f32[3,128]{1,0:T(4,128)S(1)} %answer.4._.refs_2_, f32[34,16,256]{2,1,0:T(8,128)S(1)} %get-tuple-element.59.r_ref, f32[34,16,128]{2,1,0:T(8,128)S(1)} %get-tuple-element.41.west0.refs_6_, f32[34,16,128]{2,1,0:T(8,128)S(1)} %get-tuple-element.54.west1.refs_7_, ...), custom_call_target="tpu_custom_call" | custom-call | flops 20000000 | bytes 4000000 | tf_op jit(solution)/shard_map/local/pallas_call | solution.py:611
  114.6 0.0 collective-permute-done.8.refs_1_
  114.6 1.2 update.3
  115.8 9.2 %all_to_all.34.in_ref = f32[8,8,128]{2,1,0:T(8,128)S(1)} all-to-all(f32[8,8,128]{2,1,0:T(8,128)S(1)} %get-tuple-element.61), channel_id=1, replica_groups={{0,96,192,288,384,480,576,672},{8,104,200,296,392,488,584,680},{16,112,..., dimensions={0} | all-to-all | bytes 65536 | tf_op jit(solution)/shard_map/all_to_all | solution.py:592
  125.0 11.8 %all_to_all.35.in_ref = f32[12,3,128]{2,1,0:T(4,128)S(1)} all-to-all(f32[12,3,128]{2,1,0:T(4,128)S(1)} %turn.5), channel_id=1, replica_groups={{0,8,16,24,32,40,48,56,64,72,80,88},{96,104,112,120,128,136,144,152,160..., dimensions={0} | all-to-all | bytes 36864 | tf_op jit(solution)/shard_map/all_to_all | solution.py:601
  136.8 5.7 %collective-permute-start.11 = (f32[3,128]{1,0:T(4,128)S(1)}, f32[3,128]{1,0:T(4,128)S(1)}, u32[]{:S(2)}, u32[]{:S(2)}) collective-permute-start(f32[3,128]{1,0:T(4,128)S(1)} %answer.5._.refs_2_), channel_id=1, source_target_pairs={{1,2},{2,1},{3,4},{4,3},{5,6},{6,5},{9,10},{10,9},{11,12},{12,11},... | collective-permute-start | bytes 4616 | tf_op jit(solution)/shard_map/ppermute | solution.py:519
  142.6 1.9 %collective-permute-start.10 = (f32[3,128]{1,0:T(4,128)S(1)}, f32[3,128]{1,0:T(4,128)S(1)}, u32[]{:S(2)}, u32[]{:S(2)}) collective-permute-start(f32[3,128]{1,0:T(4,128)S(1)} %answer.5._.refs_2_), channel_id=1, source_target_pairs={{0,1},{1,0},{2,3},{3,2},{4,5},{5,4},{6,7},{7,6},{8,9},{9,8},{10,11... | collective-permute-start | bytes 4616 | tf_op jit(solution)/shard_map/ppermute | solution.py:519
  144.5 1.7 %local.5.refs_4_ = f32[34,16,256]{2,1,0:T(8,128)S(1)} custom-call(f32[3,128]{1,0:T(4,128)S(1)} %answer.5._.refs_2_, f32[34,16,256]{2,1,0:T(8,128)S(1)} %get-tuple-element.62.r_ref, f32[34,16,128]{2,1,0:T(8,128)S(1)} %get-tuple-element.41.west0.refs_6_, f32[34,16,128]{2,1,0:T(8,128)S(1)} %get-tuple-element.54.west1.refs_7_, ...), custom_call_target="tpu_custom_call" | custom-call | flops 20000000 | bytes 4000000 | tf_op jit(solution)/shard_map/local/pallas_call | solution.py:611
  146.2 1.4 final.1
  (14 shorter events, 0.1 us)
Async XLA Ops:
  1.6 18.4 %collective-permute-start.1 = (f32[2,8,16,128]{3,2,1,0:T(8,128)S(1)}, f32[2,8,16,128]{3,2,1,0:T(8,128)S(1)}, u32[]{:S(2)}, u32[]{:S(2)}) collective-permute-start(f32[2,8,16,128]{3,2,1,0:T(8,128)S(1)} %get-tuple-element.35.own.refs_13_), channel_id=1, source_target_pairs={{8,16},{16,8},{24,32},{32,24},{40,48},{48,40},{56,64},{64,56},{72,... | collective-permute-start | bytes 393224 | tf_op jit(solution)/shard_map/ppermute | solution.py:519
  2.3 17.8 %collective-permute-start = (f32[2,8,16,128]{3,2,1,0:T(8,128)S(1)}, f32[2,8,16,128]{3,2,1,0:T(8,128)S(1)}, u32[]{:S(2)}, u32[]{:S(2)}) collective-permute-start(f32[2,8,16,128]{3,2,1,0:T(8,128)S(1)} %get-tuple-element.35.own.refs_13_), channel_id=1, source_target_pairs={{0,8},{8,0},{16,24},{24,16},{32,40},{40,32},{48,56},{56,48},{64,72... | collective-permute-start | bytes 393224 | tf_op jit(solution)/shard_map/ppermute | solution.py:519
  10.4 9.6 %collective-permute-start.2 = (f32[2,5,16,128]{3,2,1,0:T(8,128)S(1)}, f32[2,5,16,128]{3,2,1,0:T(8,128)S(1)}, u32[]{:S(2)}, u32[]{:S(2)}) collective-permute-start(f32[2,5,16,128]{3,2,1,0:T(8,128)S(1)} %get-tuple-element.36), channel_id=1, source_target_pairs={{0,16},{16,0},{8,24},{24,8},{32,48},{48,32},{40,56},{56,40},{64,80... | collective-permute-start | bytes 245768 | tf_op jit(solution)/shard_map/ppermute | solution.py:519
  17.5 2.6 %collective-permute-start.3 = (f32[2,5,16,128]{3,2,1,0:T(8,128)S(1)}, f32[2,5,16,128]{3,2,1,0:T(8,128)S(1)}, u32[]{:S(2)}, u32[]{:S(2)}) collective-permute-start(f32[2,5,16,128]{3,2,1,0:T(8,128)S(1)} %get-tuple-element.37), channel_id=1, source_target_pairs={{16,32},{32,16},{24,40},{40,24},{48,64},{64,48},{56,72},{72,56},{8... | collective-permute-start | bytes 245768 | tf_op jit(solution)/shard_map/ppermute | solution.py:519
  20.4 9.2 %collective-permute-start.4 = (f32[9,16,128]{2,1,0:T(8,128)S(1)}, f32[9,16,128]{2,1,0:T(8,128)S(1)}, u32[]{:S(2)}, u32[]{:S(2)}) collective-permute-start(f32[9,16,128]{2,1,0:T(8,128)S(1)} %get-tuple-element.50), channel_id=1, source_target_pairs={{0,1},{1,0},{2,3},{3,2},{4,5},{5,4},{6,7},{7,6},{8,9},{9,8},{10,11... | collective-permute-start | bytes 221192 | tf_op jit(solution)/shard_map/ppermute | solution.py:519
  24.2 5.7 %collective-permute-start.5 = (f32[9,16,128]{2,1,0:T(8,128)S(1)}, f32[9,16,128]{2,1,0:T(8,128)S(1)}, u32[]{:S(2)}, u32[]{:S(2)}) collective-permute-start(f32[9,16,128]{2,1,0:T(8,128)S(1)} %get-tuple-element.51), channel_id=1, source_target_pairs={{1,2},{2,1},{3,4},{4,3},{5,6},{6,5},{9,10},{10,9},{11,12},{12,11},... | collective-permute-start | bytes 221192 | tf_op jit(solution)/shard_map/ppermute | solution.py:519
  71.1 10.5 %collective-permute-start.7 = (f32[3,128]{1,0:T(4,128)S(1)}, f32[3,128]{1,0:T(4,128)S(1)}, u32[]{:S(2)}, u32[]{:S(2)}) collective-permute-start(f32[3,128]{1,0:T(4,128)S(1)} %answer.3._.refs_2_), channel_id=1, source_target_pairs={{1,2},{2,1},{3,4},{4,3},{5,6},{6,5},{9,10},{10,9},{11,12},{12,11},... | collective-permute-start | bytes 4616 | tf_op jit(solution)/shard_map/ppermute | solution.py:519
  76.7 4.9 %collective-permute-start.6 = (f32[3,128]{1,0:T(4,128)S(1)}, f32[3,128]{1,0:T(4,128)S(1)}, u32[]{:S(2)}, u32[]{:S(2)}) collective-permute-start(f32[3,128]{1,0:T(4,128)S(1)} %answer.3._.refs_2_), channel_id=1, source_target_pairs={{0,1},{1,0},{2,3},{3,2},{4,5},{5,4},{6,7},{7,6},{8,9},{9,8},{10,11... | collective-permute-start | bytes 4616 | tf_op jit(solution)/shard_map/ppermute | solution.py:519
  104.4 10.1 %collective-permute-start.9 = (f32[3,128]{1,0:T(4,128)S(1)}, f32[3,128]{1,0:T(4,128)S(1)}, u32[]{:S(2)}, u32[]{:S(2)}) collective-permute-start(f32[3,128]{1,0:T(4,128)S(1)} %answer.4._.refs_2_), channel_id=1, source_target_pairs={{1,2},{2,1},{3,4},{4,3},{5,6},{6,5},{9,10},{10,9},{11,12},{12,11},... | collective-permute-start | bytes 4616 | tf_op jit(solution)/shard_map/ppermute | solution.py:519
  110.3 4.3 %collective-permute-start.8 = (f32[3,128]{1,0:T(4,128)S(1)}, f32[3,128]{1,0:T(4,128)S(1)}, u32[]{:S(2)}, u32[]{:S(2)}) collective-permute-start(f32[3,128]{1,0:T(4,128)S(1)} %answer.4._.refs_2_), channel_id=1, source_target_pairs={{0,1},{1,0},{2,3},{3,2},{4,5},{5,4},{6,7},{7,6},{8,9},{9,8},{10,11... | collective-permute-start | bytes 4616 | tf_op jit(solution)/shard_map/ppermute | solution.py:519
  136.8 9.4 %collective-permute-start.11 = (f32[3,128]{1,0:T(4,128)S(1)}, f32[3,128]{1,0:T(4,128)S(1)}, u32[]{:S(2)}, u32[]{:S(2)}) collective-permute-start(f32[3,128]{1,0:T(4,128)S(1)} %answer.5._.refs_2_), channel_id=1, source_target_pairs={{1,2},{2,1},{3,4},{4,3},{5,6},{6,5},{9,10},{10,9},{11,12},{12,11},... | collective-permute-start | bytes 4616 | tf_op jit(solution)/shard_map/ppermute | solution.py:519
  142.6 3.6 %collective-permute-start.10 = (f32[3,128]{1,0:T(4,128)S(1)}, f32[3,128]{1,0:T(4,128)S(1)}, u32[]{:S(2)}, u32[]{:S(2)}) collective-permute-start(f32[3,128]{1,0:T(4,128)S(1)} %answer.5._.refs_2_), channel_id=1, source_target_pairs={{0,1},{1,0},{2,3},{3,2},{4,5},{5,4},{6,7},{7,6},{8,9},{9,8},{10,11... | collective-permute-start | bytes 4616 | tf_op jit(solution)/shard_map/ppermute | solution.py:519

commit v6 on v5

--- a/solution.py
+++ b/solution.py
@@ -54,20 +54,19 @@
                 n = (s * MX + p) * MY + q
                 mix[n, s * CX : (s + 1) * CX] = first[p] * (flat if s == 0 else 1.0)
                 rows[n] = second[q]
-    half = np.zeros((2, CX, 2 * NB))
-    spread = np.zeros((2 * NB, MZ, CY))
-    for h in range(2):
-        for s in range(MZ):
-            for p in range(MX):
-                for q in range(MY):
-                    n = h * NB + (s * MX + p) * MY + q
-                    half[h, :, n] = first[p]
-                    spread[n, s] = second[q] * (flat if s == 0 else 1.0)
-    own = np.zeros((2 * NB, MZ, LANES))
+    near = np.zeros((CX, NB))
+    spread = np.zeros((NB, MZ, CY))
+    for s in range(MZ):
+        for p in range(MX):
+            for q in range(MY):
+                n = (s * MX + p) * MY + q
+                near[:, n] = first[p]
+                spread[n, s] = second[q] * (flat if s == 0 else 1.0)
+    own = np.zeros((NB, MZ, LANES))
     own[:, :, :CY] = spread
     own[:, :, CY + 13 : CY + 16] = spread[:, :, 125:128]
     own[:, :, CY + 112 : CY + 115] = spread[:, :, 0:3]
-    side = np.zeros((2, 2 * NB, MZ, CY))
+    side = np.zeros((2, NB, MZ, CY))
     side[0, :, :, 96:112] = spread[:, :, 112:128]
     side[0, :, :, 125:128] = spread[:, :, 125:128]
     side[1, :, :, 16:32] = spread[:, :, 0:16]
@@ -75,12 +74,12 @@
     wave = np.broadcast_to(depth[1][:, None], (NZ, CY))
     mix = np.pad(mix, ((0, 0), (0, CY - MZ * CX)))
     parts = [own[:, s, k * CY : (k + 1) * CY] for s in range(MZ) for k in range(2)]
-    parts += [side[:, :, s].reshape(4 * NB, CY) for s in range(MZ)]
-    parts += [rows, mix, half.reshape(2 * CX, 2 * NB), wave]
+    parts += [side[:, :, s].reshape(2 * NB, CY) for s in range(MZ)]
+    parts += [rows, mix, np.concatenate([near, near], axis=1), wave]
     return np.concatenate(parts, axis=0).astype(np.float32)
 
 
-OWN, SIDE, MOMENT, MIX, HALF, WAVE = 0, 512, 1024, 1088, 1152, 1168
+OWN, SIDE, MOMENT, MIX, NEAR, WAVE = 0, 256, 512, 576, 640, 648
 
 
 def lane_shift(values, by):
@@ -213,13 +212,15 @@
         return jnp.concatenate([self.first[row], self.second[row]], axis=1)
 
 
-def rows_in_pairs(step):
-    def both(pair, _):
-        step(2 * pair)
-        step(2 * pair + 1)
+def each_row(step):
+    def four(group, _):
+        for k in range(4):
+            step(4 * group + k)
         return 0
 
-    lax.fori_loop(0, ROWS // 2, both, 0)
+    lax.fori_loop(0, ROWS // 4, four, 0)
+    for row in range(ROWS // 4 * 4, ROWS):
+        step(row)
 
 
 def diffusivity(conc, label, curve_ref):
@@ -281,13 +282,13 @@
     def fill(row):
         coeff[row] = diffusivity(conc[row], label[row], curve_ref)
 
-    rows_in_pairs(fill)
-    rows_in_pairs(lambda row: tile_faces(row, coeff, label, west, below))
+    each_row(fill)
+    each_row(lambda row: tile_faces(row, coeff, label, west, below))
 
     def sums(row):
         diagonal[row], source[row] = tile_sums(row, conc, west, below)
 
-    rows_in_pairs(sums)
+    each_row(sums)
     copies[2].wait()
     copies[3].wait()
 
@@ -321,8 +322,8 @@
     def fill(row):
         coeff1[row] = diffusivity(conc1[row], label1[row], curve_ref)
 
-    rows_in_pairs(fill)
-    rows_in_pairs(lambda row: tile_faces(row, coeff1, label1, west1, below1))
+    each_row(fill)
+    each_row(lambda row: tile_faces(row, coeff1, label1, west1, below1))
     coeff, label, conc = Beside(coeff0, coeff1), Beside(label0, label1), Beside(conc0, conc1)
     box = lanes_in((NZ, LANES), (0, 130), (142, 160), (224, 242), (254, 256))
 
@@ -336,7 +337,7 @@
         across = south * (c - lane_shift(c, 1))
         source_out[row] = jnp.concatenate([source0[row], source1], axis=1) - (across - lane_shift(across, -1))
 
-    rows_in_pairs(operator)
+    each_row(operator)
     spread_moments(lambda x: source_out[HALO + x, :, :CY], table_ref, inv_ref, line_ref, out_ref)
 
 
@@ -348,7 +349,7 @@
     plus = lanes_in((NZ, LANES), (253, 256), (141, 144))
     minus = lanes_in((NZ, LANES), (128, 131), (240, 243))
 
-    def solve(base, low, high, box_low, box_high, limit):
+    def solve(base, low, high, box_low, box_high, limit, u_ref, q_ref, x_ref):
         def start(row):
             if not box_low <= row <= box_high:
                 return None
@@ -397,11 +398,13 @@
         base = HALO + 8 * block
         box_low, box_high = max(8 * block - OV, -HALO), min(8 * block + 7 + OV, CX - 1 + HALO)
         at = lambda row: row - 8 * block
-        solve(base, at(low), at(high), at(box_low), at(box_high), ROWS - base)
+        boxes = (ref.at[block % 3] for ref in (u_ref, q_ref, x_ref))
+        solve(base, at(low), at(high), at(box_low), at(box_high), ROWS - base, *boxes)
     if whole:
 
         def body(number, _):
-            solve(HALO + 8 * (number + whole[0]), 0, CX - 1, -OV, CX - 1 + OV, CX + OV + 1)
+            boxes = (ref.at[0] for ref in (u_ref, q_ref, x_ref))
+            solve(HALO + 8 * (number + whole[0]), 0, CX - 1, -OV, CX - 1 + OV, CX + OV + 1, *boxes)
             return 0
 
         lax.fori_loop(0, len(whole), body, 0)
@@ -423,24 +426,29 @@
 
 
 def coarse_rows(odd, answers, table_ref, flat_ref, wavy_ref):
-    def weighted(answer):
-        blocks = []
+    near = table_ref[NEAR : NEAR + CX, :]
+    left_half = lanes_in((SPAN, CY), (0, NB))
+
+    def blocks(low, high):
+        turned = [lane_shift(a, NB) for a in (low, high)]
+        even, uneven = jnp.where(left_half, low, turned[1]), jnp.where(left_half, turned[0], high)
+        rows = []
         for block in range(5):
             choice = []
             for index in (block, block + 1):
-                row = jnp.broadcast_to(answer[index // 2 : index // 2 + 1, :], (CX, 2 * NB))
-                choice.append(row * table_ref[HALF + (index % 2) * CX : HALF + (index % 2 + 1) * CX, :])
-            blocks.append(jnp.where(odd, choice[1], choice[0]))
-        return jnp.concatenate(blocks, axis=0)
-
-    left, own, right = (weighted(a) for a in answers)
+                source = uneven if index % 2 else even
+                choice.append(jnp.broadcast_to(source[index // 2 : index // 2 + 1, :], (CX, CY)))
+            rows.append(jnp.where(odd, choice[1], choice[0]) * near)
+        return jnp.concatenate(rows, axis=0)
+
+    left, own, right = answers
+    own, sides = blocks(own, own)[:, :NB], blocks(left, right)
     dot = functools.partial(jnp.dot, precision=lax.Precision.HIGHEST, preferred_element_type=jnp.float32)
-    own_at = lambda n: dot(own, table_ref[OWN + n * CY : OWN + (n + 1) * CY, :])
+    own_at = lambda n: dot(own, table_ref[OWN + n * NB : OWN + (n + 1) * NB, :])
     for s, target in enumerate((flat_ref, wavy_ref)):
-        first = SIDE + s * 4 * NB
-        beside = dot(left, table_ref[first : first + CY, :]) + dot(right, table_ref[first + CY : first + 2 * CY, :])
+        first = SIDE + s * 2 * NB
         target[:, :CY] = own_at(2 * s)
-        target[:, CY:] = own_at(2 * s + 1) + beside
+        target[:, CY:] = own_at(2 * s + 1) + dot(sides, table_ref[first : first + 2 * NB, :])
 
 
 def update_kernel(*refs, reach, first):
@@ -613,7 +621,7 @@
             out_shape=frame,
             in_specs=[anywhere] + vmem(7),
             out_specs=vmem(1)[0],
-            scratch_shapes=[scratch(CX + 2 * OV, NZ, LANES)] * 3,
+            scratch_shapes=[scratch(3, CX + 2 * OV, NZ, LANES)] * 3,
             compiler_params=room(8),
             cost_estimate=cost(20_000_000),
             name="local",

time: 148 us -> 147 us (level)
  Pallas kernels: 18.7 us -> 16.9 us
where the time goes in v6:
time: 147 us; the launch traced here: 146 us
  blocking collectives  79 us (54%)
  starting transfers between devices  46.8 us (32%)
  Pallas kernels  16.9 us (11%)
  waiting for transfers between devices  2.33 us (2%)
    ppermute x12, starting transfers between devices, swapped(): results.append(lax.ppermute(values, axis, pairs))  46.8 us
    all_to_all x3, blocking collectives, on_device(): lax.all_to_all(partial, 'gx', 0, 0, tiled=True, axis_index_groups=along_y)  42 us
    all_to_all x3, blocking collectives, on_device(): lax.all_to_all(turned, 'gx', 0, 0, tiled=True, axis_index_groups=along_z)  36.9 us
    pallas_call x3, Pallas kernels, on_device(): pl.pallas_call(functools.partial(local_kernel, wide=reach + 1), out_shape...  6.99 us
  transfers between devices with their start and end apart: 12, of which 2 were waited for; matrix products, arithmetic and copies ran while one was open for 0% of the time, Pallas kernels for 6%

profile of v6, /device:TPU:1, one launch (start us, length us, event | category | flops | bytes accessed | tf_op | source)
XLA Modules:
  0.0 145.9 jit_solution(12332866169125549197)
XLA Ops:
  0.6 1.0 own.1
  1.6 0.7 collective-permute-start.1
  2.3 8.2 %collective-permute-start = (f32[2,8,16,128]{3,2,1,0:T(8,128)S(1)}, f32[2,8,16,128]{3,2,1,0:T(8,128)S(1)}, u32[]{:S(2)}, u32[]{:S(2)}) collective-permute-start(f32[2,8,16,128]{3,2,1,0:T(8,128)S(1)} %get-tuple-element.35.own.refs_13_), channel_id=1, source_target_pairs={{0,8},{8,0},{16,24},{24,16},{32,40},{40,32},{48,56},{56,48},{64,72... | collective-permute-start | bytes 393224 | tf_op jit(solution)/shard_map/ppermute | solution.py:527
  10.4 7.0 %collective-permute-start.2 = (f32[2,5,16,128]{3,2,1,0:T(8,128)S(1)}, f32[2,5,16,128]{3,2,1,0:T(8,128)S(1)}, u32[]{:S(2)}, u32[]{:S(2)}) collective-permute-start(f32[2,5,16,128]{3,2,1,0:T(8,128)S(1)} %get-tuple-element.36), channel_id=1, source_target_pairs={{0,16},{16,0},{8,24},{24,8},{32,48},{48,32},{40,56},{56,40},{64,80... | collective-permute-start | bytes 245768 | tf_op jit(solution)/shard_map/ppermute | solution.py:527
  17.5 0.7 collective-permute-start.3
  18.1 1.9 %collective-permute-done.2.far_one = f32[2,5,16,128]{3,2,1,0:T(8,128)S(1)} collective-permute-done((f32[2,5,16,128]{3,2,1,0:T(8,128)S(1)}, f32[2,5,16,128]{3,2,1,0:T(8,128)S(1)}, u32[]{:S(2)}, u32[]{:S(2)}) %collective-permute-start.2) | collective-permute-done | bytes 81952 | tf_op jit(solution)/shard_map/ppermute | solution.py:527
  20.0 0.0 collective-permute-done.3.far_two
  20.0 0.0 collective-permute-done.1.near_two
  20.0 0.3 strips.1
  20.4 3.8 %collective-permute-start.4 = (f32[9,16,128]{2,1,0:T(8,128)S(1)}, f32[9,16,128]{2,1,0:T(8,128)S(1)}, u32[]{:S(2)}, u32[]{:S(2)}) collective-permute-start(f32[9,16,128]{2,1,0:T(8,128)S(1)} %get-tuple-element.50), channel_id=1, source_target_pairs={{0,1},{1,0},{2,3},{3,2},{4,5},{5,4},{6,7},{7,6},{8,9},{9,8},{10,11... | collective-permute-start | bytes 221192 | tf_op jit(solution)/shard_map/ppermute | solution.py:527
  24.2 3.6 %collective-permute-start.5 = (f32[9,16,128]{2,1,0:T(8,128)S(1)}, f32[9,16,128]{2,1,0:T(8,128)S(1)}, u32[]{:S(2)}, u32[]{:S(2)}) collective-permute-start(f32[9,16,128]{2,1,0:T(8,128)S(1)} %get-tuple-element.51), channel_id=1, source_target_pairs={{1,2},{2,1},{3,4},{4,3},{5,6},{6,5},{9,10},{10,9},{11,12},{12,11},... | collective-permute-start | bytes 221192 | tf_op jit(solution)/shard_map/ppermute | solution.py:527
  27.7 1.7 %tile.1 = (f32[34,16,128]{2,1,0:T(8,128)S(1)}, f32[34,16,128]{2,1,0:T(8,128)S(1)}, f32[34,16,128]{2,1,0:T(8,128)S(1)}, f32[34,16,128]{2,1,0:T(8,128)S(1)}, f32[3...) custom-call(s32[1]{0:T(128)} %bitcast.place_ref.refs_0_, ...), custom_call_target="tpu_custom_call" | custom-call | flops 10000000 | bytes 4000000 | tf_op jit(solution)/shard_map/tile/pallas_call | solution.py:575
  29.4 0.4 collective-permute-done.5.two_ref
  29.8 2.9 %setup.1 = (f32[34,16,128]{2,1,0:T(8,128)S(1)}, f32[34,16,128]{2,1,0:T(8,128)S(1)}, f32[34,16,256]{2,1,0:T(8,128)S(1)}, f32[34,16,256]{2,1,0:T(8,128)S(1)}, f32[...) custom-call(s32[1]{0:T(128)} %bitcast.place_ref.refs_0_, f32[34,16,128]{2,1,0:T(8,128)S(1)} %get-tuple-element.38.conc0, ...), custom_call_target="tpu_custom_call" | custom-call | tf_op jit(solution)/shard_map/setup/pallas_call | solution.py:587
  32.7 23.6 %all_to_all.30.in_ref = f32[8,8,128]{2,1,0:T(8,128)S(1)} all-to-all(f32[8,8,128]{2,1,0:T(8,128)S(1)} %get-tuple-element.52), channel_id=1, replica_groups={{0,96,192,288,384,480,576,672},{8,104,200,296,392,488,584,680},{16,112,..., dimensions={0} | all-to-all | bytes 65536 | tf_op jit(solution)/shard_map/all_to_all | solution.py:600
  56.3 13.4 %all_to_all.31.in_ref = f32[12,3,128]{2,1,0:T(4,128)S(1)} all-to-all(f32[12,3,128]{2,1,0:T(4,128)S(1)} %turn.3), channel_id=1, replica_groups={{0,8,16,24,32,40,48,56,64,72,80,88},{96,104,112,120,128,136,144,152,160..., dimensions={0} | all-to-all | bytes 36864 | tf_op jit(solution)/shard_map/all_to_all | solution.py:609
  69.7 5.6 %collective-permute-start.7 = (f32[3,128]{1,0:T(4,128)S(1)}, f32[3,128]{1,0:T(4,128)S(1)}, u32[]{:S(2)}, u32[]{:S(2)}) collective-permute-start(f32[3,128]{1,0:T(4,128)S(1)} %answer.3._.refs_2_), channel_id=1, source_target_pairs={{1,2},{2,1},{3,4},{4,3},{5,6},{6,5},{9,10},{10,9},{11,12},{12,11},... | collective-permute-start | bytes 4616 | tf_op jit(solution)/shard_map/ppermute | solution.py:527
  75.3 1.9 %collective-permute-start.6 = (f32[3,128]{1,0:T(4,128)S(1)}, f32[3,128]{1,0:T(4,128)S(1)}, u32[]{:S(2)}, u32[]{:S(2)}) collective-permute-start(f32[3,128]{1,0:T(4,128)S(1)} %answer.3._.refs_2_), channel_id=1, source_target_pairs={{0,1},{1,0},{2,3},{3,2},{4,5},{5,4},{6,7},{7,6},{8,9},{9,8},{10,11... | collective-permute-start | bytes 4616 | tf_op jit(solution)/shard_map/ppermute | solution.py:527
  77.2 3.0 %local.3.refs_4_ = f32[34,16,256]{2,1,0:T(8,128)S(1)} custom-call(f32[3,128]{1,0:T(4,128)S(1)} %answer.3._.refs_2_, f32[34,16,256]{2,1,0:T(8,128)S(1)} %get-tuple-element.53.r_ref.refs_5_, f32[34,16,128]{2,1,0:T(8,128)S(1)} %get-tuple-element.41.west0.refs_6_, f32[34,16,128]{2,1,0:T(8,128)S(1)} %get-tuple-element.54.west1.refs_7_, ...), custom_call_target="tpu_custom_call" | custom-call | flops 20000000 | bytes 4000000 | tf_op jit(solution)/shard_map/local/pallas_call | solution.py:619
  80.2 1.6 %update.2 = (f32[34,16,256]{2,1,0:T(8,128)S(1)}, f32[34,16,256]{2,1,0:T(8,128)S(1)}, f32[8,8,128]{2,1,0:T(8,128)S(1)}) custom-call(s32[1]{0:T(128)} %bitcast.place_ref.refs_0_, f32[3,128]{1,0:T(4,128)S(1)} %collective-permute-done.6.refs_1_, f32[3,128]{1,0:T(4,128)S(1)} %answer.3._.refs_2_, f32[3,128]{1,0:T(4,128)S(1)} %collective-permute-done.7.refs_3_, ...), custom_call_target="tpu_custom_call" | custom-call | tf_op jit(solution)/shard_map/update/pallas_call | solution.py:634
  81.9 9.2 %all_to_all.32.in_ref = f32[8,8,128]{2,1,0:T(8,128)S(1)} all-to-all(f32[8,8,128]{2,1,0:T(8,128)S(1)} %get-tuple-element.58), channel_id=1, replica_groups={{0,96,192,288,384,480,576,672},{8,104,200,296,392,488,584,680},{16,112,..., dimensions={0} | all-to-all | bytes 65536 | tf_op jit(solution)/shard_map/all_to_all | solution.py:600
  91.1 11.8 %all_to_all.33.in_ref = f32[12,3,128]{2,1,0:T(4,128)S(1)} all-to-all(f32[12,3,128]{2,1,0:T(4,128)S(1)} %turn.4), channel_id=1, replica_groups={{0,8,16,24,32,40,48,56,64,72,80,88},{96,104,112,120,128,136,144,152,160..., dimensions={0} | all-to-all | bytes 36864 | tf_op jit(solution)/shard_map/all_to_all | solution.py:609
  102.9 5.8 %collective-permute-start.9 = (f32[3,128]{1,0:T(4,128)S(1)}, f32[3,128]{1,0:T(4,128)S(1)}, u32[]{:S(2)}, u32[]{:S(2)}) collective-permute-start(f32[3,128]{1,0:T(4,128)S(1)} %answer.4._.refs_2_), channel_id=1, source_target_pairs={{1,2},{2,1},{3,4},{4,3},{5,6},{6,5},{9,10},{10,9},{11,12},{12,11},... | collective-permute-start | bytes 4616 | tf_op jit(solution)/shard_map/ppermute | solution.py:527
  108.7 1.9 %collective-permute-start.8 = (f32[3,128]{1,0:T(4,128)S(1)}, f32[3,128]{1,0:T(4,128)S(1)}, u32[]{:S(2)}, u32[]{:S(2)}) collective-permute-start(f32[3,128]{1,0:T(4,128)S(1)} %answer.4._.refs_2_), channel_id=1, source_target_pairs={{0,1},{1,0},{2,3},{3,2},{4,5},{5,4},{6,7},{7,6},{8,9},{9,8},{10,11... | collective-permute-start | bytes 4616 | tf_op jit(solution)/shard_map/ppermute | solution.py:527
  110.7 2.3 %local.4.refs_4_ = f32[34,16,256]{2,1,0:T(8,128)S(1)} custom-call(f32[3,128]{1,0:T(4,128)S(1)} %answer.4._.refs_2_, f32[34,16,256]{2,1,0:T(8,128)S(1)} %get-tuple-element.59.r_ref, f32[34,16,128]{2,1,0:T(8,128)S(1)} %get-tuple-element.41.west0.refs_6_, f32[34,16,128]{2,1,0:T(8,128)S(1)} %get-tuple-element.54.west1.refs_7_, ...), custom_call_target="tpu_custom_call" | custom-call | flops 20000000 | bytes 4000000 | tf_op jit(solution)/shard_map/local/pallas_call | solution.py:619
  113.0 1.1 update.3
  114.1 9.2 %all_to_all.34.in_ref = f32[8,8,128]{2,1,0:T(8,128)S(1)} all-to-all(f32[8,8,128]{2,1,0:T(8,128)S(1)} %get-tuple-element.61), channel_id=1, replica_groups={{0,96,192,288,384,480,576,672},{8,104,200,296,392,488,584,680},{16,112,..., dimensions={0} | all-to-all | bytes 65536 | tf_op jit(solution)/shard_map/all_to_all | solution.py:600
  123.4 11.8 %all_to_all.35.in_ref = f32[12,3,128]{2,1,0:T(4,128)S(1)} all-to-all(f32[12,3,128]{2,1,0:T(4,128)S(1)} %turn.5), channel_id=1, replica_groups={{0,8,16,24,32,40,48,56,64,72,80,88},{96,104,112,120,128,136,144,152,160..., dimensions={0} | all-to-all | bytes 36864 | tf_op jit(solution)/shard_map/all_to_all | solution.py:609
  135.2 5.7 %collective-permute-start.11 = (f32[3,128]{1,0:T(4,128)S(1)}, f32[3,128]{1,0:T(4,128)S(1)}, u32[]{:S(2)}, u32[]{:S(2)}) collective-permute-start(f32[3,128]{1,0:T(4,128)S(1)} %answer.5._.refs_2_), channel_id=1, source_target_pairs={{1,2},{2,1},{3,4},{4,3},{5,6},{6,5},{9,10},{10,9},{11,12},{12,11},... | collective-permute-start | bytes 4616 | tf_op jit(solution)/shard_map/ppermute | solution.py:527
  140.9 1.9 %collective-permute-start.10 = (f32[3,128]{1,0:T(4,128)S(1)}, f32[3,128]{1,0:T(4,128)S(1)}, u32[]{:S(2)}, u32[]{:S(2)}) collective-permute-start(f32[3,128]{1,0:T(4,128)S(1)} %answer.5._.refs_2_), channel_id=1, source_target_pairs={{0,1},{1,0},{2,3},{3,2},{4,5},{5,4},{6,7},{7,6},{8,9},{9,8},{10,11... | collective-permute-start | bytes 4616 | tf_op jit(solution)/shard_map/ppermute | solution.py:527
  142.9 1.7 %local.5.refs_4_ = f32[34,16,256]{2,1,0:T(8,128)S(1)} custom-call(f32[3,128]{1,0:T(4,128)S(1)} %answer.5._.refs_2_, f32[34,16,256]{2,1,0:T(8,128)S(1)} %get-tuple-element.62.r_ref, f32[34,16,128]{2,1,0:T(8,128)S(1)} %get-tuple-element.41.west0.refs_6_, f32[34,16,128]{2,1,0:T(8,128)S(1)} %get-tuple-element.54.west1.refs_7_, ...), custom_call_target="tpu_custom_call" | custom-call | flops 20000000 | bytes 4000000 | tf_op jit(solution)/shard_map/local/pallas_call | solution.py:619
  144.6 1.3 final.1
  (14 shorter events, 0.1 us)
Async XLA Ops:
  1.6 18.4 %collective-permute-start.1 = (f32[2,8,16,128]{3,2,1,0:T(8,128)S(1)}, f32[2,8,16,128]{3,2,1,0:T(8,128)S(1)}, u32[]{:S(2)}, u32[]{:S(2)}) collective-permute-start(f32[2,8,16,128]{3,2,1,0:T(8,128)S(1)} %get-tuple-element.35.own.refs_13_), channel_id=1, source_target_pairs={{8,16},{16,8},{24,32},{32,24},{40,48},{48,40},{56,64},{64,56},{72,... | collective-permute-start | bytes 393224 | tf_op jit(solution)/shard_map/ppermute | solution.py:527
  2.3 17.8 %collective-permute-start = (f32[2,8,16,128]{3,2,1,0:T(8,128)S(1)}, f32[2,8,16,128]{3,2,1,0:T(8,128)S(1)}, u32[]{:S(2)}, u32[]{:S(2)}) collective-permute-start(f32[2,8,16,128]{3,2,1,0:T(8,128)S(1)} %get-tuple-element.35.own.refs_13_), channel_id=1, source_target_pairs={{0,8},{8,0},{16,24},{24,16},{32,40},{40,32},{48,56},{56,48},{64,72... | collective-permute-start | bytes 393224 | tf_op jit(solution)/shard_map/ppermute | solution.py:527
  10.4 9.6 %collective-permute-start.2 = (f32[2,5,16,128]{3,2,1,0:T(8,128)S(1)}, f32[2,5,16,128]{3,2,1,0:T(8,128)S(1)}, u32[]{:S(2)}, u32[]{:S(2)}) collective-permute-start(f32[2,5,16,128]{3,2,1,0:T(8,128)S(1)} %get-tuple-element.36), channel_id=1, source_target_pairs={{0,16},{16,0},{8,24},{24,8},{32,48},{48,32},{40,56},{56,40},{64,80... | collective-permute-start | bytes 245768 | tf_op jit(solution)/shard_map/ppermute | solution.py:527
  17.5 2.6 %collective-permute-start.3 = (f32[2,5,16,128]{3,2,1,0:T(8,128)S(1)}, f32[2,5,16,128]{3,2,1,0:T(8,128)S(1)}, u32[]{:S(2)}, u32[]{:S(2)}) collective-permute-start(f32[2,5,16,128]{3,2,1,0:T(8,128)S(1)} %get-tuple-element.37), channel_id=1, source_target_pairs={{16,32},{32,16},{24,40},{40,24},{48,64},{64,48},{56,72},{72,56},{8... | collective-permute-start | bytes 245768 | tf_op jit(solution)/shard_map/ppermute | solution.py:527
  20.4 9.1 %collective-permute-start.4 = (f32[9,16,128]{2,1,0:T(8,128)S(1)}, f32[9,16,128]{2,1,0:T(8,128)S(1)}, u32[]{:S(2)}, u32[]{:S(2)}) collective-permute-start(f32[9,16,128]{2,1,0:T(8,128)S(1)} %get-tuple-element.50), channel_id=1, source_target_pairs={{0,1},{1,0},{2,3},{3,2},{4,5},{5,4},{6,7},{7,6},{8,9},{9,8},{10,11... | collective-permute-start | bytes 221192 | tf_op jit(solution)/shard_map/ppermute | solution.py:527
  24.2 5.7 %collective-permute-start.5 = (f32[9,16,128]{2,1,0:T(8,128)S(1)}, f32[9,16,128]{2,1,0:T(8,128)S(1)}, u32[]{:S(2)}, u32[]{:S(2)}) collective-permute-start(f32[9,16,128]{2,1,0:T(8,128)S(1)} %get-tuple-element.51), channel_id=1, source_target_pairs={{1,2},{2,1},{3,4},{4,3},{5,6},{6,5},{9,10},{10,9},{11,12},{12,11},... | collective-permute-start | bytes 221192 | tf_op jit(solution)/shard_map/ppermute | solution.py:527
  69.7 10.5 %collective-permute-start.7 = (f32[3,128]{1,0:T(4,128)S(1)}, f32[3,128]{1,0:T(4,128)S(1)}, u32[]{:S(2)}, u32[]{:S(2)}) collective-permute-start(f32[3,128]{1,0:T(4,128)S(1)} %answer.3._.refs_2_), channel_id=1, source_target_pairs={{1,2},{2,1},{3,4},{4,3},{5,6},{6,5},{9,10},{10,9},{11,12},{12,11},... | collective-permute-start | bytes 4616 | tf_op jit(solution)/shard_map/ppermute | solution.py:527
  75.3 4.9 %collective-permute-start.6 = (f32[3,128]{1,0:T(4,128)S(1)}, f32[3,128]{1,0:T(4,128)S(1)}, u32[]{:S(2)}, u32[]{:S(2)}) collective-permute-start(f32[3,128]{1,0:T(4,128)S(1)} %answer.3._.refs_2_), channel_id=1, source_target_pairs={{0,1},{1,0},{2,3},{3,2},{4,5},{5,4},{6,7},{7,6},{8,9},{9,8},{10,11... | collective-permute-start | bytes 4616 | tf_op jit(solution)/shard_map/ppermute | solution.py:527
  102.9 10.1 %collective-permute-start.9 = (f32[3,128]{1,0:T(4,128)S(1)}, f32[3,128]{1,0:T(4,128)S(1)}, u32[]{:S(2)}, u32[]{:S(2)}) collective-permute-start(f32[3,128]{1,0:T(4,128)S(1)} %answer.4._.refs_2_), channel_id=1, source_target_pairs={{1,2},{2,1},{3,4},{4,3},{5,6},{6,5},{9,10},{10,9},{11,12},{12,11},... | collective-permute-start | bytes 4616 | tf_op jit(solution)/shard_map/ppermute | solution.py:527
  108.7 4.3 %collective-permute-start.8 = (f32[3,128]{1,0:T(4,128)S(1)}, f32[3,128]{1,0:T(4,128)S(1)}, u32[]{:S(2)}, u32[]{:S(2)}) collective-permute-start(f32[3,128]{1,0:T(4,128)S(1)} %answer.4._.refs_2_), channel_id=1, source_target_pairs={{0,1},{1,0},{2,3},{3,2},{4,5},{5,4},{6,7},{7,6},{8,9},{9,8},{10,11... | collective-permute-start | bytes 4616 | tf_op jit(solution)/shard_map/ppermute | solution.py:527
  135.2 9.4 %collective-permute-start.11 = (f32[3,128]{1,0:T(4,128)S(1)}, f32[3,128]{1,0:T(4,128)S(1)}, u32[]{:S(2)}, u32[]{:S(2)}) collective-permute-start(f32[3,128]{1,0:T(4,128)S(1)} %answer.5._.refs_2_), channel_id=1, source_target_pairs={{1,2},{2,1},{3,4},{4,3},{5,6},{6,5},{9,10},{10,9},{11,12},{12,11},... | collective-permute-start | bytes 4616 | tf_op jit(solution)/shard_map/ppermute | solution.py:527
  140.9 3.6 %collective-permute-start.10 = (f32[3,128]{1,0:T(4,128)S(1)}, f32[3,128]{1,0:T(4,128)S(1)}, u32[]{:S(2)}, u32[]{:S(2)}) collective-permute-start(f32[3,128]{1,0:T(4,128)S(1)} %answer.5._.refs_2_), channel_id=1, source_target_pairs={{0,1},{1,0},{2,3},{3,2},{4,5},{5,4},{6,7},{7,6},{8,9},{9,8},{10,11... | collective-permute-start | bytes 4616 | tf_op jit(solution)/shard_map/ppermute | solution.py:527

commit v7 on v6

--- a/solution.py
+++ b/solution.py
@@ -71,7 +71,7 @@
     side[0, :, :, 125:128] = spread[:, :, 125:128]
     side[1, :, :, 16:32] = spread[:, :, 0:16]
     side[1, :, :, 0:3] = spread[:, :, 0:3]
-    wave = np.broadcast_to(depth[1][:, None], (NZ, CY))
+    wave = np.broadcast_to(np.concatenate([depth[1][0::2], depth[1][1::2]])[:, None], (NZ, CY))
     mix = np.pad(mix, ((0, 0), (0, CY - MZ * CX)))
     parts = [own[:, s, k * CY : (k + 1) * CY] for s in range(MZ) for k in range(2)]
     parts += [side[:, :, s].reshape(2 * NB, CY) for s in range(MZ)]
@@ -87,7 +87,14 @@
 
 
 def depth_shift(values, by):
-    return pltpu.roll(values, by % NZ, axis=0)
+    even, uneven = values[: NZ // 2], values[NZ // 2 :]
+    if by > 0:
+        return jnp.concatenate([pltpu.roll(uneven, 1, axis=0), even], axis=0)
+    return jnp.concatenate([uneven, pltpu.roll(even, NZ // 2 - 1, axis=0)], axis=0)
+
+
+def depths(parity):
+    return pl.ds(parity, NZ // 2, stride=2)
 
 
 def lanes_in(shape, *ranges):
@@ -153,7 +160,9 @@
     for kind, copy in enumerate(copies):
         copy.wait()
         for x in range(CX):
-            out_ref[kind, x] = conc_ref[:, x, :] if kind == 0 else label_ref[:, x, :].astype(jnp.float32)
+            for parity in range(2):
+                values = (conc_ref, label_ref)[kind][depths(parity), x, :]
+                out_ref[kind, x, parity * NZ // 2 : (parity + 1) * NZ // 2] = values.astype(jnp.float32)
     for kind in range(2):
         for row in range(FAR):
             head, tail = out_ref[kind, row], out_ref[kind, CX - FAR + row]
@@ -500,8 +509,9 @@
         if reach:
             r_ref[row + HALO] = remain
         else:
-            updated_ref[:, row, :] = packed_ref[0, row] + now[:, :CY]
-            residual_ref[:, row, :] = remain[:, :CY]
+            for target, values in ((updated_ref, packed_ref[0, row] + now[:, :CY]), (residual_ref, remain[:, :CY])):
+                target[depths(0), row, :] = values[: NZ // 2]
+                target[depths(1), row, :] = values[NZ // 2 :]
         now, flow = following, onward
     if reach:
         spread_moments(lambda x: r_ref[HALO + x, :, :CY], table_ref, inv_ref, line_ref, out_ref)

time: 147 us -> 146 us (level)
  no operation moved by 1% of the time
where the time goes in v7:
time: 146 us
  blocking collectives  79 us (54%)
  starting transfers between devices  46.8 us (32%)
  Pallas kernels  16.8 us (12%)
  waiting for transfers between devices  2.33 us (2%)
    ppermute x12, starting transfers between devices, swapped(): results.append(lax.ppermute(values, axis, pairs))  46.8 us
    all_to_all x3, blocking collectives, on_device(): lax.all_to_all(partial, 'gx', 0, 0, tiled=True, axis_index_groups=along_y)  42 us
    all_to_all x3, blocking collectives, on_device(): lax.all_to_all(turned, 'gx', 0, 0, tiled=True, axis_index_groups=along_z)  36.9 us
    pallas_call x3, Pallas kernels, on_device(): pl.pallas_call(functools.partial(local_kernel, wide=reach + 1), out_shape...  6.92 us
  transfers between devices with their start and end apart: 12, of which 2 were waited for; matrix products, arithmetic and copies ran while one was open for 0% of the time, Pallas kernels for 6%

profile of v7, /device:TPU:1, one launch (start us, length us, event | category | flops | bytes accessed | tf_op | source)
XLA Modules:
  0.0 145.8 jit_solution(10666407072924042941)
XLA Ops:
  0.6 1.0 own.1
  1.6 0.7 collective-permute-start.1
  2.3 8.2 %collective-permute-start = (f32[2,8,16,128]{3,2,1,0:T(8,128)S(1)}, f32[2,8,16,128]{3,2,1,0:T(8,128)S(1)}, u32[]{:S(2)}, u32[]{:S(2)}) collective-permute-start(f32[2,8,16,128]{3,2,1,0:T(8,128)S(1)} %get-tuple-element.35.own.refs_13_), channel_id=1, source_target_pairs={{0,8},{8,0},{16,24},{24,16},{32,40},{40,32},{48,56},{56,48},{64,72... | collective-permute-start | bytes 393224 | tf_op jit(solution)/shard_map/ppermute | solution.py:537
  10.4 7.0 %collective-permute-start.2 = (f32[2,5,16,128]{3,2,1,0:T(8,128)S(1)}, f32[2,5,16,128]{3,2,1,0:T(8,128)S(1)}, u32[]{:S(2)}, u32[]{:S(2)}) collective-permute-start(f32[2,5,16,128]{3,2,1,0:T(8,128)S(1)} %get-tuple-element.36), channel_id=1, source_target_pairs={{0,16},{16,0},{8,24},{24,8},{32,48},{48,32},{40,56},{56,40},{64,80... | collective-permute-start | bytes 245768 | tf_op jit(solution)/shard_map/ppermute | solution.py:537
  17.5 0.7 collective-permute-start.3
  18.1 1.9 %collective-permute-done.2.far_one = f32[2,5,16,128]{3,2,1,0:T(8,128)S(1)} collective-permute-done((f32[2,5,16,128]{3,2,1,0:T(8,128)S(1)}, f32[2,5,16,128]{3,2,1,0:T(8,128)S(1)}, u32[]{:S(2)}, u32[]{:S(2)}) %collective-permute-start.2) | collective-permute-done | bytes 81952 | tf_op jit(solution)/shard_map/ppermute | solution.py:537
  20.0 0.3 strips.1
  20.4 3.8 %collective-permute-start.4 = (f32[9,16,128]{2,1,0:T(8,128)S(1)}, f32[9,16,128]{2,1,0:T(8,128)S(1)}, u32[]{:S(2)}, u32[]{:S(2)}) collective-permute-start(f32[9,16,128]{2,1,0:T(8,128)S(1)} %get-tuple-element.50), channel_id=1, source_target_pairs={{0,1},{1,0},{2,3},{3,2},{4,5},{5,4},{6,7},{7,6},{8,9},{9,8},{10,11... | collective-permute-start | bytes 221192 | tf_op jit(solution)/shard_map/ppermute | solution.py:537
  24.2 3.6 %collective-permute-start.5 = (f32[9,16,128]{2,1,0:T(8,128)S(1)}, f32[9,16,128]{2,1,0:T(8,128)S(1)}, u32[]{:S(2)}, u32[]{:S(2)}) collective-permute-start(f32[9,16,128]{2,1,0:T(8,128)S(1)} %get-tuple-element.51), channel_id=1, source_target_pairs={{1,2},{2,1},{3,4},{4,3},{5,6},{6,5},{9,10},{10,9},{11,12},{12,11},... | collective-permute-start | bytes 221192 | tf_op jit(solution)/shard_map/ppermute | solution.py:537
  27.7 1.7 %tile.1 = (f32[34,16,128]{2,1,0:T(8,128)S(1)}, f32[34,16,128]{2,1,0:T(8,128)S(1)}, f32[34,16,128]{2,1,0:T(8,128)S(1)}, f32[34,16,128]{2,1,0:T(8,128)S(1)}, f32[3...) custom-call(s32[1]{0:T(128)} %bitcast.place_ref.refs_0_, ...), custom_call_target="tpu_custom_call" | custom-call | flops 10000000 | bytes 4000000 | tf_op jit(solution)/shard_map/tile/pallas_call | solution.py:585
  29.4 0.4 collective-permute-done.5.two_ref
  29.8 2.9 %setup.1 = (f32[34,16,128]{2,1,0:T(8,128)S(1)}, f32[34,16,128]{2,1,0:T(8,128)S(1)}, f32[34,16,256]{2,1,0:T(8,128)S(1)}, f32[34,16,256]{2,1,0:T(8,128)S(1)}, f32[...) custom-call(s32[1]{0:T(128)} %bitcast.place_ref.refs_0_, f32[34,16,128]{2,1,0:T(8,128)S(1)} %get-tuple-element.38.conc0, ...), custom_call_target="tpu_custom_call" | custom-call | tf_op jit(solution)/shard_map/setup/pallas_call | solution.py:597
  32.7 23.6 %all_to_all.30.in_ref = f32[8,8,128]{2,1,0:T(8,128)S(1)} all-to-all(f32[8,8,128]{2,1,0:T(8,128)S(1)} %get-tuple-element.52), channel_id=1, replica_groups={{0,96,192,288,384,480,576,672},{8,104,200,296,392,488,584,680},{16,112,..., dimensions={0} | all-to-all | bytes 65536 | tf_op jit(solution)/shard_map/all_to_all | solution.py:610
  56.3 13.4 %all_to_all.31.in_ref = f32[12,3,128]{2,1,0:T(4,128)S(1)} all-to-all(f32[12,3,128]{2,1,0:T(4,128)S(1)} %turn.3), channel_id=1, replica_groups={{0,8,16,24,32,40,48,56,64,72,80,88},{96,104,112,120,128,136,144,152,160..., dimensions={0} | all-to-all | bytes 36864 | tf_op jit(solution)/shard_map/all_to_all | solution.py:619
  69.7 5.6 %collective-permute-start.7 = (f32[3,128]{1,0:T(4,128)S(1)}, f32[3,128]{1,0:T(4,128)S(1)}, u32[]{:S(2)}, u32[]{:S(2)}) collective-permute-start(f32[3,128]{1,0:T(4,128)S(1)} %answer.3._.refs_2_), channel_id=1, source_target_pairs={{1,2},{2,1},{3,4},{4,3},{5,6},{6,5},{9,10},{10,9},{11,12},{12,11},... | collective-permute-start | bytes 4616 | tf_op jit(solution)/shard_map/ppermute | solution.py:537
  75.3 1.9 %collective-permute-start.6 = (f32[3,128]{1,0:T(4,128)S(1)}, f32[3,128]{1,0:T(4,128)S(1)}, u32[]{:S(2)}, u32[]{:S(2)}) collective-permute-start(f32[3,128]{1,0:T(4,128)S(1)} %answer.3._.refs_2_), channel_id=1, source_target_pairs={{0,1},{1,0},{2,3},{3,2},{4,5},{5,4},{6,7},{7,6},{8,9},{9,8},{10,11... | collective-permute-start | bytes 4616 | tf_op jit(solution)/shard_map/ppermute | solution.py:537
  77.2 2.9 %local.3.refs_4_ = f32[34,16,256]{2,1,0:T(8,128)S(1)} custom-call(f32[3,128]{1,0:T(4,128)S(1)} %answer.3._.refs_2_, f32[34,16,256]{2,1,0:T(8,128)S(1)} %get-tuple-element.53.r_ref.refs_5_, f32[34,16,128]{2,1,0:T(8,128)S(1)} %get-tuple-element.41.west0.refs_6_, f32[34,16,128]{2,1,0:T(8,128)S(1)} %get-tuple-element.54.west1.refs_7_, ...), custom_call_target="tpu_custom_call" | custom-call | flops 20000000 | bytes 4000000 | tf_op jit(solution)/shard_map/local/pallas_call | solution.py:629
  80.2 0.0 collective-permute-done.7.refs_3_
  80.2 0.0 collective-permute-done.6.refs_1_
  80.2 1.6 %update.2 = (f32[34,16,256]{2,1,0:T(8,128)S(1)}, f32[34,16,256]{2,1,0:T(8,128)S(1)}, f32[8,8,128]{2,1,0:T(8,128)S(1)}) custom-call(s32[1]{0:T(128)} %bitcast.place_ref.refs_0_, f32[3,128]{1,0:T(4,128)S(1)} %collective-permute-done.6.refs_1_, f32[3,128]{1,0:T(4,128)S(1)} %answer.3._.refs_2_, f32[3,128]{1,0:T(4,128)S(1)} %collective-permute-done.7.refs_3_, ...), custom_call_target="tpu_custom_call" | custom-call | tf_op jit(solution)/shard_map/update/pallas_call | solution.py:644
  81.8 9.2 %all_to_all.32.in_ref = f32[8,8,128]{2,1,0:T(8,128)S(1)} all-to-all(f32[8,8,128]{2,1,0:T(8,128)S(1)} %get-tuple-element.58), channel_id=1, replica_groups={{0,96,192,288,384,480,576,672},{8,104,200,296,392,488,584,680},{16,112,..., dimensions={0} | all-to-all | bytes 65536 | tf_op jit(solution)/shard_map/all_to_all | solution.py:610
  91.1 11.8 %all_to_all.33.in_ref = f32[12,3,128]{2,1,0:T(4,128)S(1)} all-to-all(f32[12,3,128]{2,1,0:T(4,128)S(1)} %turn.4), channel_id=1, replica_groups={{0,8,16,24,32,40,48,56,64,72,80,88},{96,104,112,120,128,136,144,152,160..., dimensions={0} | all-to-all | bytes 36864 | tf_op jit(solution)/shard_map/all_to_all | solution.py:619
  102.9 5.8 %collective-permute-start.9 = (f32[3,128]{1,0:T(4,128)S(1)}, f32[3,128]{1,0:T(4,128)S(1)}, u32[]{:S(2)}, u32[]{:S(2)}) collective-permute-start(f32[3,128]{1,0:T(4,128)S(1)} %answer.4._.refs_2_), channel_id=1, source_target_pairs={{1,2},{2,1},{3,4},{4,3},{5,6},{6,5},{9,10},{10,9},{11,12},{12,11},... | collective-permute-start | bytes 4616 | tf_op jit(solution)/shard_map/ppermute | solution.py:537
  108.7 1.9 %collective-permute-start.8 = (f32[3,128]{1,0:T(4,128)S(1)}, f32[3,128]{1,0:T(4,128)S(1)}, u32[]{:S(2)}, u32[]{:S(2)}) collective-permute-start(f32[3,128]{1,0:T(4,128)S(1)} %answer.4._.refs_2_), channel_id=1, source_target_pairs={{0,1},{1,0},{2,3},{3,2},{4,5},{5,4},{6,7},{7,6},{8,9},{9,8},{10,11... | collective-permute-start | bytes 4616 | tf_op jit(solution)/shard_map/ppermute | solution.py:537
  110.6 2.3 %local.4.refs_4_ = f32[34,16,256]{2,1,0:T(8,128)S(1)} custom-call(f32[3,128]{1,0:T(4,128)S(1)} %answer.4._.refs_2_, f32[34,16,256]{2,1,0:T(8,128)S(1)} %get-tuple-element.59.r_ref, f32[34,16,128]{2,1,0:T(8,128)S(1)} %get-tuple-element.41.west0.refs_6_, f32[34,16,128]{2,1,0:T(8,128)S(1)} %get-tuple-element.54.west1.refs_7_, ...), custom_call_target="tpu_custom_call" | custom-call | flops 20000000 | bytes 4000000 | tf_op jit(solution)/shard_map/local/pallas_call | solution.py:629
  112.9 1.1 update.3
  114.1 9.2 %all_to_all.34.in_ref = f32[8,8,128]{2,1,0:T(8,128)S(1)} all-to-all(f32[8,8,128]{2,1,0:T(8,128)S(1)} %get-tuple-element.61), channel_id=1, replica_groups={{0,96,192,288,384,480,576,672},{8,104,200,296,392,488,584,680},{16,112,..., dimensions={0} | all-to-all | bytes 65536 | tf_op jit(solution)/shard_map/all_to_all | solution.py:610
  123.3 11.8 %all_to_all.35.in_ref = f32[12,3,128]{2,1,0:T(4,128)S(1)} all-to-all(f32[12,3,128]{2,1,0:T(4,128)S(1)} %turn.5), channel_id=1, replica_groups={{0,8,16,24,32,40,48,56,64,72,80,88},{96,104,112,120,128,136,144,152,160..., dimensions={0} | all-to-all | bytes 36864 | tf_op jit(solution)/shard_map/all_to_all | solution.py:619
  135.1 5.7 %collective-permute-start.11 = (f32[3,128]{1,0:T(4,128)S(1)}, f32[3,128]{1,0:T(4,128)S(1)}, u32[]{:S(2)}, u32[]{:S(2)}) collective-permute-start(f32[3,128]{1,0:T(4,128)S(1)} %answer.5._.refs_2_), channel_id=1, source_target_pairs={{1,2},{2,1},{3,4},{4,3},{5,6},{6,5},{9,10},{10,9},{11,12},{12,11},... | collective-permute-start | bytes 4616 | tf_op jit(solution)/shard_map/ppermute | solution.py:537
  140.9 1.9 %collective-permute-start.10 = (f32[3,128]{1,0:T(4,128)S(1)}, f32[3,128]{1,0:T(4,128)S(1)}, u32[]{:S(2)}, u32[]{:S(2)}) collective-permute-start(f32[3,128]{1,0:T(4,128)S(1)} %answer.5._.refs_2_), channel_id=1, source_target_pairs={{0,1},{1,0},{2,3},{3,2},{4,5},{5,4},{6,7},{7,6},{8,9},{9,8},{10,11... | collective-permute-start | bytes 4616 | tf_op jit(solution)/shard_map/ppermute | solution.py:537
  142.8 1.7 %local.5.refs_4_ = f32[34,16,256]{2,1,0:T(8,128)S(1)} custom-call(f32[3,128]{1,0:T(4,128)S(1)} %answer.5._.refs_2_, f32[34,16,256]{2,1,0:T(8,128)S(1)} %get-tuple-element.62.r_ref, f32[34,16,128]{2,1,0:T(8,128)S(1)} %get-tuple-element.41.west0.refs_6_, f32[34,16,128]{2,1,0:T(8,128)S(1)} %get-tuple-element.54.west1.refs_7_, ...), custom_call_target="tpu_custom_call" | custom-call | flops 20000000 | bytes 4000000 | tf_op jit(solution)/shard_map/local/pallas_call | solution.py:629
  144.5 1.3 final.1
  (14 shorter events, 0.1 us)
Async XLA Ops:
  1.6 18.4 %collective-permute-start.1 = (f32[2,8,16,128]{3,2,1,0:T(8,128)S(1)}, f32[2,8,16,128]{3,2,1,0:T(8,128)S(1)}, u32[]{:S(2)}, u32[]{:S(2)}) collective-permute-start(f32[2,8,16,128]{3,2,1,0:T(8,128)S(1)} %get-tuple-element.35.own.refs_13_), channel_id=1, source_target_pairs={{8,16},{16,8},{24,32},{32,24},{40,48},{48,40},{56,64},{64,56},{72,... | collective-permute-start | bytes 393224 | tf_op jit(solution)/shard_map/ppermute | solution.py:537
  2.3 17.8 %collective-permute-start = (f32[2,8,16,128]{3,2,1,0:T(8,128)S(1)}, f32[2,8,16,128]{3,2,1,0:T(8,128)S(1)}, u32[]{:S(2)}, u32[]{:S(2)}) collective-permute-start(f32[2,8,16,128]{3,2,1,0:T(8,128)S(1)} %get-tuple-element.35.own.refs_13_), channel_id=1, source_target_pairs={{0,8},{8,0},{16,24},{24,16},{32,40},{40,32},{48,56},{56,48},{64,72... | collective-permute-start | bytes 393224 | tf_op jit(solution)/shard_map/ppermute | solution.py:537
  10.4 9.6 %collective-permute-start.2 = (f32[2,5,16,128]{3,2,1,0:T(8,128)S(1)}, f32[2,5,16,128]{3,2,1,0:T(8,128)S(1)}, u32[]{:S(2)}, u32[]{:S(2)}) collective-permute-start(f32[2,5,16,128]{3,2,1,0:T(8,128)S(1)} %get-tuple-element.36), channel_id=1, source_target_pairs={{0,16},{16,0},{8,24},{24,8},{32,48},{48,32},{40,56},{56,40},{64,80... | collective-permute-start | bytes 245768 | tf_op jit(solution)/shard_map/ppermute | solution.py:537
  17.5 2.6 %collective-permute-start.3 = (f32[2,5,16,128]{3,2,1,0:T(8,128)S(1)}, f32[2,5,16,128]{3,2,1,0:T(8,128)S(1)}, u32[]{:S(2)}, u32[]{:S(2)}) collective-permute-start(f32[2,5,16,128]{3,2,1,0:T(8,128)S(1)} %get-tuple-element.37), channel_id=1, source_target_pairs={{16,32},{32,16},{24,40},{40,24},{48,64},{64,48},{56,72},{72,56},{8... | collective-permute-start | bytes 245768 | tf_op jit(solution)/shard_map/ppermute | solution.py:537
  20.4 9.1 %collective-permute-start.4 = (f32[9,16,128]{2,1,0:T(8,128)S(1)}, f32[9,16,128]{2,1,0:T(8,128)S(1)}, u32[]{:S(2)}, u32[]{:S(2)}) collective-permute-start(f32[9,16,128]{2,1,0:T(8,128)S(1)} %get-tuple-element.50), channel_id=1, source_target_pairs={{0,1},{1,0},{2,3},{3,2},{4,5},{5,4},{6,7},{7,6},{8,9},{9,8},{10,11... | collective-permute-start | bytes 221192 | tf_op jit(solution)/shard_map/ppermute | solution.py:537
  24.2 5.7 %collective-permute-start.5 = (f32[9,16,128]{2,1,0:T(8,128)S(1)}, f32[9,16,128]{2,1,0:T(8,128)S(1)}, u32[]{:S(2)}, u32[]{:S(2)}) collective-permute-start(f32[9,16,128]{2,1,0:T(8,128)S(1)} %get-tuple-element.51), channel_id=1, source_target_pairs={{1,2},{2,1},{3,4},{4,3},{5,6},{6,5},{9,10},{10,9},{11,12},{12,11},... | collective-permute-start | bytes 221192 | tf_op jit(solution)/shard_map/ppermute | solution.py:537
  69.7 10.5 %collective-permute-start.7 = (f32[3,128]{1,0:T(4,128)S(1)}, f32[3,128]{1,0:T(4,128)S(1)}, u32[]{:S(2)}, u32[]{:S(2)}) collective-permute-start(f32[3,128]{1,0:T(4,128)S(1)} %answer.3._.refs_2_), channel_id=1, source_target_pairs={{1,2},{2,1},{3,4},{4,3},{5,6},{6,5},{9,10},{10,9},{11,12},{12,11},... | collective-permute-start | bytes 4616 | tf_op jit(solution)/shard_map/ppermute | solution.py:537
  75.3 4.9 %collective-permute-start.6 = (f32[3,128]{1,0:T(4,128)S(1)}, f32[3,128]{1,0:T(4,128)S(1)}, u32[]{:S(2)}, u32[]{:S(2)}) collective-permute-start(f32[3,128]{1,0:T(4,128)S(1)} %answer.3._.refs_2_), channel_id=1, source_target_pairs={{0,1},{1,0},{2,3},{3,2},{4,5},{5,4},{6,7},{7,6},{8,9},{9,8},{10,11... | collective-permute-start | bytes 4616 | tf_op jit(solution)/shard_map/ppermute | solution.py:537
  102.9 10.1 %collective-permute-start.9 = (f32[3,128]{1,0:T(4,128)S(1)}, f32[3,128]{1,0:T(4,128)S(1)}, u32[]{:S(2)}, u32[]{:S(2)}) collective-permute-start(f32[3,128]{1,0:T(4,128)S(1)} %answer.4._.refs_2_), channel_id=1, source_target_pairs={{1,2},{2,1},{3,4},{4,3},{5,6},{6,5},{9,10},{10,9},{11,12},{12,11},... | collective-permute-start | bytes 4616 | tf_op jit(solution)/shard_map/ppermute | solution.py:537
  108.7 4.2 %collective-permute-start.8 = (f32[3,128]{1,0:T(4,128)S(1)}, f32[3,128]{1,0:T(4,128)S(1)}, u32[]{:S(2)}, u32[]{:S(2)}) collective-permute-start(f32[3,128]{1,0:T(4,128)S(1)} %answer.4._.refs_2_), channel_id=1, source_target_pairs={{0,1},{1,0},{2,3},{3,2},{4,5},{5,4},{6,7},{7,6},{8,9},{9,8},{10,11... | collective-permute-start | bytes 4616 | tf_op jit(solution)/shard_map/ppermute | solution.py:537
  135.1 9.4 %collective-permute-start.11 = (f32[3,128]{1,0:T(4,128)S(1)}, f32[3,128]{1,0:T(4,128)S(1)}, u32[]{:S(2)}, u32[]{:S(2)}) collective-permute-start(f32[3,128]{1,0:T(4,128)S(1)} %answer.5._.refs_2_), channel_id=1, source_target_pairs={{1,2},{2,1},{3,4},{4,3},{5,6},{6,5},{9,10},{10,9},{11,12},{12,11},... | collective-permute-start | bytes 4616 | tf_op jit(solution)/shard_map/ppermute | solution.py:537
  140.9 3.6 %collective-permute-start.10 = (f32[3,128]{1,0:T(4,128)S(1)}, f32[3,128]{1,0:T(4,128)S(1)}, u32[]{:S(2)}, u32[]{:S(2)}) collective-permute-start(f32[3,128]{1,0:T(4,128)S(1)} %answer.5._.refs_2_), channel_id=1, source_target_pairs={{0,1},{1,0},{2,3},{3,2},{4,5},{5,4},{6,7},{7,6},{8,9},{9,8},{10,11... | collective-permute-start | bytes 4616 | tf_op jit(solution)/shard_map/ppermute | solution.py:537
